TPU v7x, 32 devices: a whole 2x2x4 slice. The times are simulated.
32 devices in a mesh: lat: 4 (over y, x), lon: 8 (over z, core).
Axes of the slice: x: 2, y: 2, z: 4, core: 2. Of those that a mesh axis runs over, the one named last changes fastest.
Arguments:
- tracers: bfloat16 [64, 256, 1024], P('lat', 'lon'), may hold values from -6 to 6
- east_wind: bfloat16 [64, 256, 128], P('lat', 'lon'), may hold values from -0.5 to 0.5
- north_wind: bfloat16 [64, 256, 128], P('lat', 'lon'), may hold values from -0.5 to 0.5
- span_of: int32 [64, 256], P('lat', 'lon'), may hold values from 0 to 511, as said below
- slot_of: int32 [64, 256], P('lat', 'lon'), may hold values from 0 to 47
- inverses: bfloat16 [512, 128, 128], P(('lat', 'lon'))
Outputs:
- tendency: float32 [64, 256, 1024], P('lat', 'lon')
Inputs may be any that keep to these rules, and one draw needn't show every extreme that they name: `span_of`: together with slot_of, every (span, slot) pair is named by at most one column. Span c belongs to device c // 16 in the mesh's order (lat index times the lon size plus lon index). The columns of one device name spans of one owner at most 24 times, and in every draw some owner gets exactly 24 columns from every device.
All inputs are finite; a program needn't handle non-finite values.
Results may differ from a plain program's by a relative error of at most 0.0028.
Values may be sent and summed in bfloat16 or wider, within the bound.
No kernel may reach another device: no remote copies, remote signals or barrier semaphores. Data moves between devices by JAX's collectives and lax.ppermute only.
A program may use at most 64 MiB of HBM per device.

v0:
```python
import jax
import jax.numpy as jnp
from jax import lax
from jax.sharding import PartitionSpec as P

CAP = 64


DIFFUSE = 0.1


def extended_2(cells, sides, width, closed):
    for axis, dim in sides:
        count = lax.axis_size(axis)
        ends = count if closed else count - 1
        head = lax.slice_in_dim(cells, 0, width, axis=dim)
        tail = lax.slice_in_dim(cells, cells.shape[dim] - width, cells.shape[dim], axis=dim)
        cells = jnp.concatenate(
            [
                lax.ppermute(tail, axis, [(i, (i + 1) % count) for i in range(ends)]),
                cells,
                lax.ppermute(head, axis, [((i + 1) % count, i) for i in range(ends)]),
            ],
            axis=dim,
        )
    return cells


def east_west(extended, levels):
    width = extended.shape[2] - levels
    rows = extended.shape[0]
    cells = extended.shape[1]
    field = extended[:, :, :width].astype(jnp.float32).reshape(rows, cells, width // levels, levels)
    wind = extended[:, :, width:].astype(jnp.float32).reshape(rows, cells, 1, levels)
    face_wind = 0.5 * (wind[:, :-1] + wind[:, 1:])
    flux = face_wind * (0.5 * (field[:, :-1] + field[:, 1:])) - DIFFUSE * (
        field[:, 1:] - field[:, :-1]
    )
    return -(flux[:, 1:] - flux[:, :-1])


def north_south(extended, levels, first_band, last_band):
    width = extended.shape[2] - levels
    rows = extended.shape[0]
    cells = extended.shape[1]
    field = extended[:, :, :width].astype(jnp.float32).reshape(rows, cells, width // levels, levels)
    wind = extended[:, :, width:].astype(jnp.float32).reshape(rows, cells, 1, levels)
    face_wind = 0.5 * (wind[:-1] + wind[1:])
    flux = face_wind * (0.5 * (field[:-1] + field[1:])) - DIFFUSE * (field[1:] - field[:-1])
    faces = jnp.arange(rows - 1, dtype=jnp.int32)
    dropped = jnp.logical_or(
        jnp.logical_and(faces == 0, first_band), jnp.logical_and(faces == rows - 2, last_band)
    )
    flux = jnp.where(dropped[:, None, None, None], jnp.float32(0.0), flux)
    return -(flux[1:] - flux[:-1])


def shards(tracers, east_wind, north_wind, span_of, slot_of, inverses):
    levels = east_wind.shape[2]
    rows = tracers.shape[0]
    cells = tracers.shape[1]
    width = tracers.shape[2]
    lat_count = lax.axis_size("lat")
    devices = lat_count * lax.axis_size("lon")
    lat_here = lax.axis_index("lat")
    along_lon = jnp.concatenate([tracers, east_wind], axis=2)
    along_lat = jnp.concatenate([tracers, north_wind], axis=2)
    lon_ext = extended_2(along_lon, (("lon", 1),), 1, True)
    lat_ext = extended_2(along_lat, (("lat", 0),), 1, False)
    dynamics = east_west(lon_ext, levels) + north_south(
        lat_ext, levels, lat_here == 0, lat_here == lat_count - 1
    )
    dynamics = dynamics.reshape(rows * cells, width)
    state = (tracers.reshape(rows * cells, width).astype(jnp.float32) + dynamics).astype(
        jnp.bfloat16
    )
    owned = inverses.shape[0]
    pair = 3 * rows * cells // (2 * devices)
    spans = span_of.reshape(-1)
    owner = spans // owned
    dest_slot = spans % owned * CAP + slot_of.reshape(-1)
    one_hot = (owner[:, None] == jnp.arange(devices, dtype=jnp.int32)[None, :]).astype(jnp.int32)
    before = jnp.cumsum(one_hot, axis=0) - one_hot
    rank = jnp.sum(before * one_hot, axis=1)
    position = owner * pair + rank
    outgoing = jnp.zeros((devices * pair, width), jnp.bfloat16).at[position].set(state)
    targets = jnp.full((devices * pair,), owned * CAP, jnp.int32).at[position].set(dest_slot)
    arrived, arrived_slots = (
        lax.all_to_all(outgoing, ("lat", "lon"), split_axis=0, concat_axis=0, tiled=True),
        lax.all_to_all(targets, ("lat", "lon"), split_axis=0, concat_axis=0, tiled=True),
    )
    slots = (
        jnp.zeros((owned * CAP, width), jnp.bfloat16).at[arrived_slots].set(arrived, mode="drop")
    )
    block = slots.reshape(owned, CAP, width // levels, levels)
    relaxed = jnp.einsum("clm,cstm->cstl", inverses, block, preferred_element_type=jnp.float32)
    physics = (relaxed - block.astype(jnp.float32)).astype(jnp.bfloat16).reshape(owned * CAP, width)
    replies = jnp.take(physics, arrived_slots, axis=0, mode="fill", fill_value=0)
    returned = lax.all_to_all(replies, ("lat", "lon"), split_axis=0, concat_axis=0, tiled=True)
    physics_home = returned[position]
    tendency = dynamics + physics_home.astype(jnp.float32)
    return tendency.reshape(rows, cells, width)


def solution(mesh):
    in_specs = (
        P("lat", "lon", None),
        P("lat", "lon", None),
        P("lat", "lon", None),
        P("lat", "lon"),
        P("lat", "lon"),
        P(("lat", "lon"), None, None),
    )
    out_specs = P("lat", "lon", None)
    return jax.shard_map(shards, mesh=mesh, in_specs=in_specs, out_specs=out_specs, check_vma=False)
```

profile of v0, /device:TPU:0, one launch (start us, length us, event | category | flops | bytes accessed | tf_op | source)
XLA Modules:
  0.0 148.9 jit_solution(8687566116804377409)
XLA Ops:
  0.0 0.8 reshape.235
  0.8 0.8 reshape.236
  1.6 0.8 reshape.234
  2.4 0.8 reshape.238
  3.2 1.2 reduce-window.6
  4.8 2.4 %scatter_custom_fusion = s32[768]{0:T(1024)S(1)} fusion(s32[512]{0:T(512)S(1)} %bitcast.107, s32[512]{0:T(512)S(1)} %get-tuple-element.11, s32[]{:T(128)} %constant.70.clone.1), kind=kCustom, calls=%fused_computation.78 | custom fusion | bytes 3076 | tf_op jit(solution)/shard_map/scatter | solution.py:87
  7.2 0.7 all_to_all.24
  7.9 7.3 %all-to-all-start = ((s32[32,24,1]{1,2,0:T(1,128)}), s32[32,24,1]{1,2,0:T(1,128)S(1)}, u32[]{:S(2)}, u32[]{:S(2)}) async-start(s32[32,24,1]{1,2,0:T(1,128)} %bitcast.6), calls=%async_computation | async-start | bytes 32768 | tf_op jit(solution)/shard_map/all_to_all | solution.py:90
  15.2 1.4 constant_dynamic-update-slice_fusion.1
  16.7 1.3 collective-permute-start.3
  18.0 4.5 %collective-permute-start.2 = (bf16[1,32,1152]{2,1,0:T(8,128)(2,1)S(1)}, bf16[1,32,1152]{2,1,0:T(8,128)(2,1)S(1)}, u32[]{:S(2)}, u32[]{:S(2)}) collective-permute-start(bf16[1,32,1152]{2,1,0:T(8,128)(2,1)S(1)} %get-tuple-element.9), channel_id=1, source_target_pairs={{0,8},{8,16},{16,24},{1,9},{9,17},{17,25},{2,10},{10,18},{18,26},{... | collective-permute-start | bytes 221192 | tf_op jit(solution)/shard_map/ppermute | solution.py:20
  22.6 0.6 copy_dynamic-update-slice_fusion
  23.3 2.9 %collective-permute-start.1 = (bf16[16,1,1152]{2,0,1:T(8,128)(2,1)S(1)}, bf16[16,1,1152]{2,0,1:T(8,128)(2,1)S(1)}, u32[]{:S(2)}, u32[]{:S(2)}) collective-permute-start(bf16[16,1,1152]{2,0,1:T(8,128)(2,1)S(1)} %get-tuple-element.8), channel_id=1, source_target_pairs={{1,0},{2,1},{3,2},{4,3},{5,4},{6,5},{7,6},{0,7},{9,8},{10,9},{11,1... | collective-permute-start | bytes 110600 | tf_op jit(solution)/shard_map/ppermute | solution.py:22
  26.1 1.6 %collective-permute-done.1 = bf16[16,1,1152]{2,0,1:T(8,128)(2,1)S(1)} collective-permute-done((bf16[16,1,1152]{2,0,1:T(8,128)(2,1)S(1)}, bf16[16,1,1152]{2,0,1:T(8,128)(2,1)S(1)}, u32[]{:S(2)}, u32[]{:S(2)}) %collective-permute-start.1) | collective-permute-done | bytes 36896 | tf_op jit(solution)/shard_map/ppermute | solution.py:22
  27.8 3.5 %collective-permute-done = bf16[16,1,1152]{2,0,1:T(8,128)(2,1)S(1)} collective-permute-done((bf16[16,1,1152]{2,0,1:T(8,128)(2,1)S(1)}, bf16[16,1,1152]{2,0,1:T(8,128)(2,1)S(1)}, u32[]{:S(2)}, u32[]{:S(2)}) %collective-permute-start) | collective-permute-done | bytes 36896 | tf_op jit(solution)/shard_map/ppermute | solution.py:20
  35.9 1.5 %copy.38 = f32[16,32,8,128]{3,2,1,0:T(8,128)} copy(f32[16,32,8,128]{3,2,0,1:T(8,128)S(1)} %fusion.4) | data formatting | bytes 4194304 | tf_op jit(solution)/shard_map/add | solution.py:70
  37.9 5.1 %scatter_custom_fusion.1 = bf16[768,1024]{1,0:T(8,128)(2,1)} fusion(s32[512]{0:T(512)S(1)} %bitcast.108, f32[64,8,8,128]{3,2,1,0:T(8,128)} %bitcast.100, bf16[512,1024]{1,0:T(8,128)(2,1)S(1)} %bitcast.94, bf16[]{:T(256)} %constant.79.clone.1), kind=kCustom, calls=%fused_computation.27 | custom fusion | flops 1572864 | bytes 4718594 | tf_op jit(solution)/shard_map/scatter | solution.py:86
  43.1 2.9 %all-to-all-start.1 = ((bf16[32,24,1024]{2,1,0:T(8,128)(2,1)}), bf16[32,24,1024]{2,1,0:T(8,128)(2,1)S(1)}, u32[]{:S(2)}, u32[]{:S(2)}) async-start(bf16[32,24,1024]{2,1,0:T(8,128)(2,1)} %bitcast.9), calls=%async_computation.1 | async-start | bytes 3145728 | tf_op jit(solution)/shard_map/all_to_all | solution.py:89
  46.5 0.7 reduce.7
  47.4 37.3 %all-to-all-done.1 = bf16[32,24,1024]{2,1,0:T(8,128)(2,1)S(1)} async-done(((bf16[32,24,1024]{2,1,0:T(8,128)(2,1)}), bf16[32,24,1024]{2,1,0:T(8,128)(2,1)S(1)}, u32[]{:S(2)}, u32[]{:S(2)}) %all-to-all-start.1) | async-done | bytes 1572896 | tf_op jit(solution)/shard_map/all_to_all | solution.py:89
  84.7 1.1 copy-done.4
  85.8 7.0 %scatter_custom_fusion.2 = bf16[1024,1024]{1,0:T(8,128)(2,1)S(1)} fusion(s32[768]{0:T(1024)S(1)} %fusion.20, bf16[768,1024]{1,0:T(8,128)(2,1)} %bitcast.105, bf16[]{:T(256)} %constant.79.clone.1), kind=kCustom, calls=%fused_computation.29 | custom fusion | bytes 2097664 | tf_op jit(solution)/shard_map/scatter | solution.py:93
  92.9 0.6 copy.46
  93.5 0.7 subtract_convert_fusion
  94.2 0.6 copy.61
  94.9 3.6 %gather_fusion = bf16[768,1024]{1,0:T(8,128)(2,1)} fusion(bf16[1024,1024]{1,0:T(8,128)(2,1)S(1)} %bitcast.89, s32[1024]{0:T(1024)S(1)} %pad_clamp_fusion.1), kind=kCustom, calls=%fused_computation | custom fusion | bytes 3148800 | tf_op jit(solution)/shard_map/jit(_take)/gather | solution.py:98
  98.4 2.7 %broadcast_select_fusion = bf16[32,24,1024]{2,1,0:T(8,128)(2,1)} fusion(bf16[32,24,1024]{2,1,0:T(8,128)(2,1)} %bitcast.103, pred[32,24]{1,0:T(8,128)(4,1)S(1)} %compare_and_fusion), kind=kLoop, calls=%fused_computation.22 | loop fusion | flops 786432 | bytes 3146496 | tf_op jit(solution)/shard_map/jit(_take)/select_n | solution.py:98
  101.1 2.7 %all-to-all-start.2 = ((bf16[32,24,1024]{2,1,0:T(8,128)(2,1)}), bf16[32,24,1024]{2,1,0:T(8,128)(2,1)S(1)}, u32[]{:S(2)}, u32[]{:S(2)}) async-start(bf16[32,24,1024]{2,1,0:T(8,128)(2,1)} %broadcast_select_fusion), calls=%async_computation.2 | async-start | bytes 3145728 | tf_op jit(solution)/shard_map/all_to_all | solution.py:99
  103.9 2.7 %reshape.233 = f32[16,32,1024]{2,0,1:T(8,128)} reshape(f32[16,32,8,128]{3,2,0,1:T(8,128)} %copy-done.1) | data formatting | bytes 4194304 | tf_op jit(solution)/shard_map/reshape | solution.py:73
  106.5 36.2 %all-to-all-done.2 = bf16[32,24,1024]{2,1,0:T(8,128)(2,1)S(1)} async-done(((bf16[32,24,1024]{2,1,0:T(8,128)(2,1)}), bf16[32,24,1024]{2,1,0:T(8,128)(2,1)S(1)}, u32[]{:S(2)}, u32[]{:S(2)}) %all-to-all-start.2) | async-done | bytes 1572896 | tf_op jit(solution)/shard_map/all_to_all | solution.py:99
  142.7 2.0 %gather_fusion.1 = bf16[512,1024]{1,0:T(8,128)(2,1)S(1)} fusion(bf16[768,1024]{1,0:T(8,128)(2,1)S(1)} %bitcast.90, s32[1024]{0:T(1024)S(1)} %pad_clamp_fusion), kind=kCustom, calls=%fused_computation.1 | custom fusion | bytes 2099200 | tf_op jit(solution)/shard_map/gather | solution.py:100
  144.8 4.1 %convert_add_fusion = f32[16,32,1024]{2,1,0:T(8,128)} fusion(bf16[16,32,1024]{2,1,0:T(8,128)(2,1)S(1)} %bitcast.104, f32[16,32,1024]{2,0,1:T(8,128)} %reshape.233), kind=kLoop, calls=%fused_computation.20 | loop fusion | flops 1048576 | bytes 5242880 | tf_op jit(solution)/shard_map/add | solution.py:101
  (52 shorter events, 6.2 us)
Async XLA Ops:
  0.0 93.5 %copy-start = (bf16[16,128,128]{2,1,0:T(8,128)(2,1)S(1)}, bf16[16,128,128]{2,1,0:T(8,128)(2,1)}, u32[]{:S(2)}) copy-start(bf16[16,128,128]{2,1,0:T(8,128)(2,1)} %param.11) | copy-start | bytes 1572868
  0.0 16.6 %copy-start.5 = (bf16[16,32,128]{2,1,0:T(8,128)(2,1)S(1)}, bf16[16,32,128]{2,1,0:T(8,128)(2,1)}, u32[]{:S(2)}) copy-start(bf16[16,32,128]{2,1,0:T(8,128)(2,1)} %param.8) | copy-start | bytes 393220
  7.9 35.2 %all-to-all-start = ((s32[32,24,1]{1,2,0:T(1,128)}), s32[32,24,1]{1,2,0:T(1,128)S(1)}, u32[]{:S(2)}, u32[]{:S(2)}) async-start(s32[32,24,1]{1,2,0:T(1,128)} %bitcast.6), calls=%async_computation | async-start | bytes 32768 | tf_op jit(solution)/shard_map/all_to_all | solution.py:90
  15.2 7.4 %copy-start.2 = (bf16[16,32,1024]{2,1,0:T(8,128)(2,1)S(1)}, bf16[16,32,1024]{2,1,0:T(8,128)(2,1)}, u32[]{:S(2)}) copy-start(bf16[16,32,1024]{2,1,0:T(8,128)(2,1)} %param.6) | copy-start | bytes 3145732
  15.2 7.9 %copy-start.6 = (bf16[16,32,128]{2,1,0:T(8,128)(2,1)S(1)}, bf16[16,32,128]{2,1,0:T(8,128)(2,1)}, u32[]{:S(2)}) copy-start(bf16[16,32,128]{2,1,0:T(8,128)(2,1)} %param.7) | copy-start | bytes 393220
  16.7 16.0 %collective-permute-start.3 = (bf16[1,32,1152]{2,1,0:T(8,128)(2,1)S(1)}, bf16[1,32,1152]{2,1,0:T(8,128)(2,1)S(1)}, u32[]{:S(2)}, u32[]{:S(2)}) collective-permute-start(bf16[1,32,1152]{2,1,0:T(8,128)(2,1)S(1)} %get-tuple-element.10), channel_id=1, source_target_pairs={{8,0},{16,8},{24,16},{9,1},{17,9},{25,17},{10,2},{18,10},{26,18},{... | collective-permute-start | bytes 221192 | tf_op jit(solution)/shard_map/ppermute | solution.py:22
  18.0 14.7 %collective-permute-start.2 = (bf16[1,32,1152]{2,1,0:T(8,128)(2,1)S(1)}, bf16[1,32,1152]{2,1,0:T(8,128)(2,1)S(1)}, u32[]{:S(2)}, u32[]{:S(2)}) collective-permute-start(bf16[1,32,1152]{2,1,0:T(8,128)(2,1)S(1)} %get-tuple-element.9), channel_id=1, source_target_pairs={{0,8},{8,16},{16,24},{1,9},{9,17},{17,25},{2,10},{10,18},{18,26},{... | collective-permute-start | bytes 221192 | tf_op jit(solution)/shard_map/ppermute | solution.py:20
  23.3 4.5 %collective-permute-start.1 = (bf16[16,1,1152]{2,0,1:T(8,128)(2,1)S(1)}, bf16[16,1,1152]{2,0,1:T(8,128)(2,1)S(1)}, u32[]{:S(2)}, u32[]{:S(2)}) collective-permute-start(bf16[16,1,1152]{2,0,1:T(8,128)(2,1)S(1)} %get-tuple-element.8), channel_id=1, source_target_pairs={{1,0},{2,1},{3,2},{4,3},{5,4},{6,5},{7,6},{0,7},{9,8},{10,9},{11,1... | collective-permute-start | bytes 110600 | tf_op jit(solution)/shard_map/ppermute | solution.py:22
  26.1 5.2 %collective-permute-start = (bf16[16,1,1152]{2,0,1:T(8,128)(2,1)S(1)}, bf16[16,1,1152]{2,0,1:T(8,128)(2,1)S(1)}, u32[]{:S(2)}, u32[]{:S(2)}) collective-permute-start(bf16[16,1,1152]{2,0,1:T(8,128)(2,1)S(1)} %get-tuple-element.7), channel_id=1, source_target_pairs={{0,1},{1,2},{2,3},{3,4},{4,5},{5,6},{6,7},{7,0},{8,9},{9,10},{10,1... | collective-permute-start | bytes 110600 | tf_op jit(solution)/shard_map/ppermute | solution.py:20
  35.9 2.0 %copy-start.1 = (f32[16,32,8,128]{3,2,0,1:T(8,128)}, f32[16,32,8,128]{3,2,0,1:T(8,128)S(1)}, u32[]{:S(2)}) copy-start(f32[16,32,8,128]{3,2,0,1:T(8,128)S(1)} %fusion.4) | copy-start | bytes 6291460
  35.9 2.0 %copy-start.3 = (bf16[16,32,1024]{2,1,0:T(8,128)(2,1)S(1)}, bf16[16,32,1024]{2,1,0:T(8,128)(2,1)}, u32[]{:S(2)}) copy-start(bf16[16,32,1024]{2,1,0:T(8,128)(2,1)} %param.6) | copy-start | bytes 3145732
  43.1 41.6 %all-to-all-start.1 = ((bf16[32,24,1024]{2,1,0:T(8,128)(2,1)}), bf16[32,24,1024]{2,1,0:T(8,128)(2,1)S(1)}, u32[]{:S(2)}, u32[]{:S(2)}) async-start(bf16[32,24,1024]{2,1,0:T(8,128)(2,1)} %bitcast.9), calls=%async_computation.1 | async-start | bytes 3145728 | tf_op jit(solution)/shard_map/all_to_all | solution.py:89
  84.7 1.1 copy-start.4
  101.1 41.6 %all-to-all-start.2 = ((bf16[32,24,1024]{2,1,0:T(8,128)(2,1)}), bf16[32,24,1024]{2,1,0:T(8,128)(2,1)S(1)}, u32[]{:S(2)}, u32[]{:S(2)}) async-start(bf16[32,24,1024]{2,1,0:T(8,128)(2,1)} %broadcast_select_fusion), calls=%async_computation.2 | async-start | bytes 3145728 | tf_op jit(solution)/shard_map/all_to_all | solution.py:99
where the time goes:
time: 150 us; the launch traced here: 149 us
  waiting for transfers between devices  78.7 us (52%)
  local copies, waits for them, and re-layouts  30.6 us (20%)
  starting transfers between devices  21.6 us (14%)
  other arithmetic  16.9 us (11%)
    all_to_all x1, waiting for transfers between devices, shards(): lax.all_to_all(outgoing, ('lat', 'lon'), split_axis=0, concat_axis=0, til...  37.3 us
    all_to_all x1, waiting for transfers between devices, shards(): lax.all_to_all(replies, ('lat', 'lon'), split_axis=0, concat_axis=0, tile...  36.2 us
    all_to_all x1, starting transfers between devices, shards(): lax.all_to_all(targets, ('lat', 'lon'), split_axis=0, concat_axis=0, tile...  7.3 us
    scatter x1, local copies, waits for them, and re-layouts, shards(): jnp.zeros((owned * CAP, width), jnp.bfloat16).at[arrived_slots]  7.03 us
    unnamed x21, local copies, waits for them, and re-layouts  6.36 us
    scatter x1, other arithmetic, shards(): jnp.zeros((devices * pair, width), jnp.bfloat16).at[position].set(state)  5.14 us
    ppermute x2, starting transfers between devices, extended_2(): lax.ppermute(tail, axis, [(i, (i + 1) % count) for i in range(ends)])  4.55 us
    ppermute x2, starting transfers between devices, extended_2(): lax.ppermute(head, axis, [((i + 1) % count, i) for i in range(ends)])  4.16 us
  transfers between devices with their start and end apart: 7, of which 4 were waited for; matrix products, arithmetic and copies ran while one was open for 12% of the time, Pallas kernels for 0%

commit v1 on v0

v1 whole, which is shorter than its diff:
```python
import functools

import jax
import jax.numpy as jnp
from jax import lax
from jax.experimental import pallas as pl
from jax.experimental.pallas import tpu as pltpu
from jax.sharding import Mesh
from jax.sharding import PartitionSpec as P

SLOTS = 48
GROUP = 16
DIFFUSE = 0.1
GROUP_AXES = ("lat", "lo")
LON_AXES = ("hi", "lo")
COUNT_LANE = 127

VMEM = pl.BlockSpec(memory_space=pltpu.VMEM)
SMEM = pl.BlockSpec(memory_space=pltpu.SMEM)


def plan_kernel(cap, me_ref, packed_ref, pos_ref, meta_ref, count):
    me = me_ref[0]
    rows, cells = packed_ref.shape
    peers = meta_ref.shape[0]
    for x in range(peers):
        count[x] = 0

    def row(i, carry):
        for j in range(cells):
            packed = packed_ref[i, j]
            peer = packed >> 8
            rank = count[peer]
            count[peer] = rank + 1
            meta_ref[peer, rank] = packed & 255
            pos_ref[i * cells + j] = (peer ^ me) * cap + rank
        return carry

    lax.fori_loop(0, rows, row, 0)
    for x in range(peers):
        meta_ref[x, COUNT_LANE] = count[x]


def sort_kernel(cap, me_ref, meta_ref, list_ref, count_ref):
    me = me_ref[0]
    spans = count_ref.shape[0]
    for k in range(spans):
        count_ref[k] = 0

    def peer(x, carry):
        base = (x ^ me) * cap

        def column(r, carry):
            k = meta_ref[x, r]
            n = count_ref[k]
            count_ref[k] = n + 1
            list_ref[k * SLOTS + n] = base + r
            return carry

        return lax.fori_loop(0, meta_ref[x, COUNT_LANE], column, carry)

    lax.fori_loop(0, meta_ref.shape[0], peer, 0)

    def pad(k, carry):
        n = count_ref[k]
        last = list_ref[k * SLOTS + jnp.maximum(n - 1, 0)]

        def fill(r, carry):
            list_ref[k * SLOTS + r] = last
            return carry

        return lax.fori_loop(n, (n + GROUP - 1) // GROUP * GROUP, fill, carry)

    lax.fori_loop(0, spans, pad, 0)


def flux_kernel(
    pos_ref,
    open_ref,
    q_ref,
    u_ref,
    v_ref,
    west_ref,
    east_ref,
    south_ref,
    north_ref,
    send_ref,
    dyn_ref,
    cell,
    wind,
    face_x,
    wind_y,
    face_y,
    edge,
    flux_y,
):
    rows, cells, width = q_ref.shape
    levels = u_ref.shape[2]
    tracers = width // levels
    f32 = jnp.float32
    line = (cells + 2) * tracers

    def spread(block, first, count, stride):
        for t in range(tracers):
            cell[pl.ds(first + t, count, stride=stride), :] = block(t).astype(f32)

    lanes = lambda t: slice(t * levels, (t + 1) * levels)
    spread(lambda t: south_ref[:, lanes(t)], tracers, cells, tracers)
    spread(lambda t: north_ref[:, lanes(t)], (rows + 1) * line + tracers, cells, tracers)
    spread(lambda t: west_ref[:, lanes(t)], line, rows, line)
    spread(lambda t: east_ref[:, lanes(t)], line + (cells + 1) * tracers, rows, line)

    def relayout(i, carry):
        spread(
            lambda t: q_ref[i, :, lanes(t)], (i + 1) * line + tracers, cells, tracers
        )
        return carry

    lax.fori_loop(0, rows, relayout, 0)

    edge[0:rows, :] = west_ref[:, width:].astype(f32)
    edge[rows : 2 * rows, :] = east_ref[:, width:].astype(f32)
    stride = face_x.shape[0] // rows

    def faces(i, carry):
        wind[0:1, :] = edge[pl.ds(i, 1), :]
        wind[1 : cells + 1, :] = u_ref[i].astype(f32)
        wind[cells + 1 : cells + 2, :] = edge[pl.ds(rows + i, 1), :]
        face_x[pl.ds(pl.multiple_of(i * stride, 8), stride), :] = 0.25 * (
            wind[0:stride, :] + wind[1 : stride + 1, :]
        )
        return carry

    lax.fori_loop(0, rows, faces, 0)
    wind_y[0:cells, :] = south_ref[:, width:].astype(f32)
    wind_y[cells : (rows + 1) * cells, :] = v_ref[...].reshape(rows * cells, levels).astype(f32)
    wind_y[(rows + 1) * cells :, :] = north_ref[:, width:].astype(f32)
    face_y[...] = 0.25 * (wind_y[: (rows + 1) * cells, :] + wind_y[cells:, :])
    south_open, north_open = open_ref[0].astype(f32), open_ref[1].astype(f32)
    face_y[0:cells, :] = face_y[0:cells, :] * south_open
    face_y[rows * cells :, :] = face_y[rows * cells :, :] * north_open

    def tile(i, j):
        first = (i * (cells + 2) + j) * tracers
        return cell[pl.ds(pl.multiple_of(first, tracers), tracers), :]

    def spread_row(ref, r):
        return jnp.broadcast_to(ref[pl.ds(r, 1), :], (tracers, levels))

    for j in range(cells):
        low, high = tile(0, j + 1), tile(1, j + 1)
        flux_y[j * tracers : (j + 1) * tracers, :] = spread_row(face_y, j) * (low + high) - (
            DIFFUSE * south_open
        ) * (high - low)

    def row(i, carry):
        diffuse_y = DIFFUSE * jnp.where(i == rows - 1, north_open, 1.0)
        here = tile(i + 1, 1)
        last = tile(i + 1, 0)
        flux_w = spread_row(face_x, i * stride) * (last + here) - DIFFUSE * (here - last)
        for j in range(cells):
            after = tile(i + 1, j + 2)
            flux_e = spread_row(face_x, i * stride + j + 1) * (here + after) - DIFFUSE * (
                after - here
            )
            above = tile(i + 2, j + 1)
            flux_n = spread_row(face_y, (i + 1) * cells + j) * (here + above) - diffuse_y * (
                above - here
            )
            flux_s = flux_y[j * tracers : (j + 1) * tracers, :]
            flux_y[j * tracers : (j + 1) * tracers, :] = flux_n
            dyn = (flux_w - flux_e) + (flux_s - flux_n)
            column = i * cells + j
            dyn_ref[pl.ds(pl.multiple_of(column * tracers, tracers), tracers), :] = dyn
            send_ref[pos_ref[column]] = (here + dyn).astype(jnp.bfloat16)
            here, flux_w = after, flux_e
        return carry

    lax.fori_loop(0, rows, row, 0)


def relax_kernel(list_ref, count_ref, x_ref, own_ref, pair_ref, y_ref):
    tracers, levels = x_ref.shape[1:]
    owned = own_ref.shape[0]

    def relax(w_ref, first):
        def span(k, carry):
            n = count_ref[first + k]
            for part in range(SLOTS // GROUP):

                @pl.when(n > part * GROUP)
                def _():
                    base = (first + k) * SLOTS + part * GROUP
                    at = [list_ref[base + c] for c in range(GROUP)]
                    x = jnp.concatenate([x_ref[a].astype(jnp.float32) for a in at], axis=0)
                    y = lax.dot_general(
                        x.astype(jnp.bfloat16),
                        w_ref[k],
                        (((1,), (1,)), ((), ())),
                        preferred_element_type=jnp.float32,
                    )
                    y = y - x
                    for c, a in enumerate(at):
                        y_ref[a] = y[c * tracers : (c + 1) * tracers].astype(jnp.bfloat16)

            return carry

        lax.fori_loop(0, owned, span, 0)

    relax(own_ref, 0)
    relax(pair_ref, owned)


def finish_kernel(pos_ref, y_ref, dyn_ref, out_ref, total):
    rows, cells, width = out_ref.shape
    tracers, levels = y_ref.shape[1:]
    first = pl.program_id(0) * rows * cells

    def row(i, carry):
        for j in range(cells):
            column = i * cells + j
            at = pl.multiple_of(column * tracers, tracers)
            total[j * tracers : (j + 1) * tracers, :] = dyn_ref[pl.ds(at, tracers), :] + y_ref[
                pos_ref[first + column]
            ].astype(jnp.float32)
        for t in range(tracers):
            out_ref[i, :, t * levels : (t + 1) * levels] = total[
                pl.ds(t, cells, stride=tracers), :
            ]
        return carry

    lax.fori_loop(0, rows, row, 0)


def shift(x, axis, by, closed):
    count = lax.axis_size(axis)
    pairs = [(i, (i + by) % count) for i in range(count) if closed or 0 <= i + by < count]
    return lax.ppermute(x, axis, pairs)


def shards(tracers, east_wind, north_wind, span_of, slot_of, inverses):
    levels = east_wind.shape[2]
    rows, cells, width = tracers.shape
    kinds = width // levels
    columns = rows * cells
    lats, lows = lax.axis_size("lat"), lax.axis_size("lo")
    lons = lax.axis_size("hi") * lows
    peers = lats * lows
    owned = inverses.shape[0]
    cap = 2 * (3 * columns // (2 * lats * lons))
    lat, hi, lo = lax.axis_index("lat"), lax.axis_index("hi"), lax.axis_index("lo")
    me = (lat * lows + lo).astype(jnp.int32)
    me_arg = me.reshape(1)

    lon_edge = lambda j: jnp.concatenate([tracers[:, j, :], east_wind[:, j, :]], axis=1)
    lat_edge = lambda i: jnp.concatenate([tracers[i], north_wind[i]], axis=1)
    west = shift(lon_edge(cells - 1), LON_AXES, 1, True)
    east = shift(lon_edge(0), LON_AXES, -1, True)
    south = shift(lat_edge(rows - 1), "lat", 1, False)
    north = shift(lat_edge(0), "lat", -1, False)
    pair = lax.ppermute(inverses, "hi", [(0, 1), (1, 0)])

    owner = span_of // owned
    owner_lon = owner % lons
    peer = (owner // lons * lows + owner_lon % lows) ^ me
    local = jnp.where(owner_lon // lows == hi, 0, owned) + span_of % owned
    packed = peer * 256 + local

    pos, meta = pl.pallas_call(
        functools.partial(plan_kernel, cap),
        out_shape=(
            jax.ShapeDtypeStruct((columns,), jnp.int32),
            jax.ShapeDtypeStruct((peers, 128), jnp.int32),
        ),
        in_specs=[SMEM, SMEM],
        out_specs=(SMEM, SMEM),
        scratch_shapes=[pltpu.SMEM((peers,), jnp.int32)],
        name="plan",
    )(me_arg, packed)

    open_faces = jnp.stack([lat > 0, lat < lats - 1]).astype(jnp.int32)
    stride = (cells + 1 + 7) // 8 * 8
    f32 = jnp.float32
    send, dyn = pl.pallas_call(
        flux_kernel,
        out_shape=(
            jax.ShapeDtypeStruct((peers * cap, kinds, levels), jnp.bfloat16),
            jax.ShapeDtypeStruct((columns * kinds, levels), f32),
        ),
        in_specs=[SMEM, SMEM] + [VMEM] * 7,
        out_specs=(VMEM, VMEM),
        scratch_shapes=[
            pltpu.VMEM(((rows + 2) * (cells + 2) * kinds, levels), f32),
            pltpu.VMEM((stride + 8, levels), f32),
            pltpu.VMEM((rows * stride, levels), f32),
            pltpu.VMEM(((rows + 2) * cells, levels), f32),
            pltpu.VMEM(((rows + 1) * cells, levels), f32),
            pltpu.VMEM((2 * rows, levels), f32),
            pltpu.VMEM((cells * kinds, levels), f32),
        ],
        compiler_params=pltpu.CompilerParams(vmem_limit_bytes=24 << 20),
        name="flux",
    )(pos, open_faces, tracers, east_wind, north_wind, west, east, south, north)

    def exchange(x):
        x = x.reshape(peers, cap, kinds, levels)
        x = lax.all_to_all(x, GROUP_AXES, split_axis=0, concat_axis=0, tiled=True)
        return x.reshape(peers * cap, kinds, levels)

    send, meta = lax.optimization_barrier((send, meta))
    arrived = exchange(send)
    bits = [(axis, b) for axis, n in (("lat", lats), ("lo", lows)) for b in reversed(range(n.bit_length() - 1))]
    meta = meta.reshape((2,) * len(bits) + (128,))
    for axis, b in bits:
        n = lax.axis_size(axis)
        other = lax.ppermute(meta[1], axis, [(i, i ^ (1 << b)) for i in range(n)])
        meta = jnp.stack([meta[0], other], axis=-2)
    meta = meta.reshape(peers, 128)

    spans = 2 * owned
    order, count = pl.pallas_call(
        functools.partial(sort_kernel, cap),
        out_shape=(
            jax.ShapeDtypeStruct((spans * SLOTS,), jnp.int32),
            jax.ShapeDtypeStruct((spans,), jnp.int32),
        ),
        in_specs=[SMEM, SMEM],
        out_specs=(SMEM, SMEM),
        name="sort",
    )(me_arg, meta)

    physics = pl.pallas_call(
        relax_kernel,
        out_shape=jax.ShapeDtypeStruct((peers * cap, kinds, levels), jnp.bfloat16),
        in_specs=[SMEM, SMEM, VMEM, VMEM, VMEM],
        out_specs=VMEM,
        compiler_params=pltpu.CompilerParams(vmem_limit_bytes=16 << 20),
        name="relax",
    )(order, count, arrived, inverses, pair)

    returned = exchange(physics)
    step = 4
    return pl.pallas_call(
        finish_kernel,
        out_shape=jax.ShapeDtypeStruct((rows, cells, width), f32),
        grid=(rows // step,),
        in_specs=[
            SMEM,
            pl.BlockSpec((peers * cap, kinds, levels), lambda i: (0, 0, 0)),
            pl.BlockSpec((step * cells * kinds, levels), lambda i: (i, 0)),
        ],
        out_specs=pl.BlockSpec((step, cells, width), lambda i: (i, 0, 0)),
        scratch_shapes=[pltpu.VMEM((cells * kinds, levels), f32)],
        compiler_params=pltpu.CompilerParams(vmem_limit_bytes=16 << 20),
        name="finish",
    )(pos, returned, dyn)


def solution(mesh):
    lats, lons = mesh.devices.shape
    split = Mesh(mesh.devices.reshape(lats, 2, lons // 2), ("lat", "hi", "lo"))
    block = P("lat", LON_AXES, None)
    in_specs = (
        block,
        block,
        block,
        P("lat", LON_AXES),
        P("lat", LON_AXES),
        P(("lat", "hi", "lo"), None, None),
    )
    return jax.shard_map(shards, mesh=split, in_specs=in_specs, out_specs=block, check_vma=False)
```

time: 150 us -> 116 us (0.77)
  waiting for transfers between devices: 78.7 us -> 18.7 us
  Pallas kernels: 0 us -> 31.2 us
  blocking collectives: 0 us -> 24.5 us
  local copies, waits for them, and re-layouts: 30.6 us -> 8.77 us
  other arithmetic: 16.9 us -> 2.06 us
  starting transfers between devices: 21.6 us -> 29.2 us
    all_to_all x3 -> x1, waiting for transfers between devices: 73.5 us -> 0.01 us  [exchange(): x = lax.all_to_all(x, GROUP_AXES, split_axis=0, concat_axis=0, tiled=True)]
    pallas_call x0 -> x5, Pallas kernels: none -> 31.2 us  [the longest x1 10 us: shards(): pl.pallas_call(relax_kernel, out_shape=jax.ShapeDtypeStruct((peers * cap,...]
    all_to_all x0 -> x1, blocking collectives: none -> 24.5 us  [exchange(): x = lax.all_to_all(x, GROUP_AXES, split_axis=0, concat_axis=0, tiled=True)]
    ppermute x4 -> x9, starting transfers between devices: 8.71 us -> 24.1 us  [the longest x4 12.4 us: shards(): other = lax.ppermute(meta[1], axis, [(i, i ^ 1 << b) for i in range(n)])]
    ppermute x4 -> x9, waiting for transfers between devices: 5.17 us -> 18.7 us  [the longest x4 18.7 us: shards(): other = lax.ppermute(meta[1], axis, [(i, i ^ 1 << b) for i in range(n)])]
    scatter x2 -> x0, local copies, waits for them, and re-layouts: 9.48 us -> none  [the longest x1 7.03 us: shards(): jnp.zeros((owned * CAP, width), jnp.bfloat16).at[arrived_slots]]
    all_to_all x3 -> x1, starting transfers between devices: 12.9 us -> 5.11 us  [exchange(): x = lax.all_to_all(x, GROUP_AXES, split_axis=0, concat_axis=0, tiled=True)]
    reshape x5 -> x0, local copies, waits for them, and re-layouts: 5.85 us -> none  [the longest x1 2.69 us: shards(): dynamics = dynamics.reshape(rows * cells, width)]
  transfers between devices with their start and end apart: 7 -> 10, of which waited for: 4 -> 4; matrix products, arithmetic and copies ran while one was open for 12% -> 4% of each run, Pallas kernels for 0% -> 13%
where the time goes in v1:
time: 116 us; the launch traced here: 115 us
  Pallas kernels  31.2 us (27%)
  starting transfers between devices  29.2 us (25%)
  blocking collectives  24.5 us (21%)
  waiting for transfers between devices  18.7 us (16%)
  local copies, waits for them, and re-layouts  8.77 us (8%)
  other arithmetic  2.06 us (2%)
    all_to_all x1, blocking collectives, exchange(): x = lax.all_to_all(x, GROUP_AXES, split_axis=0, concat_axis=0, tiled=True)  24.5 us
    ppermute x4, waiting for transfers between devices, shards(): other = lax.ppermute(meta[1], axis, [(i, i ^ 1 << b) for i in range(n)])  18.7 us
    ppermute x4, starting transfers between devices, shards(): other = lax.ppermute(meta[1], axis, [(i, i ^ 1 << b) for i in range(n)])  12.4 us
    pallas_call x1, Pallas kernels, shards(): pl.pallas_call(relax_kernel, out_shape=jax.ShapeDtypeStruct((peers * cap,...  10 us
    ppermute x4, starting transfers between devices, shift(): return lax.ppermute(x, axis, pairs)  9.77 us
    pallas_call x1, Pallas kernels, shards(): pl.pallas_call(functools.partial(sort_kernel, cap), out_shape=(jax.ShapeD...  9.58 us
    unnamed x26, local copies, waits for them, and re-layouts  5.15 us
    all_to_all x1, starting transfers between devices, exchange(): x = lax.all_to_all(x, GROUP_AXES, split_axis=0, concat_axis=0, tiled=True)  5.11 us
  transfers between devices with their start and end apart: 10, of which 4 were waited for; matrix products, arithmetic and copies ran while one was open for 4% of the time, Pallas kernels for 13%

profile of v1, /device:TPU:0, one launch (start us, length us, event | category | flops | bytes accessed | tf_op | source)
XLA Modules:
  0.0 114.7 jit_solution(7572008737350316205)
XLA Ops:
  0.0 1.0 slice_bitcast_fusion
  1.0 0.7 slice_bitcast_fusion.2
  1.7 4.8 %collective-permute-start.2 = (bf16[32,1152]{1,0:T(8,128)(2,1)S(1)}, bf16[32,1152]{1,0:T(8,128)(2,1)S(1)}, u32[]{:S(2)}, u32[]{:S(2)}) collective-permute-start(bf16[32,1152]{1,0:T(8,128)(2,1)S(1)} %pad_maximum_fusion), channel_id=1, source_target_pairs={{0,8},{8,16},{16,24},{1,9},{9,17},{17,25},{2,10},{10,18},{18,26},{... | collective-permute-start | bytes 221192 | tf_op jit(solution)/shard_map/ppermute | solution.py:238
  6.6 1.3 %collective-permute-start.3 = (bf16[32,1152]{1,0:T(8,128)(2,1)S(1)}, bf16[32,1152]{1,0:T(8,128)(2,1)S(1)}, u32[]{:S(2)}, u32[]{:S(2)}) collective-permute-start(bf16[32,1152]{1,0:T(8,128)(2,1)S(1)} %pad_maximum_fusion.1), channel_id=1, source_target_pairs={{8,0},{16,8},{24,16},{9,1},{17,9},{25,17},{10,2},{18,10},{26,18},{... | collective-permute-start | bytes 221192 | tf_op jit(solution)/shard_map/ppermute | solution.py:238
  7.9 1.1 fusion.18
  9.0 0.8 fusion.19
  10.0 3.6 %collective-permute-start.1 = (bf16[16,1152]{1,0:T(8,128)(2,1)S(1)}, bf16[16,1152]{1,0:T(8,128)(2,1)S(1)}, u32[]{:S(2)}, u32[]{:S(2)}) collective-permute-start(bf16[16,1152]{1,0:T(8,128)(2,1)S(1)} %pad_maximum_fusion.3), channel_id=1, source_target_pairs={{0,7},{1,0},{2,1},{3,2},{4,3},{5,4},{6,5},{7,6},{8,15},{9,8},{10,9... | collective-permute-start | bytes 110600 | tf_op jit(solution)/shard_map/ppermute | solution.py:238
  13.5 1.3 %fusion.4.packed_ref = s32[16,32]{1,0:T(8,128)} fusion(s32[16,32]{1,0:T(8,128)} %param.9, s32[]{:T(128)S(6)} %axis_index.38, s32[]{:T(128)} %add.29), kind=kLoop, calls=%fused_computation.27 | loop fusion | flops 33280 | bytes 4104 | tf_op jit(solution)/shard_map/add | solution.py:267
  14.9 0.1 add_convert_fusion.open_ref
  14.9 4.8 %plan.1 = (s32[512]{0:T(512)}, s32[16,128]{1,0:T(8,128)}) custom-call(s32[1]{0:T(128)} %bitcast.me_ref, s32[16,32]{1,0:T(8,128)} %fusion.4.packed_ref), custom_call_target="tpu_custom_call" | custom-call | tf_op jit(solution)/shard_map/plan/pallas_call | solution.py:269
  19.8 0.9 copy-done.4
  20.7 0.9 copy-done.5
  21.6 0.7 copy-done.7
  22.3 3.8 %flux.1 = (bf16[768,8,128]{2,1,0:T(8,128)(2,1)}, f32[4096,128]{1,0:T(8,128)S(1)}) custom-call(s32[512]{0:T(512)S(1)} %copy-done.7, s32[2]{0:T(128)S(1)} %add_convert_fusion.open_ref, bf16[16,32,1024]{2,1,0:T(8,128)(2,1)S(1)} %copy-done.2, bf16[16,32,128]{2,1,0:T(8,128)(2,1)S(1)} %copy-done.4, bf16[16,32,128]{2,1,0:T(8,128)(2,1)S(1)} %copy-done.5, ...), custom_call_target="tpu_custom_call" | custom-call | tf_op jit(solution)/shard_map/flux/pallas_call | solution.py:284
  26.1 1.3 %copy-done = f32[4096,128]{1,0:T(8,128)} copy-done((f32[4096,128]{1,0:T(8,128)}, f32[4096,128]{1,0:T(8,128)S(1)}, u32[]{:S(2)}) %copy-start) | copy-done | bytes 2097176
  27.4 5.1 %all-to-all-start = ((bf16[16,48,8,128]{3,2,1,0:T(8,128)(2,1)}), bf16[16,48,8,128]{3,2,1,0:T(8,128)(2,1)S(1)}, u32[]{:S(2)}, u32[]{:S(2)}) async-start(bf16[16,48,8,128]{3,2,1,0:T(8,128)(2,1)} %bitcast.28), calls=%async_computation | async-start | bytes 3145728 | tf_op jit(solution)/shard_map/all_to_all | solution.py:307
  32.5 1.9 %collective-permute-start.8 = (bf16[16,128,128]{2,1,0:T(8,128)(2,1)S(1)}, bf16[16,128,128]{2,1,0:T(8,128)(2,1)S(1)}, u32[]{:S(2)}, u32[]{:S(2)}) collective-permute-start(bf16[16,128,128]{2,1,0:T(8,128)(2,1)S(1)} %copy-done.3), channel_id=1, source_target_pairs={{0,4},{4,0},{1,5},{5,1},{2,6},{6,2},{3,7},{7,3},{8,12},{12,8},{9,1... | collective-permute-start | bytes 1572872 | tf_op jit(solution)/shard_map/ppermute | solution.py:261
  34.4 1.9 %collective-permute-start.4 = (s32[2,2,2,128]{3,2,1,0:T(2,128)S(1)}, s32[2,2,2,128]{3,2,1,0:T(2,128)S(1)}, u32[]{:S(2)}, u32[]{:S(2)}) collective-permute-start(s32[2,2,2,128]{3,2,1,0:T(2,128)S(1)} %bitcast.66), channel_id=1, source_target_pairs={{0,16},{8,24},{16,0},{24,8},{1,17},{9,25},{17,1},{25,9},{2,18},{10... | collective-permute-start | bytes 12296 | tf_op jit(solution)/shard_map/ppermute | solution.py:316
  36.3 8.9 %collective-permute-done.4 = s32[2,2,2,128]{3,2,1,0:T(2,128)S(1)} collective-permute-done((s32[2,2,2,128]{3,2,1,0:T(2,128)S(1)}, s32[2,2,2,128]{3,2,1,0:T(2,128)S(1)}, u32[]{:S(2)}, u32[]{:S(2)}) %collective-permute-start.4) | collective-permute-done | bytes 4128 | tf_op jit(solution)/shard_map/ppermute | solution.py:316
  45.3 1.6 %collective-permute-start.5 = (s32[2,2,2,128]{3,2,1,0:T(2,128)S(1)}, s32[2,2,2,128]{3,2,1,0:T(2,128)S(1)}, u32[]{:S(2)}, u32[]{:S(2)}) collective-permute-start(s32[2,2,2,128]{3,2,1,0:T(2,128)S(1)} %get-tuple-element.34), channel_id=1, source_target_pairs={{0,8},{8,0},{16,24},{24,16},{1,9},{9,1},{17,25},{25,17},{2,10},{10... | collective-permute-start | bytes 12296 | tf_op jit(solution)/shard_map/ppermute | solution.py:316
  46.8 2.1 %collective-permute-done.5 = s32[2,2,2,128]{3,2,1,0:T(2,128)S(1)} collective-permute-done((s32[2,2,2,128]{3,2,1,0:T(2,128)S(1)}, s32[2,2,2,128]{3,2,1,0:T(2,128)S(1)}, u32[]{:S(2)}, u32[]{:S(2)}) %collective-permute-start.5) | collective-permute-done | bytes 4128 | tf_op jit(solution)/shard_map/ppermute | solution.py:316
  49.0 8.9 %collective-permute-start.6 = (s32[2,2,2,128]{3,2,1,0:T(2,128)S(1)}, s32[2,2,2,128]{3,2,1,0:T(2,128)S(1)}, u32[]{:S(2)}, u32[]{:S(2)}) collective-permute-start(s32[2,2,2,128]{3,2,1,0:T(2,128)S(1)} %get-tuple-element.32), channel_id=1, source_target_pairs={{0,2},{1,3},{2,0},{3,1},{4,6},{5,7},{6,4},{7,5},{8,10},{9,11},{10,... | collective-permute-start | bytes 12296 | tf_op jit(solution)/shard_map/ppermute | solution.py:316
  57.8 6.5 %collective-permute-done.6 = s32[2,2,2,128]{3,2,1,0:T(2,128)S(1)} collective-permute-done((s32[2,2,2,128]{3,2,1,0:T(2,128)S(1)}, s32[2,2,2,128]{3,2,1,0:T(2,128)S(1)}, u32[]{:S(2)}, u32[]{:S(2)}) %collective-permute-start.6) | collective-permute-done | bytes 4128 | tf_op jit(solution)/shard_map/ppermute | solution.py:316
  64.4 0.1 collective-permute-start.7
  64.4 1.2 %collective-permute-done.7 = s32[2,2,2,128]{3,2,1,0:T(2,128)S(1)} collective-permute-done((s32[2,2,2,128]{3,2,1,0:T(2,128)S(1)}, s32[2,2,2,128]{3,2,1,0:T(2,128)S(1)}, u32[]{:S(2)}, u32[]{:S(2)}) %collective-permute-start.7) | collective-permute-done | bytes 4128 | tf_op jit(solution)/shard_map/ppermute | solution.py:316
  65.6 0.6 pad_add_fusion
  66.2 9.6 %sort.1 = (s32[1536]{0:T(1024)}, s32[32]{0:T(128)}) custom-call(s32[1]{0:T(128)} %bitcast.me_ref, s32[16,128]{1,0:T(8,128)} %bitcast.56), custom_call_target="tpu_custom_call" | custom-call | tf_op jit(solution)/shard_map/sort/pallas_call | solution.py:321
  75.8 0.7 copy-done.6
  76.5 0.6 copy-done.9
  77.1 10.0 %relax.1 = bf16[768,8,128]{2,1,0:T(8,128)(2,1)S(1)} custom-call(s32[1536]{0:T(1024)S(1)} %copy-done.6, s32[32]{0:T(128)S(1)} %copy-done.9, bf16[768,8,128]{2,1,0:T(8,128)(2,1)S(1)} %bitcast.51, bf16[16,128,128]{2,1,0:T(8,128)(2,1)S(1)} %copy-done.3, bf16[16,128,128]{2,1,0:T(8,128)(2,1)S(1)} %collective-permute-done.8.pair_ref), custom_call_target="tpu_custom_call" | custom-call | tf_op jit(solution)/shard_map/relax/pallas_call | solution.py:332
  87.2 24.5 %all_to_all.10 = bf16[16,48,8,128]{3,2,1,0:T(8,128)(2,1)S(1)} all-to-all(bf16[16,48,8,128]{3,2,1,0:T(8,128)(2,1)S(1)} %bitcast.52), channel_id=1, replica_groups=mesh['lat'=4,'hi'=2,'lo'=4] {'lat','lo'}, dimensions={0} | all-to-all | bytes 3145728 | tf_op jit(solution)/shard_map/all_to_all | solution.py:307
  111.7 3.0 %finish.1 = f32[16,32,1024]{2,1,0:T(8,128)} custom-call(s32[512]{0:T(512)S(1)} %copy-done.8, bf16[768,8,128]{2,1,0:T(8,128)(2,1)S(1)} %bitcast.53, f32[4096,128]{1,0:T(8,128)S(1)} %copy-done.1), custom_call_target="tpu_custom_call" | custom-call | tf_op jit(solution)/shard_map/finish/pallas_call | solution.py:343
  (35 shorter events, 0.2 us)
Async XLA Ops:
  0.0 19.8 %copy-start.2 = (bf16[16,32,1024]{2,1,0:T(8,128)(2,1)S(1)}, bf16[16,32,1024]{2,1,0:T(8,128)(2,1)}, u32[]{:S(2)}) copy-start(bf16[16,32,1024]{2,1,0:T(8,128)(2,1)} %q_ref.1) | copy-start | bytes 3145732
  1.7 18.1 %collective-permute-start.2 = (bf16[32,1152]{1,0:T(8,128)(2,1)S(1)}, bf16[32,1152]{1,0:T(8,128)(2,1)S(1)}, u32[]{:S(2)}, u32[]{:S(2)}) collective-permute-start(bf16[32,1152]{1,0:T(8,128)(2,1)S(1)} %pad_maximum_fusion), channel_id=1, source_target_pairs={{0,8},{8,16},{16,24},{1,9},{9,17},{17,25},{2,10},{10,18},{18,26},{... | collective-permute-start | bytes 221192 | tf_op jit(solution)/shard_map/ppermute | solution.py:238
  6.6 13.2 %collective-permute-start.3 = (bf16[32,1152]{1,0:T(8,128)(2,1)S(1)}, bf16[32,1152]{1,0:T(8,128)(2,1)S(1)}, u32[]{:S(2)}, u32[]{:S(2)}) collective-permute-start(bf16[32,1152]{1,0:T(8,128)(2,1)S(1)} %pad_maximum_fusion.1), channel_id=1, source_target_pairs={{8,0},{16,8},{24,16},{9,1},{17,9},{25,17},{10,2},{18,10},{26,18},{... | collective-permute-start | bytes 221192 | tf_op jit(solution)/shard_map/ppermute | solution.py:238
  9.9 9.9 %collective-permute-start = (bf16[16,1152]{1,0:T(8,128)(2,1)S(1)}, bf16[16,1152]{1,0:T(8,128)(2,1)S(1)}, u32[]{:S(2)}, u32[]{:S(2)}) collective-permute-start(bf16[16,1152]{1,0:T(8,128)(2,1)S(1)} %pad_maximum_fusion.2), channel_id=1, source_target_pairs={{0,1},{1,2},{2,3},{3,4},{4,5},{5,6},{6,7},{7,0},{8,9},{9,10},{10,1... | collective-permute-start | bytes 110600 | tf_op jit(solution)/shard_map/ppermute | solution.py:238
  10.0 9.8 %collective-permute-start.1 = (bf16[16,1152]{1,0:T(8,128)(2,1)S(1)}, bf16[16,1152]{1,0:T(8,128)(2,1)S(1)}, u32[]{:S(2)}, u32[]{:S(2)}) collective-permute-start(bf16[16,1152]{1,0:T(8,128)(2,1)S(1)} %pad_maximum_fusion.3), channel_id=1, source_target_pairs={{0,7},{1,0},{2,1},{3,2},{4,3},{5,4},{6,5},{7,6},{8,15},{9,8},{10,9... | collective-permute-start | bytes 110600 | tf_op jit(solution)/shard_map/ppermute | solution.py:238
  19.8 0.9 copy-start.4
  20.7 0.9 copy-start.5
  21.6 0.7 copy-start.7
  26.1 1.3 %copy-start = (f32[4096,128]{1,0:T(8,128)}, f32[4096,128]{1,0:T(8,128)S(1)}, u32[]{:S(2)}) copy-start(f32[4096,128]{1,0:T(8,128)S(1)} %get-tuple-element.20.dyn_ref) | copy-start | bytes 6291460
  27.4 5.1 %copy-start.3 = (bf16[16,128,128]{2,1,0:T(8,128)(2,1)S(1)}, bf16[16,128,128]{2,1,0:T(8,128)(2,1)}, u32[]{:S(2)}) copy-start(bf16[16,128,128]{2,1,0:T(8,128)(2,1)} %own_ref.1) | copy-start | bytes 1572868
  27.4 7.0 %copy-start.10 = (s32[16,128]{1,0:T(8,128)S(1)}, s32[16,128]{1,0:T(8,128)}, u32[]{:S(2)}) copy-start(s32[16,128]{1,0:T(8,128)} %get-tuple-element.16) | copy-start | bytes 24580
  27.4 48.4 %all-to-all-start = ((bf16[16,48,8,128]{3,2,1,0:T(8,128)(2,1)}), bf16[16,48,8,128]{3,2,1,0:T(8,128)(2,1)S(1)}, u32[]{:S(2)}, u32[]{:S(2)}) async-start(bf16[16,48,8,128]{3,2,1,0:T(8,128)(2,1)} %bitcast.28), calls=%async_computation | async-start | bytes 3145728 | tf_op jit(solution)/shard_map/all_to_all | solution.py:307
  32.5 43.3 %collective-permute-start.8 = (bf16[16,128,128]{2,1,0:T(8,128)(2,1)S(1)}, bf16[16,128,128]{2,1,0:T(8,128)(2,1)S(1)}, u32[]{:S(2)}, u32[]{:S(2)}) collective-permute-start(bf16[16,128,128]{2,1,0:T(8,128)(2,1)S(1)} %copy-done.3), channel_id=1, source_target_pairs={{0,4},{4,0},{1,5},{5,1},{2,6},{6,2},{3,7},{7,3},{8,12},{12,8},{9,1... | collective-permute-start | bytes 1572872 | tf_op jit(solution)/shard_map/ppermute | solution.py:261
  34.4 10.8 %collective-permute-start.4 = (s32[2,2,2,128]{3,2,1,0:T(2,128)S(1)}, s32[2,2,2,128]{3,2,1,0:T(2,128)S(1)}, u32[]{:S(2)}, u32[]{:S(2)}) collective-permute-start(s32[2,2,2,128]{3,2,1,0:T(2,128)S(1)} %bitcast.66), channel_id=1, source_target_pairs={{0,16},{8,24},{16,0},{24,8},{1,17},{9,25},{17,1},{25,9},{2,18},{10... | collective-permute-start | bytes 12296 | tf_op jit(solution)/shard_map/ppermute | solution.py:316
  45.3 3.7 %collective-permute-start.5 = (s32[2,2,2,128]{3,2,1,0:T(2,128)S(1)}, s32[2,2,2,128]{3,2,1,0:T(2,128)S(1)}, u32[]{:S(2)}, u32[]{:S(2)}) collective-permute-start(s32[2,2,2,128]{3,2,1,0:T(2,128)S(1)} %get-tuple-element.34), channel_id=1, source_target_pairs={{0,8},{8,0},{16,24},{24,16},{1,9},{9,1},{17,25},{25,17},{2,10},{10... | collective-permute-start | bytes 12296 | tf_op jit(solution)/shard_map/ppermute | solution.py:316
  49.0 15.4 %collective-permute-start.6 = (s32[2,2,2,128]{3,2,1,0:T(2,128)S(1)}, s32[2,2,2,128]{3,2,1,0:T(2,128)S(1)}, u32[]{:S(2)}, u32[]{:S(2)}) collective-permute-start(s32[2,2,2,128]{3,2,1,0:T(2,128)S(1)} %get-tuple-element.32), channel_id=1, source_target_pairs={{0,2},{1,3},{2,0},{3,1},{4,6},{5,7},{6,4},{7,5},{8,10},{9,11},{10,... | collective-permute-start | bytes 12296 | tf_op jit(solution)/shard_map/ppermute | solution.py:316
  64.4 1.2 %collective-permute-start.7 = (s32[2,2,2,128]{3,2,1,0:T(2,128)S(1)}, s32[2,2,2,128]{3,2,1,0:T(2,128)S(1)}, u32[]{:S(2)}, u32[]{:S(2)}) collective-permute-start(s32[2,2,2,128]{3,2,1,0:T(2,128)S(1)} %get-tuple-element.30), channel_id=1, source_target_pairs={{0,1},{1,0},{2,3},{3,2},{4,5},{5,4},{6,7},{7,6},{8,9},{9,8},{10,11... | collective-permute-start | bytes 12296 | tf_op jit(solution)/shard_map/ppermute | solution.py:316
  75.8 0.7 copy-start.6
  76.5 0.6 copy-start.9
  87.2 24.6 %copy-start.1 = (f32[4096,128]{1,0:T(8,128)S(1)}, f32[4096,128]{1,0:T(8,128)}, u32[]{:S(2)}) copy-start(f32[4096,128]{1,0:T(8,128)} %copy-done) | copy-start | bytes 6291460
  87.2 24.6 %copy-start.8 = (s32[512]{0:T(512)S(1)}, s32[512]{0:T(512)}, u32[]{:S(2)}) copy-start(s32[512]{0:T(512)} %get-tuple-element.13.pos_ref) | copy-start | bytes 6148

commit v2 on v1

v2 whole, which is shorter than its diff:
```python
import functools

import jax
import jax.numpy as jnp
from jax import lax
from jax.experimental import pallas as pl
from jax.experimental.pallas import tpu as pltpu
from jax.sharding import Mesh
from jax.sharding import PartitionSpec as P

SLOTS = 48
DIFFUSE = 0.1
GROUP_AXES = ("lat", "lo")
LON_AXES = ("hi", "lo")

VMEM = pl.BlockSpec(memory_space=pltpu.VMEM)
ANY = pl.BlockSpec(memory_space=pl.ANY)
SMEM = pl.BlockSpec(memory_space=pltpu.SMEM)


def log2(n):
    return n.bit_length() - 1


def edge_kernel(q_hbm, u_hbm, v_hbm, first_ref, last_ref, low_ref, high_ref, q_side, u_side, wide, sems):
    rows, cells, width = q_hbm.shape
    side = q_side.shape[2]
    copies = []

    def copy(source, target):
        copies.append(pltpu.make_async_copy(source, target, sems.at[len(copies)]))
        copies[-1].start()

    copy(q_hbm.at[:, 0:side, :], q_side.at[0])
    copy(u_hbm.at[:, 0:side, :], u_side.at[0])
    copy(q_hbm.at[:, cells - side : cells, :], q_side.at[1])
    copy(u_hbm.at[:, cells - side : cells, :], u_side.at[1])
    copy(q_hbm.at[0], low_ref.at[:, 0:width])
    copy(v_hbm.at[0], low_ref.at[:, width:])
    copy(q_hbm.at[rows - 1], high_ref.at[:, 0:width])
    copy(v_hbm.at[rows - 1], high_ref.at[:, width:])
    for c in copies:
        c.wait()
    for n, (ref, j) in enumerate(((first_ref, 0), (last_ref, side - 1))):
        for i in range(rows):
            wide[i : i + 1, 0:width] = q_side[n, i].astype(jnp.float32)[j : j + 1]
            wide[i : i + 1, width:] = u_side[n, i].astype(jnp.float32)[j : j + 1]
        ref[...] = wide[...].astype(jnp.bfloat16)


def plan(place_ref, span_ref, slot_ref, send_ref, pos_ref, member, pos, cap, owned, lons, lows):
    rows, cells = span_ref.shape
    stored = cap + 1
    peers = send_ref.shape[0] // stored
    f32, bf16 = jnp.float32, jnp.bfloat16
    span, slot = span_ref[...], slot_ref[...]
    owner = span >> log2(owned)
    owner_lon = owner & (lons - 1)
    peer = ((owner >> log2(lons)) << log2(lows)) + (owner_lon & (lows - 1))
    far = (owner_lon >> log2(lows)) != place_ref[0]
    local = (span & (owned - 1)) + jnp.where(far, owned, 0)
    iota = lambda shape, axis: lax.broadcasted_iota(jnp.int32, shape, axis)
    for i in range(rows):
        member[i * peers : (i + 1) * peers, :] = jnp.where(
            iota((peers, cells), 0) == peer[i : i + 1], 1.0, 0.0
        )
    hot = member[...].astype(bf16)
    dot = functools.partial(jnp.dot, preferred_element_type=f32)
    within = dot(hot, (iota((cells, cells), 0) < iota((cells, cells), 1)).astype(f32).astype(bf16))
    pairs = (rows * peers, rows * peers)
    to, of = iota(pairs, 0), iota(pairs, 1)
    same = (to & (peers - 1)) == (of & (peers - 1))
    lower = jnp.where(same & (of < (to & -peers)), 1.0, 0.0).astype(bf16)
    before = within + jnp.sum(dot(lower, hot), axis=1, keepdims=True)
    before = before * member[...]
    lists = jnp.zeros((3 * peers, 128), f32)
    for i in range(rows):
        block = slice(i * peers, (i + 1) * peers)
        rank = jnp.sum(before[block], axis=0, keepdims=True).astype(jnp.int32)
        pos[i : i + 1, 0:cells] = peer[i : i + 1] * stored + rank
        pos_ref[i : i + 1, 0:cells] = peer[i : i + 1] * cap + rank
        chosen = jnp.where(iota((128, cells), 0) == rank, 1.0, 0.0).astype(bf16)
        mine = member[block]
        values = jnp.concatenate(
            [mine * local[i : i + 1].astype(f32), mine * slot[i : i + 1].astype(f32), mine], axis=0
        )
        lists = lists + lax.dot_general(
            values.astype(bf16), chosen, (((1,), (1,)), ((), ())), preferred_element_type=f32
        )
    spans = jnp.where(lists[2 * peers :] > 0.5, lists[:peers], 2.0 * owned)
    slots = lists[peers : 2 * peers]
    tile = send_ref.shape[1:]
    for p in range(peers):
        send_ref[p * stored + cap] = jnp.where(
            iota(tile, 0) == 0,
            jnp.broadcast_to(spans[p : p + 1], tile),
            jnp.broadcast_to(slots[p : p + 1], tile),
        ).astype(bf16)


def flux_kernel(
    cap,
    owned,
    lons,
    lows,
    place_ref,
    span_ref,
    slot_ref,
    q_ref,
    u_hbm,
    v_hbm,
    west_ref,
    east_ref,
    south_ref,
    north_ref,
    send_ref,
    pos_ref,
    dyn_hbm,
    member,
    pos,
    pos_s,
    u_ref,
    v_ref,
    dyn_ref,
    sems,
    row_sems,
    cell,
    wind,
    face_x,
    wind_y,
    face_y,
    edge,
    flux_y,
):
    rows, cells, width = q_ref.shape
    levels = u_ref.shape[2]
    tracers = width // levels
    f32 = jnp.float32
    line = (cells + 2) * tracers
    u_copy = pltpu.make_async_copy(u_hbm, u_ref, sems.at[0])
    v_copy = pltpu.make_async_copy(v_hbm, v_ref, sems.at[1])
    u_copy.start()
    v_copy.start()
    plan(place_ref, span_ref, slot_ref, send_ref, pos_ref, member, pos, cap, owned, lons, lows)
    pos_copy = pltpu.make_async_copy(pos, pos_s, sems.at[2])
    pos_copy.start()

    def spread(block, first, count, stride):
        for t in range(tracers):
            cell[pl.ds(first + t, count, stride=stride), :] = block(t).astype(f32)

    lanes = lambda t: slice(t * levels, (t + 1) * levels)
    spread(lambda t: south_ref[:, lanes(t)], tracers, cells, tracers)
    spread(lambda t: north_ref[:, lanes(t)], (rows + 1) * line + tracers, cells, tracers)
    spread(lambda t: west_ref[:, lanes(t)], line, rows, line)
    spread(lambda t: east_ref[:, lanes(t)], line + (cells + 1) * tracers, rows, line)

    def relayout(i, carry):
        spread(
            lambda t: q_ref[i, :, lanes(t)], (i + 1) * line + tracers, cells, tracers
        )
        return carry

    lax.fori_loop(0, rows, relayout, 0)

    u_copy.wait()
    v_copy.wait()
    edge[0:rows, :] = west_ref[:, width:].astype(f32)
    edge[rows : 2 * rows, :] = east_ref[:, width:].astype(f32)
    stride = face_x.shape[0] // rows

    def faces(i, carry):
        wind[0:1, :] = edge[pl.ds(i, 1), :]
        wind[1 : cells + 1, :] = u_ref[i].astype(f32)
        wind[cells + 1 : cells + 2, :] = edge[pl.ds(rows + i, 1), :]
        face_x[pl.ds(pl.multiple_of(i * stride, 8), stride), :] = 0.25 * (
            wind[0:stride, :] + wind[1 : stride + 1, :]
        )
        return carry

    lax.fori_loop(0, rows, faces, 0)
    wind_y[0:cells, :] = south_ref[:, width:].astype(f32)
    wind_y[cells : (rows + 1) * cells, :] = v_ref[...].reshape(rows * cells, levels).astype(f32)
    wind_y[(rows + 1) * cells :, :] = north_ref[:, width:].astype(f32)
    face_y[...] = 0.25 * (wind_y[: (rows + 1) * cells, :] + wind_y[cells:, :])
    south_open, north_open = place_ref[1].astype(f32), place_ref[2].astype(f32)
    face_y[0:cells, :] = face_y[0:cells, :] * south_open
    face_y[rows * cells :, :] = face_y[rows * cells :, :] * north_open

    def tile(i, j):
        first = (i * (cells + 2) + j) * tracers
        return cell[pl.ds(pl.multiple_of(first, tracers), tracers), :]

    def spread_row(ref, r):
        return jnp.broadcast_to(ref[pl.ds(r, 1), :], (tracers, levels))

    for j in range(cells):
        low, high = tile(0, j + 1), tile(1, j + 1)
        flux_y[j * tracers : (j + 1) * tracers, :] = spread_row(face_y, j) * (low + high) - (
            DIFFUSE * south_open
        ) * (high - low)

    pos_copy.wait()

    def dyn_copy(i):
        rows_i = pl.ds(pl.multiple_of(i * cells * tracers, tracers), cells * tracers)
        return pltpu.make_async_copy(dyn_ref.at[rows_i], dyn_hbm.at[rows_i], row_sems.at[i])

    def row(i, carry):
        diffuse_y = DIFFUSE * jnp.where(i == rows - 1, north_open, 1.0)
        here = tile(i + 1, 1)
        last = tile(i + 1, 0)
        flux_w = spread_row(face_x, i * stride) * (last + here) - DIFFUSE * (here - last)
        for j in range(cells):
            after = tile(i + 1, j + 2)
            flux_e = spread_row(face_x, i * stride + j + 1) * (here + after) - DIFFUSE * (
                after - here
            )
            above = tile(i + 2, j + 1)
            flux_n = spread_row(face_y, (i + 1) * cells + j) * (here + above) - diffuse_y * (
                above - here
            )
            flux_s = flux_y[j * tracers : (j + 1) * tracers, :]
            flux_y[j * tracers : (j + 1) * tracers, :] = flux_n
            dyn = (flux_w - flux_e) + (flux_s - flux_n)
            column = i * cells + j
            dyn_ref[pl.ds(pl.multiple_of(column * tracers, tracers), tracers), :] = dyn
            send_ref[pos_s[i, j]] = (here + dyn).astype(jnp.bfloat16)
            here, flux_w = after, flux_e
        dyn_copy(i).start()
        return carry

    lax.fori_loop(0, rows, row, 0)

    def drain(i, carry):
        dyn_copy(i).wait()
        return carry

    lax.fori_loop(0, rows, drain, 0)


def relax_kernel(x_ref, own_ref, near_ref, far_ref, y_ref, pos, pos_s, sem, slots):
    tracers, levels = x_ref.shape[1:]
    owned = own_ref.shape[0]
    peers, lanes = pos.shape
    stored = x_ref.shape[0] // peers
    cap = stored - 1
    f32 = jnp.float32
    for p in range(peers):
        listed = x_ref[p * stored + cap].astype(f32)
        pos[p : p + 1, :] = (listed[0:1] * SLOTS + listed[1:2]).astype(jnp.int32)
    copy = pltpu.make_async_copy(pos, pos_s, sem)
    copy.start()
    copy.wait()

    def place(at):
        return pl.ds(pl.multiple_of(at * tracers, tracers), tracers)

    def scatter(p, carry):
        for r in range(cap):
            slots[place(pos_s[p, r]), :] = x_ref[p * stored + r].astype(f32)
        return carry

    lax.fori_loop(0, peers, scatter, 0)
    block = SLOTS * tracers

    def relax(w_ref, first):
        def span(k, carry):
            at = pl.ds(pl.multiple_of((first + k) * block, block), block)
            x = slots[at, :]
            y = lax.dot_general(
                x.astype(jnp.bfloat16),
                w_ref[k],
                (((1,), (1,)), ((), ())),
                preferred_element_type=f32,
            )
            slots[at, :] = y - x
            return carry

        lax.fori_loop(0, w_ref.shape[0], span, 0, unroll=2)

    relax(own_ref, 0)
    relax(near_ref, owned)
    relax(far_ref, owned + near_ref.shape[0])

    def gather(p, carry):
        for r in range(cap):
            y_ref[p * cap + r] = slots[place(pos_s[p, r]), :].astype(jnp.bfloat16)
        return carry

    lax.fori_loop(0, peers, gather, 0)


def finish_kernel(pos_ref, y_ref, dyn_ref, out_ref, total):
    rows, cells, width = out_ref.shape
    tracers, levels = y_ref.shape[1:]
    first = pl.program_id(0) * rows

    def row(i, carry):
        for j in range(cells):
            column = i * cells + j
            at = pl.multiple_of(column * tracers, tracers)
            total[j * tracers : (j + 1) * tracers, :] = dyn_ref[pl.ds(at, tracers), :] + y_ref[
                pos_ref[first + i, j]
            ].astype(jnp.float32)
        for t in range(tracers):
            out_ref[i, :, t * levels : (t + 1) * levels] = total[
                pl.ds(t, cells, stride=tracers), :
            ]
        return carry

    lax.fori_loop(0, rows, row, 0)


def shift(x, axis, by, closed):
    count = lax.axis_size(axis)
    pairs = [(i, (i + by) % count) for i in range(count) if closed or 0 <= i + by < count]
    return lax.ppermute(x, axis, pairs)


def shards(tracers, east_wind, north_wind, span_of, slot_of, inverses):
    levels = east_wind.shape[2]
    rows, cells, width = tracers.shape
    kinds = width // levels
    columns = rows * cells
    lats, lows = lax.axis_size("lat"), lax.axis_size("lo")
    lons = lax.axis_size("hi") * lows
    peers = lats * lows
    owned = inverses.shape[0]
    cap = 2 * (3 * columns // (2 * lats * lons))
    stored = cap + 1
    lat, hi = lax.axis_index("lat"), lax.axis_index("hi")
    f32, bf16, i32 = jnp.float32, jnp.bfloat16, jnp.int32
    dma = pltpu.SemaphoreType.DMA
    params = lambda mib: pltpu.CompilerParams(vmem_limit_bytes=mib << 20)

    side = 8
    first, last, low, high = pl.pallas_call(
        edge_kernel,
        out_shape=(jax.ShapeDtypeStruct((rows, width + levels), bf16),) * 2
        + (jax.ShapeDtypeStruct((cells, width + levels), bf16),) * 2,
        in_specs=[ANY] * 3,
        out_specs=(VMEM,) * 4,
        scratch_shapes=[
            pltpu.VMEM((2, rows, side, width), bf16),
            pltpu.VMEM((2, rows, side, levels), bf16),
            pltpu.VMEM((rows, width + levels), f32),
            dma((8,)),
        ],
        compiler_params=params(8),
        name="edges",
    )(tracers, east_wind, north_wind)
    south = shift(high, "lat", 1, False)
    north = shift(low, "lat", -1, False)
    west = shift(last, LON_AXES, 1, True)
    east = shift(first, LON_AXES, -1, True)
    swap = lambda x: lax.ppermute(x, "hi", [(0, 1), (1, 0)])
    near = swap(inverses[: owned // 2])
    far = swap(inverses[owned // 2 :])

    place = jnp.stack([hi, lat > 0, lat < lats - 1]).astype(i32)
    stride = (cells + 1 + 7) // 8 * 8
    send, pos, dyn = pl.pallas_call(
        functools.partial(flux_kernel, cap, owned, lons, lows),
        out_shape=(
            jax.ShapeDtypeStruct((peers * stored, kinds, levels), bf16),
            jax.ShapeDtypeStruct((rows, 128), i32),
            jax.ShapeDtypeStruct((columns * kinds, levels), f32),
        ),
        in_specs=[SMEM, VMEM, VMEM, VMEM, ANY, ANY] + [VMEM] * 4,
        out_specs=(VMEM, VMEM, ANY),
        scratch_shapes=[
            pltpu.VMEM((rows * peers, cells), f32),
            pltpu.VMEM((rows, 128), i32),
            pltpu.SMEM((rows, 128), i32),
            pltpu.VMEM((rows, cells, levels), bf16),
            pltpu.VMEM((rows, cells, levels), bf16),
            pltpu.VMEM((columns * kinds, levels), f32),
            dma((3,)),
            dma((rows,)),
            pltpu.VMEM(((rows + 2) * (cells + 2) * kinds, levels), f32),
            pltpu.VMEM((stride + 8, levels), f32),
            pltpu.VMEM((rows * stride, levels), f32),
            pltpu.VMEM(((rows + 2) * cells, levels), f32),
            pltpu.VMEM(((rows + 1) * cells, levels), f32),
            pltpu.VMEM((2 * rows, levels), f32),
            pltpu.VMEM((cells * kinds, levels), f32),
        ],
        compiler_params=params(24),
        name="flux",
    )(place, span_of, slot_of, tracers, east_wind, north_wind, west, east, south, north)

    def exchange(x):
        x = x.reshape(peers, -1, kinds, levels)
        x = lax.all_to_all(x, GROUP_AXES, split_axis=0, concat_axis=0, tiled=True)
        return x.reshape(-1, kinds, levels)

    send, near = lax.optimization_barrier((send, near))
    arrived = exchange(send)
    physics = pl.pallas_call(
        relax_kernel,
        out_shape=jax.ShapeDtypeStruct((peers * cap, kinds, levels), bf16),
        in_specs=[VMEM] * 4,
        out_specs=VMEM,
        scratch_shapes=[
            pltpu.VMEM((peers, 128), i32),
            pltpu.SMEM((peers, 128), i32),
            dma,
            pltpu.VMEM(((2 * owned * SLOTS + 1) * kinds, levels), f32),
        ],
        compiler_params=params(24),
        name="relax",
    )(arrived, inverses, near, far)

    returned = exchange(physics)
    step = 4
    return pl.pallas_call(
        finish_kernel,
        out_shape=jax.ShapeDtypeStruct((rows, cells, width), f32),
        grid=(rows // step,),
        in_specs=[
            SMEM,
            pl.BlockSpec((peers * cap, kinds, levels), lambda i: (0, 0, 0)),
            pl.BlockSpec((step * cells * kinds, levels), lambda i: (i, 0)),
        ],
        out_specs=pl.BlockSpec((step, cells, width), lambda i: (i, 0, 0)),
        scratch_shapes=[pltpu.VMEM((cells * kinds, levels), f32)],
        compiler_params=params(16),
        name="finish",
    )(pos, returned, dyn)


def solution(mesh):
    lats, lons = mesh.devices.shape
    split = Mesh(mesh.devices.reshape(lats, 2, lons // 2), ("lat", "hi", "lo"))
    block = P("lat", LON_AXES, None)
    in_specs = (
        block,
        block,
        block,
        P("lat", LON_AXES),
        P("lat", LON_AXES),
        P(("lat", "hi", "lo"), None, None),
    )
    return jax.shard_map(shards, mesh=split, in_specs=in_specs, out_specs=block, check_vma=False)
```

time: 116 us -> 99.2 us (0.86)
  Pallas kernels: 31.2 us -> 16.4 us
  waiting for transfers between devices: 18.7 us -> 32.5 us
  starting transfers between devices: 29.2 us -> 16.4 us
  other arithmetic: 2.06 us -> 0.08 us
    pallas_call x3 -> x2, Pallas kernels: 18.2 us -> 7.51 us  [the longest x1 7.22 us: shards(): pl.pallas_call(functools.partial(flux_kernel, cap, owned, lons, lows), ou...]
    ppermute x5 -> x2, starting transfers between devices: 14.3 us -> 4.24 us  [shards(): swap = lambda x: lax.ppermute(x, 'hi', [(0, 1), (1, 0)])]
    ppermute x5 -> x2, waiting for transfers between devices: 18.7 us -> 25.7 us  [shards(): swap = lambda x: lax.ppermute(x, 'hi', [(0, 1), (1, 0)])]
    ppermute x4, waiting for transfers between devices: 0.01 us -> 4.86 us  [shift(): return lax.ppermute(x, axis, pairs)]
    pallas_call x1, Pallas kernels: 10 us -> 5.91 us  [shards(): pl.pallas_call(relax_kernel, out_shape=jax.ShapeDtypeStruct((peers * cap,...]
    unnamed x26 -> x22, local copies, waits for them, and re-layouts: 5.15 us -> 7.51 us
    all_to_all x1, waiting for transfers between devices: 0.01 us -> 1.96 us  [exchange(): x = lax.all_to_all(x, GROUP_AXES, split_axis=0, concat_axis=0, tiled=True)]
    squeeze x2 -> x0, local copies, waits for them, and re-layouts: 1.69 us -> none  [shards(): lat_edge = lambda i: jnp.concatenate([tracers[i], north_wind[i]], axis=1)]
  transfers between devices with their start and end apart: 10 -> 7, of which waited for: 4 -> 4; matrix products, arithmetic and copies ran while one was open for 4% -> 0% of each run, Pallas kernels for 13% -> 8%
where the time goes in v2:
time: 99.2 us; the launch traced here: 98.8 us
  waiting for transfers between devices  32.5 us (33%)
  blocking collectives  24.5 us (25%)
  starting transfers between devices  16.4 us (17%)
  Pallas kernels  16.4 us (17%)
  local copies, waits for them, and re-layouts  8.66 us (9%)
    ppermute x2, waiting for transfers between devices, shards(): swap = lambda x: lax.ppermute(x, 'hi', [(0, 1), (1, 0)])  25.7 us
    all_to_all x1, blocking collectives, exchange(): x = lax.all_to_all(x, GROUP_AXES, split_axis=0, concat_axis=0, tiled=True)  24.5 us
    ppermute x4, starting transfers between devices, shift(): return lax.ppermute(x, axis, pairs)  8.27 us
    unnamed x22, local copies, waits for them, and re-layouts  7.51 us
    pallas_call x1, Pallas kernels, shards(): pl.pallas_call(functools.partial(flux_kernel, cap, owned, lons, lows), ou...  7.22 us
    pallas_call x1, Pallas kernels, shards(): pl.pallas_call(relax_kernel, out_shape=jax.ShapeDtypeStruct((peers * cap,...  5.91 us
    ppermute x4, waiting for transfers between devices, shift(): return lax.ppermute(x, axis, pairs)  4.86 us
    ppermute x2, starting transfers between devices, shards(): swap = lambda x: lax.ppermute(x, 'hi', [(0, 1), (1, 0)])  4.24 us
  transfers between devices with their start and end apart: 7, of which 4 were waited for; matrix products, arithmetic and copies ran while one was open for 0% of the time, Pallas kernels for 8%

profile of v2, /device:TPU:0, one launch (start us, length us, event | category | flops | bytes accessed | tf_op | source)
XLA Modules:
  0.0 98.8 jit_solution(10433340293452624394)
XLA Ops:
  0.0 1.2 %fusion = (bf16[8,128,128]{2,1,0:T(8,128)(2,1)S(1)}, bf16[8,128,128]{2,1,0:T(8,128)(2,1)S(1)}) fusion(bf16[16,128,128]{2,1,0:T(8,128)(2,1)} %own_ref.1), kind=kLoop, calls=%fused_computation.1 | loop fusion | bytes 1048576 | tf_op jit(solution)/shard_map/slice | solution.py:359
  1.2 4.1 %collective-permute-start.4 = (bf16[8,128,128]{2,1,0:T(8,128)(2,1)S(1)}, bf16[8,128,128]{2,1,0:T(8,128)(2,1)S(1)}, u32[]{:S(2)}, u32[]{:S(2)}) collective-permute-start(bf16[8,128,128]{2,1,0:T(8,128)(2,1)S(1)} %get-tuple-element.24), channel_id=1, source_target_pairs={{0,4},{4,0},{1,5},{5,1},{2,6},{6,2},{3,7},{7,3},{8,12},{12,8},{9,1... | collective-permute-start | bytes 786440 | tf_op jit(solution)/shard_map/ppermute | solution.py:357
  5.3 0.9 copy-done.5
  6.2 0.9 copy-done.7
  7.1 0.3 edges.1
  7.4 0.1 collective-permute-start
  7.4 3.5 %collective-permute-start.1 = (bf16[16,1152]{1,0:T(8,128)(2,1)S(1)}, bf16[16,1152]{1,0:T(8,128)(2,1)S(1)}, u32[]{:S(2)}, u32[]{:S(2)}) collective-permute-start(bf16[16,1152]{1,0:T(8,128)(2,1)S(1)} %get-tuple-element.15), channel_id=1, source_target_pairs={{0,7},{1,0},{2,1},{3,2},{4,3},{5,4},{6,5},{7,6},{8,15},{9,8},{10,9... | collective-permute-start | bytes 110600 | tf_op jit(solution)/shard_map/ppermute | solution.py:318
  11.0 3.4 %collective-permute-start.2 = (bf16[32,1152]{1,0:T(8,128)(2,1)S(1)}, bf16[32,1152]{1,0:T(8,128)(2,1)S(1)}, u32[]{:S(2)}, u32[]{:S(2)}) collective-permute-start(bf16[32,1152]{1,0:T(8,128)(2,1)S(1)} %get-tuple-element.16), channel_id=1, source_target_pairs={{0,8},{8,16},{16,24},{1,9},{9,17},{17,25},{2,10},{10,18},{18,26},{... | collective-permute-start | bytes 221192 | tf_op jit(solution)/shard_map/ppermute | solution.py:318
  14.4 1.3 %collective-permute-start.3 = (bf16[32,1152]{1,0:T(8,128)(2,1)S(1)}, bf16[32,1152]{1,0:T(8,128)(2,1)S(1)}, u32[]{:S(2)}, u32[]{:S(2)}) collective-permute-start(bf16[32,1152]{1,0:T(8,128)(2,1)S(1)} %get-tuple-element.17), channel_id=1, source_target_pairs={{8,0},{16,8},{24,16},{9,1},{17,9},{25,17},{10,2},{18,10},{26,18},{... | collective-permute-start | bytes 221192 | tf_op jit(solution)/shard_map/ppermute | solution.py:318
  15.7 0.1 pad_add_fusion.place_ref
  15.7 0.0 collective-permute-done.west_ref
  15.7 0.0 collective-permute-done.1.east_ref
  15.8 0.6 collective-permute-done.2.south_ref
  16.3 4.3 %collective-permute-done.3.north_ref = bf16[32,1152]{1,0:T(8,128)(2,1)S(1)} collective-permute-done((bf16[32,1152]{1,0:T(8,128)(2,1)S(1)}, bf16[32,1152]{1,0:T(8,128)(2,1)S(1)}, u32[]{:S(2)}, u32[]{:S(2)}) %collective-permute-start.3) | collective-permute-done | bytes 73760 | tf_op jit(solution)/shard_map/ppermute | solution.py:318
  20.6 0.9 copy-done.6
  21.5 0.9 copy-done.8
  22.4 0.7 copy-done.9
  23.1 0.7 copy-done.10
  23.8 7.2 %flux.1 = (bf16[784,8,128]{2,1,0:T(8,128)(2,1)S(1)}, s32[16,128]{1,0:T(8,128)S(1)}, f32[4096,128]{1,0:T(8,128)S(1)}) custom-call(s32[3]{0:T(128)S(1)} %pad_add_fusion.place_ref, s32[16,32]{1,0:T(8,128)S(1)} %copy-done.9, s32[16,32]{1,0:T(8,128)S(1)} %copy-done.10, bf16[16,32,1024]{2,1,0:T(8,128)(2,1)S(1)} %copy-done, bf16[16,32,128]{2,1,0:T(8,128)(2,1)S(1)} %copy-done.6, ...), custom_call_target="tpu_custom_call" | custom-call | tf_op jit(solution)/shard_map/flux/pallas_call | solution.py:363
  31.0 0.0 copy-start.1
  31.1 1.3 %copy-done.1 = f32[4096,128]{1,0:T(8,128)} copy-done((f32[4096,128]{1,0:T(8,128)}, f32[4096,128]{1,0:T(8,128)S(1)}, u32[]{:S(2)}) %copy-start.1) | copy-done | bytes 2097176
  32.4 1.2 %copy-done.4 = bf16[784,8,128]{2,1,0:T(8,128)(2,1)} copy-done((bf16[784,8,128]{2,1,0:T(8,128)(2,1)}, bf16[784,8,128]{2,1,0:T(8,128)(2,1)S(1)}, u32[]{:S(2)}) %copy-start.4) | copy-done | bytes 1605656
  33.5 0.0 collective-permute-done.4.near_ref
  33.5 3.9 %all-to-all-start = ((bf16[16,49,8,128]{3,2,1,0:T(8,128)(2,1)}), bf16[16,49,8,128]{3,2,1,0:T(8,128)(2,1)S(1)}, u32[]{:S(2)}, u32[]{:S(2)}) async-start(bf16[16,49,8,128]{3,2,1,0:T(8,128)(2,1)} %bitcast.10), calls=%async_computation | async-start | bytes 3211264 | tf_op jit(solution)/shard_map/all_to_all | solution.py:395
  37.5 0.1 collective-permute-start.5
  37.6 25.7 %collective-permute-done.5.far_ref = bf16[8,128,128]{2,1,0:T(8,128)(2,1)S(1)} collective-permute-done((bf16[8,128,128]{2,1,0:T(8,128)(2,1)S(1)}, bf16[8,128,128]{2,1,0:T(8,128)(2,1)S(1)}, u32[]{:S(2)}, u32[]{:S(2)}) %collective-permute-start.5) | collective-permute-done | bytes 262176 | tf_op jit(solution)/shard_map/ppermute | solution.py:357
  63.3 2.0 %all-to-all-done = bf16[16,49,8,128]{3,2,1,0:T(8,128)(2,1)S(1)} async-done(((bf16[16,49,8,128]{3,2,1,0:T(8,128)(2,1)}), bf16[16,49,8,128]{3,2,1,0:T(8,128)(2,1)S(1)}, u32[]{:S(2)}, u32[]{:S(2)}) %all-to-all-start) | async-done | bytes 1605664 | tf_op jit(solution)/shard_map/all_to_all | solution.py:395
  65.3 0.0 copy-done.3
  65.3 5.9 %relax.1 = bf16[768,8,128]{2,1,0:T(8,128)(2,1)S(1)} custom-call(bf16[784,8,128]{2,1,0:T(8,128)(2,1)S(1)} %bitcast.7, bf16[16,128,128]{2,1,0:T(8,128)(2,1)S(1)} %copy-done.3, bf16[8,128,128]{2,1,0:T(8,128)(2,1)S(1)} %collective-permute-done.4.near_ref, bf16[8,128,128]{2,1,0:T(8,128)(2,1)S(1)} %collective-permute-done.5.far_ref), custom_call_target="tpu_custom_call" | custom-call | tf_op jit(solution)/shard_map/relax/pallas_call | solution.py:400
  71.2 0.0 copy-start.2
  71.2 24.5 %all_to_all.10 = bf16[16,48,8,128]{3,2,1,0:T(8,128)(2,1)S(1)} all-to-all(bf16[16,48,8,128]{3,2,1,0:T(8,128)(2,1)S(1)} %bitcast.8), channel_id=1, replica_groups=mesh['lat'=4,'hi'=2,'lo'=4] {'lat','lo'}, dimensions={0} | all-to-all | bytes 3145728 | tf_op jit(solution)/shard_map/all_to_all | solution.py:395
  95.8 3.0 %finish.1 = f32[16,32,1024]{2,1,0:T(8,128)} custom-call(s32[16,128]{1,0:T(8,128)S(1)} %get-tuple-element.18.pos_ref, bf16[768,8,128]{2,1,0:T(8,128)(2,1)S(1)} %bitcast.9, f32[4096,128]{1,0:T(8,128)S(1)} %copy-done.2), custom_call_target="tpu_custom_call" | custom-call | tf_op jit(solution)/shard_map/finish/pallas_call | solution.py:417
  (11 shorter events, 0.0 us)
Async XLA Ops:
  0.0 5.3 %copy-start = (bf16[16,32,1024]{2,1,0:T(8,128)(2,1)S(1)}, bf16[16,32,1024]{2,1,0:T(8,128)(2,1)}, u32[]{:S(2)}) copy-start(bf16[16,32,1024]{2,1,0:T(8,128)(2,1)} %q_ref.1) | copy-start | bytes 3145732
  1.2 32.4 %collective-permute-start.4 = (bf16[8,128,128]{2,1,0:T(8,128)(2,1)S(1)}, bf16[8,128,128]{2,1,0:T(8,128)(2,1)S(1)}, u32[]{:S(2)}, u32[]{:S(2)}) collective-permute-start(bf16[8,128,128]{2,1,0:T(8,128)(2,1)S(1)} %get-tuple-element.24), channel_id=1, source_target_pairs={{0,4},{4,0},{1,5},{5,1},{2,6},{6,2},{3,7},{7,3},{8,12},{12,8},{9,1... | collective-permute-start | bytes 786440 | tf_op jit(solution)/shard_map/ppermute | solution.py:357
  5.3 0.9 copy-start.5
  6.2 0.9 copy-start.7
  7.4 8.4 %collective-permute-start = (bf16[16,1152]{1,0:T(8,128)(2,1)S(1)}, bf16[16,1152]{1,0:T(8,128)(2,1)S(1)}, u32[]{:S(2)}, u32[]{:S(2)}) collective-permute-start(bf16[16,1152]{1,0:T(8,128)(2,1)S(1)} %get-tuple-element.14), channel_id=1, source_target_pairs={{0,1},{1,2},{2,3},{3,4},{4,5},{5,6},{6,7},{7,0},{8,9},{9,10},{10,1... | collective-permute-start | bytes 110600 | tf_op jit(solution)/shard_map/ppermute | solution.py:318
  7.4 8.3 %collective-permute-start.1 = (bf16[16,1152]{1,0:T(8,128)(2,1)S(1)}, bf16[16,1152]{1,0:T(8,128)(2,1)S(1)}, u32[]{:S(2)}, u32[]{:S(2)}) collective-permute-start(bf16[16,1152]{1,0:T(8,128)(2,1)S(1)} %get-tuple-element.15), channel_id=1, source_target_pairs={{0,7},{1,0},{2,1},{3,2},{4,3},{5,4},{6,5},{7,6},{8,15},{9,8},{10,9... | collective-permute-start | bytes 110600 | tf_op jit(solution)/shard_map/ppermute | solution.py:318
  11.0 5.4 %collective-permute-start.2 = (bf16[32,1152]{1,0:T(8,128)(2,1)S(1)}, bf16[32,1152]{1,0:T(8,128)(2,1)S(1)}, u32[]{:S(2)}, u32[]{:S(2)}) collective-permute-start(bf16[32,1152]{1,0:T(8,128)(2,1)S(1)} %get-tuple-element.16), channel_id=1, source_target_pairs={{0,8},{8,16},{16,24},{1,9},{9,17},{17,25},{2,10},{10,18},{18,26},{... | collective-permute-start | bytes 221192 | tf_op jit(solution)/shard_map/ppermute | solution.py:318
  14.4 6.2 %collective-permute-start.3 = (bf16[32,1152]{1,0:T(8,128)(2,1)S(1)}, bf16[32,1152]{1,0:T(8,128)(2,1)S(1)}, u32[]{:S(2)}, u32[]{:S(2)}) collective-permute-start(bf16[32,1152]{1,0:T(8,128)(2,1)S(1)} %get-tuple-element.17), channel_id=1, source_target_pairs={{8,0},{16,8},{24,16},{9,1},{17,9},{25,17},{10,2},{18,10},{26,18},{... | collective-permute-start | bytes 221192 | tf_op jit(solution)/shard_map/ppermute | solution.py:318
  20.6 0.9 copy-start.6
  21.5 0.9 copy-start.8
  22.4 0.7 copy-start.9
  23.1 0.7 copy-start.10
  31.0 1.3 %copy-start.1 = (f32[4096,128]{1,0:T(8,128)}, f32[4096,128]{1,0:T(8,128)S(1)}, u32[]{:S(2)}) copy-start(f32[4096,128]{1,0:T(8,128)S(1)} %get-tuple-element.22.dyn_ref) | copy-start | bytes 6291460
  32.4 1.2 %copy-start.4 = (bf16[784,8,128]{2,1,0:T(8,128)(2,1)}, bf16[784,8,128]{2,1,0:T(8,128)(2,1)S(1)}, u32[]{:S(2)}) copy-start(bf16[784,8,128]{2,1,0:T(8,128)(2,1)S(1)} %get-tuple-element.20) | copy-start | bytes 4816900
  33.5 31.7 %copy-start.3 = (bf16[16,128,128]{2,1,0:T(8,128)(2,1)S(1)}, bf16[16,128,128]{2,1,0:T(8,128)(2,1)}, u32[]{:S(2)}) copy-start(bf16[16,128,128]{2,1,0:T(8,128)(2,1)} %own_ref.1) | copy-start | bytes 1572868
  33.5 31.7 %all-to-all-start = ((bf16[16,49,8,128]{3,2,1,0:T(8,128)(2,1)}), bf16[16,49,8,128]{3,2,1,0:T(8,128)(2,1)S(1)}, u32[]{:S(2)}, u32[]{:S(2)}) async-start(bf16[16,49,8,128]{3,2,1,0:T(8,128)(2,1)} %bitcast.10), calls=%async_computation | async-start | bytes 3211264 | tf_op jit(solution)/shard_map/all_to_all | solution.py:395
  37.5 25.9 %collective-permute-start.5 = (bf16[8,128,128]{2,1,0:T(8,128)(2,1)S(1)}, bf16[8,128,128]{2,1,0:T(8,128)(2,1)S(1)}, u32[]{:S(2)}, u32[]{:S(2)}) collective-permute-start(bf16[8,128,128]{2,1,0:T(8,128)(2,1)S(1)} %get-tuple-element.23), channel_id=1, source_target_pairs={{0,4},{4,0},{1,5},{5,1},{2,6},{6,2},{3,7},{7,3},{8,12},{12,8},{9,1... | collective-permute-start | bytes 786440 | tf_op jit(solution)/shard_map/ppermute | solution.py:357
  71.2 24.6 %copy-start.2 = (f32[4096,128]{1,0:T(8,128)S(1)}, f32[4096,128]{1,0:T(8,128)}, u32[]{:S(2)}) copy-start(f32[4096,128]{1,0:T(8,128)} %copy-done.1) | copy-start | bytes 6291460

commit v3 on v2

--- a/solution.py
+++ b/solution.py
@@ -8,13 +8,15 @@
 from jax.sharding import Mesh
 from jax.sharding import PartitionSpec as P
 
+FLUX_COST = 10
+TURN_COST = 30
 SLOTS = 48
 DIFFUSE = 0.1
 GROUP_AXES = ("lat", "lo")
 LON_AXES = ("hi", "lo")
 
 VMEM = pl.BlockSpec(memory_space=pltpu.VMEM)
-ANY = pl.BlockSpec(memory_space=pl.ANY)
+ANY = pl.BlockSpec(memory_space=pltpu.HBM)
 SMEM = pl.BlockSpec(memory_space=pltpu.SMEM)
 
 
@@ -22,30 +24,41 @@
     return n.bit_length() - 1
 
 
-def edge_kernel(q_hbm, u_hbm, v_hbm, first_ref, last_ref, low_ref, high_ref, q_side, u_side, wide, sems):
+def parities(place, lons):
+    return place & 1, (place >> log2(lons)) & 1
+
+
+def edge_kernel(
+    lons, place_ref, q_hbm, u_hbm, v_hbm, lon_a, lon_b, lat_a, lat_b, q_side, u_side, wide, sems
+):
     rows, cells, width = q_hbm.shape
     side = q_side.shape[2]
+    odd_lon, odd_lat = parities(place_ref[0], lons)
     copies = []
 
     def copy(source, target):
         copies.append(pltpu.make_async_copy(source, target, sems.at[len(copies)]))
         copies[-1].start()
 
-    copy(q_hbm.at[:, 0:side, :], q_side.at[0])
-    copy(u_hbm.at[:, 0:side, :], u_side.at[0])
-    copy(q_hbm.at[:, cells - side : cells, :], q_side.at[1])
-    copy(u_hbm.at[:, cells - side : cells, :], u_side.at[1])
-    copy(q_hbm.at[0], low_ref.at[:, 0:width])
-    copy(v_hbm.at[0], low_ref.at[:, width:])
-    copy(q_hbm.at[rows - 1], high_ref.at[:, 0:width])
-    copy(v_hbm.at[rows - 1], high_ref.at[:, width:])
-    for c in copies:
+    for n, odd in enumerate((odd_lon, 1 - odd_lon)):
+        near = pl.ds(pl.multiple_of(jnp.where(odd == 1, 0, cells - side), side), side)
+        copy(q_hbm.at[:, near, :], q_side.at[n])
+        copy(u_hbm.at[:, near, :], u_side.at[n])
+    for ref, odd in ((lat_a, odd_lat), (lat_b, 1 - odd_lat)):
+        i = jnp.where(odd == 1, 0, rows - 1)
+        copy(q_hbm.at[i], ref.at[:, 0:width])
+        copy(v_hbm.at[i], ref.at[:, width:])
+    for c in copies[:4]:
         c.wait()
-    for n, (ref, j) in enumerate(((first_ref, 0), (last_ref, side - 1))):
+    for n, (ref, odd) in enumerate(((lon_a, odd_lon), (lon_b, 1 - odd_lon))):
+        first = odd == 1
         for i in range(rows):
-            wide[i : i + 1, 0:width] = q_side[n, i].astype(jnp.float32)[j : j + 1]
-            wide[i : i + 1, width:] = u_side[n, i].astype(jnp.float32)[j : j + 1]
+            q, u = q_side[n, i].astype(jnp.float32), u_side[n, i].astype(jnp.float32)
+            wide[i : i + 1, 0:width] = jnp.where(first, q[0:1], q[side - 1 :])
+            wide[i : i + 1, width:] = jnp.where(first, u[0:1], u[side - 1 :])
         ref[...] = wide[...].astype(jnp.bfloat16)
+    for c in copies[4:]:
+        c.wait()
 
 
 def plan(place_ref, span_ref, slot_ref, send_ref, pos_ref, member, pos, cap, owned, lons, lows):
@@ -57,7 +70,7 @@
     owner = span >> log2(owned)
     owner_lon = owner & (lons - 1)
     peer = ((owner >> log2(lons)) << log2(lows)) + (owner_lon & (lows - 1))
-    far = (owner_lon >> log2(lows)) != place_ref[0]
+    far = (owner_lon >> log2(lows)) != ((place_ref[0] >> log2(lows)) & 1)
     local = (span & (owned - 1)) + jnp.where(far, owned, 0)
     iota = lambda shape, axis: lax.broadcasted_iota(jnp.int32, shape, axis)
     for i in range(rows):
@@ -101,70 +114,74 @@
 def flux_kernel(
     cap,
     owned,
+    lats,
     lons,
     lows,
     place_ref,
-    span_ref,
-    slot_ref,
-    q_ref,
-    u_hbm,
-    v_hbm,
-    west_ref,
-    east_ref,
-    south_ref,
-    north_ref,
-    send_ref,
-    pos_ref,
-    dyn_hbm,
-    member,
-    pos,
-    pos_s,
-    u_ref,
-    v_ref,
-    dyn_ref,
-    sems,
-    row_sems,
-    cell,
-    wind,
-    face_x,
-    wind_y,
-    face_y,
-    edge,
-    flux_y,
+    *refs,
 ):
+    sources, (send_ref, pos_ref, dyn_hbm), rest = refs[:9], refs[9:12], refs[12:]
+    held, rest = rest[:7], rest[7:]
+    (
+        sems,
+        row_sems,
+        member,
+        pos,
+        pos_s,
+        dyn_ref,
+        cell,
+        wind,
+        face_x,
+        wind_y,
+        face_y,
+        edge,
+        flux_y,
+    ) = rest
+    span_ref, slot_ref, q_ref, u_ref, v_ref, lon_ref, lat_ref = held
+    west_ref, east_ref = lon_ref.at[0], lon_ref.at[1]
+    south_ref, north_ref = lat_ref.at[0], lat_ref.at[1]
+    odd_lon, odd_lat = parities(place_ref[0], lons)
+    targets = held[:5] + (
+        lon_ref.at[1 - odd_lon],
+        lon_ref.at[odd_lon],
+        lat_ref.at[1 - odd_lat],
+        lat_ref.at[odd_lat],
+    )
     rows, cells, width = q_ref.shape
     levels = u_ref.shape[2]
     tracers = width // levels
     f32 = jnp.float32
     line = (cells + 2) * tracers
-    u_copy = pltpu.make_async_copy(u_hbm, u_ref, sems.at[0])
-    v_copy = pltpu.make_async_copy(v_hbm, v_ref, sems.at[1])
-    u_copy.start()
-    v_copy.start()
-    plan(place_ref, span_ref, slot_ref, send_ref, pos_ref, member, pos, cap, owned, lons, lows)
-    pos_copy = pltpu.make_async_copy(pos, pos_s, sems.at[2])
-    pos_copy.start()
+    copies = [pltpu.make_async_copy(a, b, sems.at[n]) for n, (a, b) in enumerate(zip(sources, targets))]
+    for copy in copies:
+        copy.start()
 
     def spread(block, first, count, stride):
         for t in range(tracers):
             cell[pl.ds(first + t, count, stride=stride), :] = block(t).astype(f32)
 
     lanes = lambda t: slice(t * levels, (t + 1) * levels)
+    copies[2].wait()
+
+    def relayout(i, carry):
+        spread(
+            lambda t: q_ref[i, :, lanes(t)], (i + 1) * line + tracers, cells, tracers
+        )
+        return carry
+
+    lax.fori_loop(0, rows, relayout, 0)
+    for copy in copies[:2]:
+        copy.wait()
+    plan(place_ref, span_ref, slot_ref, send_ref, pos_ref, member, pos, cap, owned, lons, lows)
+    pos_copy = pltpu.make_async_copy(pos, pos_s, sems.at[len(copies)])
+    pos_copy.start()
+    for copy in copies[3:]:
+        copy.wait()
     spread(lambda t: south_ref[:, lanes(t)], tracers, cells, tracers)
     spread(lambda t: north_ref[:, lanes(t)], (rows + 1) * line + tracers, cells, tracers)
     spread(lambda t: west_ref[:, lanes(t)], line, rows, line)
     spread(lambda t: east_ref[:, lanes(t)], line + (cells + 1) * tracers, rows, line)
 
-    def relayout(i, carry):
-        spread(
-            lambda t: q_ref[i, :, lanes(t)], (i + 1) * line + tracers, cells, tracers
-        )
-        return carry
-
-    lax.fori_loop(0, rows, relayout, 0)
-
-    u_copy.wait()
-    v_copy.wait()
     edge[0:rows, :] = west_ref[:, width:].astype(f32)
     edge[rows : 2 * rows, :] = east_ref[:, width:].astype(f32)
     stride = face_x.shape[0] // rows
@@ -183,7 +200,9 @@
     wind_y[cells : (rows + 1) * cells, :] = v_ref[...].reshape(rows * cells, levels).astype(f32)
     wind_y[(rows + 1) * cells :, :] = north_ref[:, width:].astype(f32)
     face_y[...] = 0.25 * (wind_y[: (rows + 1) * cells, :] + wind_y[cells:, :])
-    south_open, north_open = place_ref[1].astype(f32), place_ref[2].astype(f32)
+    lat = place_ref[0] >> log2(lons)
+    south_open = jnp.where(lat > 0, 1.0, 0.0)
+    north_open = jnp.where(lat < lats - 1, 1.0, 0.0)
     face_y[0:cells, :] = face_y[0:cells, :] * south_open
     face_y[rows * cells :, :] = face_y[rows * cells :, :] * north_open
 
@@ -239,9 +258,15 @@
     lax.fori_loop(0, rows, drain, 0)
 
 
-def relax_kernel(x_ref, own_ref, near_ref, far_ref, y_ref, pos, pos_s, sem, slots):
+def turn_kernel(own_ref, pair_ref, out_ref):
+    owned = own_ref.shape[0]
+    for k in range(owned):
+        out_ref[k] = own_ref[k].T
+        out_ref[owned + k] = pair_ref[k].T
+
+
+def relax_kernel(x_ref, w_ref, y_ref, pos, pos_s, sem, slots):
     tracers, levels = x_ref.shape[1:]
-    owned = own_ref.shape[0]
     peers, lanes = pos.shape
     stored = x_ref.shape[0] // peers
     cap = stored - 1
@@ -264,24 +289,14 @@
     lax.fori_loop(0, peers, scatter, 0)
     block = SLOTS * tracers
 
-    def relax(w_ref, first):
-        def span(k, carry):
-            at = pl.ds(pl.multiple_of((first + k) * block, block), block)
-            x = slots[at, :]
-            y = lax.dot_general(
-                x.astype(jnp.bfloat16),
-                w_ref[k],
-                (((1,), (1,)), ((), ())),
-                preferred_element_type=f32,
-            )
-            slots[at, :] = y - x
-            return carry
-
-        lax.fori_loop(0, w_ref.shape[0], span, 0, unroll=2)
-
-    relax(own_ref, 0)
-    relax(near_ref, owned)
-    relax(far_ref, owned + near_ref.shape[0])
+    def span(k, carry):
+        at = pl.ds(pl.multiple_of(k * block, block), block)
+        x = slots[at, :]
+        y = jnp.dot(x.astype(jnp.bfloat16), w_ref[k], preferred_element_type=f32)
+        slots[at, :] = y - x
+        return carry
+
+    lax.fori_loop(0, w_ref.shape[0], span, 0, unroll=8)
 
     def gather(p, carry):
         for r in range(cap):
@@ -291,31 +306,37 @@
     lax.fori_loop(0, peers, gather, 0)
 
 
-def finish_kernel(pos_ref, y_ref, dyn_ref, out_ref, total):
-    rows, cells, width = out_ref.shape
+def finish_kernel(pos_ref, y_ref, dyn_ref, out_hbm, total, out, sems):
+    rows, cells, width = out.shape
     tracers, levels = y_ref.shape[1:]
-    first = pl.program_id(0) * rows
+
+    def copy(i):
+        return pltpu.make_async_copy(out.at[i], out_hbm.at[i], sems.at[i])
 
     def row(i, carry):
         for j in range(cells):
-            column = i * cells + j
-            at = pl.multiple_of(column * tracers, tracers)
+            at = pl.multiple_of((i * cells + j) * tracers, tracers)
             total[j * tracers : (j + 1) * tracers, :] = dyn_ref[pl.ds(at, tracers), :] + y_ref[
-                pos_ref[first + i, j]
+                pos_ref[i, j]
             ].astype(jnp.float32)
         for t in range(tracers):
-            out_ref[i, :, t * levels : (t + 1) * levels] = total[
-                pl.ds(t, cells, stride=tracers), :
-            ]
+            out[i, :, t * levels : (t + 1) * levels] = total[pl.ds(t, cells, stride=tracers), :]
+        copy(i).start()
         return carry
 
     lax.fori_loop(0, rows, row, 0)
 
-
-def shift(x, axis, by, closed):
+    def drain(i, carry):
+        copy(i).wait()
+        return carry
+
+    lax.fori_loop(0, rows, drain, 0)
+
+
+def in_pairs(x, axis, first):
     count = lax.axis_size(axis)
-    pairs = [(i, (i + by) % count) for i in range(count) if closed or 0 <= i + by < count]
-    return lax.ppermute(x, axis, pairs)
+    pairs = [(i % count, (i + 1) % count) for i in range(first, count + first, 2)]
+    return lax.ppermute(x, axis, pairs + [(b, a) for a, b in pairs])
 
 
 def shards(tracers, east_wind, north_wind, span_of, slot_of, inverses):
@@ -329,17 +350,17 @@
     owned = inverses.shape[0]
     cap = 2 * (3 * columns // (2 * lats * lons))
     stored = cap + 1
-    lat, hi = lax.axis_index("lat"), lax.axis_index("hi")
     f32, bf16, i32 = jnp.float32, jnp.bfloat16, jnp.int32
     dma = pltpu.SemaphoreType.DMA
     params = lambda mib: pltpu.CompilerParams(vmem_limit_bytes=mib << 20)
 
     side = 8
-    first, last, low, high = pl.pallas_call(
-        edge_kernel,
+    place = lax.axis_index(("lat", "hi", "lo")).astype(i32).reshape(1)
+    lon_a, lon_b, lat_a, lat_b = pl.pallas_call(
+        functools.partial(edge_kernel, lons),
         out_shape=(jax.ShapeDtypeStruct((rows, width + levels), bf16),) * 2
         + (jax.ShapeDtypeStruct((cells, width + levels), bf16),) * 2,
-        in_specs=[ANY] * 3,
+        in_specs=[SMEM] + [ANY] * 3,
         out_specs=(VMEM,) * 4,
         scratch_shapes=[
             pltpu.VMEM((2, rows, side, width), bf16),
@@ -347,37 +368,35 @@
             pltpu.VMEM((rows, width + levels), f32),
             dma((8,)),
         ],
-        compiler_params=params(8),
+        compiler_params=params(62),
         name="edges",
-    )(tracers, east_wind, north_wind)
-    south = shift(high, "lat", 1, False)
-    north = shift(low, "lat", -1, False)
-    west = shift(last, LON_AXES, 1, True)
-    east = shift(first, LON_AXES, -1, True)
-    swap = lambda x: lax.ppermute(x, "hi", [(0, 1), (1, 0)])
-    near = swap(inverses[: owned // 2])
-    far = swap(inverses[owned // 2 :])
-
-    place = jnp.stack([hi, lat > 0, lat < lats - 1]).astype(i32)
+    )(place, tracers, east_wind, north_wind)
+    lon_a, lon_b = in_pairs(lon_a, LON_AXES, 0), in_pairs(lon_b, LON_AXES, 1)
+    lat_a, lat_b = in_pairs(lat_a, "lat", 0), in_pairs(lat_b, "lat", 1)
+    matrices, lon_a, lon_b = lax.optimization_barrier((inverses, lon_a, lon_b))
+    pair = lax.ppermute(matrices, "hi", [(0, 1), (1, 0)])
+
     stride = (cells + 1 + 7) // 8 * 8
+    fields = (span_of, slot_of, tracers, east_wind, north_wind, lon_a, lon_b, lat_a, lat_b)
+    held = [(x.shape, x.dtype) for x in fields[:5]] + [((2,) + x.shape, x.dtype) for x in (lon_a, lat_a)]
+    cost = lambda us: pl.CostEstimate(flops=us * 1_000_000_000, bytes_accessed=1 << 20, transcendentals=0)
     send, pos, dyn = pl.pallas_call(
-        functools.partial(flux_kernel, cap, owned, lons, lows),
+        functools.partial(flux_kernel, cap, owned, lats, lons, lows),
         out_shape=(
             jax.ShapeDtypeStruct((peers * stored, kinds, levels), bf16),
             jax.ShapeDtypeStruct((rows, 128), i32),
             jax.ShapeDtypeStruct((columns * kinds, levels), f32),
         ),
-        in_specs=[SMEM, VMEM, VMEM, VMEM, ANY, ANY] + [VMEM] * 4,
+        in_specs=[SMEM] + [ANY] * 9,
         out_specs=(VMEM, VMEM, ANY),
-        scratch_shapes=[
+        scratch_shapes=[pltpu.VMEM(*x) for x in held]
+        + [
+            dma((10,)),
+            dma((rows,)),
             pltpu.VMEM((rows * peers, cells), f32),
             pltpu.VMEM((rows, 128), i32),
             pltpu.SMEM((rows, 128), i32),
-            pltpu.VMEM((rows, cells, levels), bf16),
-            pltpu.VMEM((rows, cells, levels), bf16),
             pltpu.VMEM((columns * kinds, levels), f32),
-            dma((3,)),
-            dma((rows,)),
             pltpu.VMEM(((rows + 2) * (cells + 2) * kinds, levels), f32),
             pltpu.VMEM((stride + 8, levels), f32),
             pltpu.VMEM((rows * stride, levels), f32),
@@ -386,21 +405,30 @@
             pltpu.VMEM((2 * rows, levels), f32),
             pltpu.VMEM((cells * kinds, levels), f32),
         ],
-        compiler_params=params(24),
+        compiler_params=params(62),
+        cost_estimate=cost(FLUX_COST),
         name="flux",
-    )(place, span_of, slot_of, tracers, east_wind, north_wind, west, east, south, north)
+    )(place, *fields)
 
     def exchange(x):
         x = x.reshape(peers, -1, kinds, levels)
         x = lax.all_to_all(x, GROUP_AXES, split_axis=0, concat_axis=0, tiled=True)
         return x.reshape(-1, kinds, levels)
 
-    send, near = lax.optimization_barrier((send, near))
     arrived = exchange(send)
+    turned = pl.pallas_call(
+        turn_kernel,
+        out_shape=jax.ShapeDtypeStruct((2 * owned, levels, levels), bf16),
+        in_specs=[VMEM] * 2,
+        out_specs=VMEM,
+        compiler_params=params(16),
+        cost_estimate=cost(TURN_COST),
+        name="turn",
+    )(inverses, pair)
     physics = pl.pallas_call(
         relax_kernel,
         out_shape=jax.ShapeDtypeStruct((peers * cap, kinds, levels), bf16),
-        in_specs=[VMEM] * 4,
+        in_specs=[VMEM] * 2,
         out_specs=VMEM,
         scratch_shapes=[
             pltpu.VMEM((peers, 128), i32),
@@ -410,21 +438,19 @@
         ],
         compiler_params=params(24),
         name="relax",
-    )(arrived, inverses, near, far)
+    )(arrived, turned)
 
     returned = exchange(physics)
-    step = 4
     return pl.pallas_call(
         finish_kernel,
         out_shape=jax.ShapeDtypeStruct((rows, cells, width), f32),
-        grid=(rows // step,),
-        in_specs=[
-            SMEM,
-            pl.BlockSpec((peers * cap, kinds, levels), lambda i: (0, 0, 0)),
-            pl.BlockSpec((step * cells * kinds, levels), lambda i: (i, 0)),
+        in_specs=[SMEM, VMEM, VMEM],
+        out_specs=ANY,
+        scratch_shapes=[
+            pltpu.VMEM((cells * kinds, levels), f32),
+            pltpu.VMEM((rows, cells, width), f32),
+            dma((rows,)),
         ],
-        out_specs=pl.BlockSpec((step, cells, width), lambda i: (i, 0, 0)),
-        scratch_shapes=[pltpu.VMEM((cells * kinds, levels), f32)],
         compiler_params=params(16),
         name="finish",
     )(pos, returned, dyn)

time: 99.2 us -> 86.9 us (0.88)
  local copies, waits for them, and re-layouts: 8.66 us -> 3.13 us
  waiting for transfers between devices: 32.5 us -> 29.5 us
  starting transfers between devices: 16.4 us -> 14.4 us
  Pallas kernels: 16.4 us -> 14.8 us
    ppermute x6 -> x5, waiting for transfers between devices: 30.6 us -> 13.1 us  [the longest x1 11.1 us: shards(): pair = lax.ppermute(matrices, 'hi', [(0, 1), (1, 0)])]
    all_to_all x1, waiting for transfers between devices: 1.96 us -> 16.4 us  [exchange(): x = lax.all_to_all(x, GROUP_AXES, split_axis=0, concat_axis=0, tiled=True)]
    unnamed x22 -> x18, local copies, waits for them, and re-layouts: 7.51 us -> 3.13 us
    ppermute x6 -> x5, starting transfers between devices: 12.5 us -> 8.72 us  [the longest x4 8.21 us: in_pairs(): return lax.ppermute(x, axis, pairs + [(b, a) for a, b in pairs])]
    pallas_call x1, Pallas kernels: 5.91 us -> 3.91 us  [shards(): pl.pallas_call(relax_kernel, out_shape=jax.ShapeDtypeStruct((peers * cap,...]
    all_to_all x1, starting transfers between devices: 3.91 us -> 5.66 us  [exchange(): x = lax.all_to_all(x, GROUP_AXES, split_axis=0, concat_axis=0, tiled=True)]
    slice x1 -> x0, local copies, waits for them, and re-layouts: 1.15 us -> none  [shards(): far = swap(inverses[owned // 2:])]
    pallas_call x2 -> x3, Pallas kernels: 7.51 us -> 8.54 us  [the longest x1 6.23 us: shards(): pl.pallas_call(functools.partial(flux_kernel, cap, owned, lats, lons, low...]
  transfers between devices with their start and end apart: 7 -> 6, of which waited for: 4 -> 3; matrix products, arithmetic and copies ran while one was open for 0% -> 0% of each run, Pallas kernels for 8% -> 8%
where the time goes in v3:
time: 86.9 us; the launch traced here: 86.5 us
  waiting for transfers between devices  29.5 us (34%)
  blocking collectives  24.5 us (28%)
  Pallas kernels  14.8 us (17%)
  starting transfers between devices  14.4 us (17%)
  local copies, waits for them, and re-layouts  3.13 us (4%)
    all_to_all x1, blocking collectives, exchange(): x = lax.all_to_all(x, GROUP_AXES, split_axis=0, concat_axis=0, tiled=True)  24.5 us
    all_to_all x1, waiting for transfers between devices, exchange(): x = lax.all_to_all(x, GROUP_AXES, split_axis=0, concat_axis=0, tiled=True)  16.4 us
    ppermute x1, waiting for transfers between devices, shards(): pair = lax.ppermute(matrices, 'hi', [(0, 1), (1, 0)])  11.1 us
    ppermute x4, starting transfers between devices, in_pairs(): return lax.ppermute(x, axis, pairs + [(b, a) for a, b in pairs])  8.21 us
    pallas_call x1, Pallas kernels, shards(): pl.pallas_call(functools.partial(flux_kernel, cap, owned, lats, lons, low...  6.23 us
    all_to_all x1, starting transfers between devices, exchange(): x = lax.all_to_all(x, GROUP_AXES, split_axis=0, concat_axis=0, tiled=True)  5.66 us
    pallas_call x1, Pallas kernels, shards(): pl.pallas_call(relax_kernel, out_shape=jax.ShapeDtypeStruct((peers * cap,...  3.91 us
    unnamed x18, local copies, waits for them, and re-layouts  3.13 us
  transfers between devices with their start and end apart: 6, of which 3 were waited for; matrix products, arithmetic and copies ran while one was open for 0% of the time, Pallas kernels for 8%

profile of v3, /device:TPU:0, one launch (start us, length us, event | category | flops | bytes accessed | tf_op | source)
XLA Modules:
  0.0 86.5 jit_solution(2522451425709003084)
XLA Ops:
  0.0 2.0 %edges.1 = (bf16[16,1152]{1,0:T(8,128)(2,1)}, bf16[16,1152]{1,0:T(8,128)(2,1)}, bf16[32,1152]{1,0:T(8,128)(2,1)}, bf16[32,1152]{1,0:T(8,128)(2,1)}) custom-call(s32[1]{0:T(128)} %bitcast.place_ref, bf16[16,32,1024]{2,1,0:T(8,128)(2,1)} %refs_2_.1, bf16[16,32,128]{2,1,0:T(8,128)(2,1)} %refs_3_.1, bf16[16,32,128]{2,1,0:T(8,128)(2,1)} %refs_4_.1), custom_call_target="tpu_custom_call" | custom-call | tf_op jit(solution)/shard_map/edges/pallas_call | solution.py:359
  2.0 3.0 %collective-permute-start.2 = (bf16[32,1152]{1,0:T(8,128)(2,1)}, bf16[32,1152]{1,0:T(8,128)(2,1)S(1)}, u32[]{:S(2)}, u32[]{:S(2)}) collective-permute-start(bf16[32,1152]{1,0:T(8,128)(2,1)} %get-tuple-element.19), channel_id=1, source_target_pairs={{0,8},{16,24},{8,0},{24,16},{1,9},{17,25},{9,1},{25,17},{2,10},{18... | collective-permute-start | bytes 221192 | tf_op jit(solution)/shard_map/ppermute | solution.py:339
  5.0 1.5 %collective-permute-start.3 = (bf16[32,1152]{1,0:T(8,128)(2,1)}, bf16[32,1152]{1,0:T(8,128)(2,1)S(1)}, u32[]{:S(2)}, u32[]{:S(2)}) collective-permute-start(bf16[32,1152]{1,0:T(8,128)(2,1)} %get-tuple-element.20), channel_id=1, source_target_pairs={{8,16},{24,0},{16,8},{0,24},{9,17},{25,1},{17,9},{1,25},{10,18},{2... | collective-permute-start | bytes 221192 | tf_op jit(solution)/shard_map/ppermute | solution.py:339
  6.5 0.0 collective-permute-start
  6.5 3.7 %collective-permute-start.1 = (bf16[16,1152]{1,0:T(8,128)(2,1)}, bf16[16,1152]{1,0:T(8,128)(2,1)S(1)}, u32[]{:S(2)}, u32[]{:S(2)}) collective-permute-start(bf16[16,1152]{1,0:T(8,128)(2,1)} %get-tuple-element.16), channel_id=1, source_target_pairs={{1,2},{3,4},{5,6},{7,0},{2,1},{4,3},{6,5},{0,7},{9,10},{11,12},{13... | collective-permute-start | bytes 110600 | tf_op jit(solution)/shard_map/ppermute | solution.py:339
  10.2 0.0 collective-permute-done.refs_5_
  10.2 0.0 copy-start.7
  10.2 2.0 %collective-permute-done.1.refs_6_ = bf16[16,1152]{1,0:T(8,128)(2,1)S(1)} collective-permute-done((bf16[16,1152]{1,0:T(8,128)(2,1)}, bf16[16,1152]{1,0:T(8,128)(2,1)S(1)}, u32[]{:S(2)}, u32[]{:S(2)}) %collective-permute-start.1) | collective-permute-done | bytes 36896 | tf_op jit(solution)/shard_map/ppermute | solution.py:339
  12.2 0.0 copy-start.8
  12.2 0.5 collective-permute-start.4
  12.7 0.0 collective-permute-done.2.refs_7_
  12.7 0.0 collective-permute-done.3.refs_8_
  12.7 0.0 copy-done.7
  12.7 0.1 copy-done.8
  12.8 0.5 copy-done.5
  13.3 0.6 copy-done.6
  13.9 6.2 %flux.1 = (bf16[784,8,128]{2,1,0:T(8,128)(2,1)}, s32[16,128]{1,0:T(8,128)}, f32[4096,128]{1,0:T(8,128)}) custom-call(s32[1]{0:T(128)} %bitcast.place_ref, s32[16,32]{1,0:T(8,128)} %refs_0_.1, s32[16,32]{1,0:T(8,128)} %refs_1_.1, bf16[16,32,1024]{2,1,0:T(8,128)(2,1)} %refs_2_.1, bf16[16,32,128]{2,1,0:T(8,128)(2,1)} %refs_3_.1, bf16[16,32,128]{2,1,0:T(8,128)(2,1)} %refs_4_.1, ...), custom_call_target="tpu_custom_call" | custom-call | flops 10000000000 | bytes 1048576 | tf_op jit(solution)/shard_map/flux/pallas_call | solution.py:383
  20.2 0.0 copy-start.2
  20.2 5.7 %all-to-all-start = ((bf16[16,49,8,128]{3,2,1,0:T(8,128)(2,1)}), bf16[16,49,8,128]{3,2,1,0:T(8,128)(2,1)S(1)}, u32[]{:S(2)}, u32[]{:S(2)}) async-start(bf16[16,49,8,128]{3,2,1,0:T(8,128)(2,1)} %bitcast.8), calls=%async_computation | async-start | bytes 3211264 | tf_op jit(solution)/shard_map/all_to_all | solution.py:415
  25.9 11.1 %collective-permute-done.4.pair_ref = bf16[16,128,128]{2,1,0:T(8,128)(2,1)S(1)} collective-permute-done((bf16[16,128,128]{2,1,0:T(8,128)(2,1)}, bf16[16,128,128]{2,1,0:T(8,128)(2,1)S(1)}, u32[]{:S(2)}, u32[]{:S(2)}) %collective-permute-start.4) | collective-permute-done | bytes 524320 | tf_op jit(solution)/shard_map/ppermute | solution.py:377
  37.0 0.8 copy-done.3
  37.8 0.0 copy-done.2
  37.8 1.0 %copy-done.4 = bf16[16,128,128]{2,1,0:T(8,128)(2,1)S(1)} copy-done((bf16[16,128,128]{2,1,0:T(8,128)(2,1)S(1)}, bf16[16,128,128]{2,1,0:T(8,128)(2,1)}, u32[]{:S(2)}) %copy-start.4) | copy-done | bytes 524312
  38.9 0.3 turn.1.w_ref
  39.2 16.4 %all-to-all-done = bf16[16,49,8,128]{3,2,1,0:T(8,128)(2,1)S(1)} async-done(((bf16[16,49,8,128]{3,2,1,0:T(8,128)(2,1)}), bf16[16,49,8,128]{3,2,1,0:T(8,128)(2,1)S(1)}, u32[]{:S(2)}, u32[]{:S(2)}) %all-to-all-start) | async-done | bytes 1605664 | tf_op jit(solution)/shard_map/all_to_all | solution.py:415
  55.6 3.9 %relax.1 = bf16[768,8,128]{2,1,0:T(8,128)(2,1)S(1)} custom-call(bf16[784,8,128]{2,1,0:T(8,128)(2,1)S(1)} %bitcast.5, bf16[32,128,128]{2,1,0:T(8,128)(2,1)S(1)} %turn.1.w_ref), custom_call_target="tpu_custom_call" | custom-call | tf_op jit(solution)/shard_map/relax/pallas_call | solution.py:428
  59.6 0.0 copy-start
  59.6 0.0 copy-start.1
  59.6 24.5 %all_to_all.10 = bf16[16,48,8,128]{3,2,1,0:T(8,128)(2,1)S(1)} all-to-all(bf16[16,48,8,128]{3,2,1,0:T(8,128)(2,1)S(1)} %bitcast.6), channel_id=1, replica_groups=mesh['lat'=4,'hi'=2,'lo'=4] {'lat','lo'}, dimensions={0} | all-to-all | bytes 3145728 | tf_op jit(solution)/shard_map/all_to_all | solution.py:415
  84.1 0.0 copy-done
  84.1 0.0 copy-done.1
  84.1 2.4 %finish.1 = f32[16,32,1024]{2,1,0:T(8,128)} custom-call(s32[16,128]{1,0:T(8,128)S(1)} %copy-done.1, bf16[768,8,128]{2,1,0:T(8,128)(2,1)S(1)} %bitcast.7, f32[4096,128]{1,0:T(8,128)S(1)} %copy-done), custom_call_target="tpu_custom_call" | custom-call | tf_op jit(solution)/shard_map/finish/pallas_call | solution.py:444
  (4 shorter events, 0.0 us)
Async XLA Ops:
  2.0 10.7 %collective-permute-start.2 = (bf16[32,1152]{1,0:T(8,128)(2,1)}, bf16[32,1152]{1,0:T(8,128)(2,1)S(1)}, u32[]{:S(2)}, u32[]{:S(2)}) collective-permute-start(bf16[32,1152]{1,0:T(8,128)(2,1)} %get-tuple-element.19), channel_id=1, source_target_pairs={{0,8},{16,24},{8,0},{24,16},{1,9},{17,25},{9,1},{25,17},{2,10},{18... | collective-permute-start | bytes 221192 | tf_op jit(solution)/shard_map/ppermute | solution.py:339
  5.0 7.7 %collective-permute-start.3 = (bf16[32,1152]{1,0:T(8,128)(2,1)}, bf16[32,1152]{1,0:T(8,128)(2,1)S(1)}, u32[]{:S(2)}, u32[]{:S(2)}) collective-permute-start(bf16[32,1152]{1,0:T(8,128)(2,1)} %get-tuple-element.20), channel_id=1, source_target_pairs={{8,16},{24,0},{16,8},{0,24},{9,17},{25,1},{17,9},{1,25},{10,18},{2... | collective-permute-start | bytes 221192 | tf_op jit(solution)/shard_map/ppermute | solution.py:339
  6.5 3.7 %collective-permute-start = (bf16[16,1152]{1,0:T(8,128)(2,1)}, bf16[16,1152]{1,0:T(8,128)(2,1)S(1)}, u32[]{:S(2)}, u32[]{:S(2)}) collective-permute-start(bf16[16,1152]{1,0:T(8,128)(2,1)} %get-tuple-element.15), channel_id=1, source_target_pairs={{0,1},{2,3},{4,5},{6,7},{1,0},{3,2},{5,4},{7,6},{8,9},{10,11},{12,... | collective-permute-start | bytes 110600 | tf_op jit(solution)/shard_map/ppermute | solution.py:339
  6.5 5.7 %collective-permute-start.1 = (bf16[16,1152]{1,0:T(8,128)(2,1)}, bf16[16,1152]{1,0:T(8,128)(2,1)S(1)}, u32[]{:S(2)}, u32[]{:S(2)}) collective-permute-start(bf16[16,1152]{1,0:T(8,128)(2,1)} %get-tuple-element.16), channel_id=1, source_target_pairs={{1,2},{3,4},{5,6},{7,0},{2,1},{4,3},{6,5},{0,7},{9,10},{11,12},{13... | collective-permute-start | bytes 110600 | tf_op jit(solution)/shard_map/ppermute | solution.py:339
  10.2 2.5 %copy-start.7 = (bf16[16,1152]{1,0:T(8,128)(2,1)}, bf16[16,1152]{1,0:T(8,128)(2,1)S(1)}, u32[]{:S(2)}) copy-start(bf16[16,1152]{1,0:T(8,128)(2,1)S(1)} %collective-permute-done.refs_5_) | copy-start | bytes 110596
  12.2 0.6 copy-start.8
  12.2 24.8 %collective-permute-start.4 = (bf16[16,128,128]{2,1,0:T(8,128)(2,1)}, bf16[16,128,128]{2,1,0:T(8,128)(2,1)S(1)}, u32[]{:S(2)}, u32[]{:S(2)}) collective-permute-start(bf16[16,128,128]{2,1,0:T(8,128)(2,1)} %own_ref.1), channel_id=1, source_target_pairs={{0,4},{4,0},{1,5},{5,1},{2,6},{6,2},{3,7},{7,3},{8,12},{12,8},{9,1... | collective-permute-start | bytes 1572872 | tf_op jit(solution)/shard_map/ppermute | solution.py:377
  12.7 0.6 copy-start.5
  13.3 0.6 copy-start.6
  20.2 17.6 %copy-start.2 = (bf16[16,128,128]{2,1,0:T(8,128)(2,1)S(1)}, bf16[16,128,128]{2,1,0:T(8,128)(2,1)}, u32[]{:S(2)}) copy-start(bf16[16,128,128]{2,1,0:T(8,128)(2,1)} %own_ref.1) | copy-start | bytes 1572868
  20.2 35.5 %all-to-all-start = ((bf16[16,49,8,128]{3,2,1,0:T(8,128)(2,1)}), bf16[16,49,8,128]{3,2,1,0:T(8,128)(2,1)S(1)}, u32[]{:S(2)}, u32[]{:S(2)}) async-start(bf16[16,49,8,128]{3,2,1,0:T(8,128)(2,1)} %bitcast.8), calls=%async_computation | async-start | bytes 3211264 | tf_op jit(solution)/shard_map/all_to_all | solution.py:415
  37.0 0.8 copy-start.3
  37.8 1.0 %copy-start.4 = (bf16[16,128,128]{2,1,0:T(8,128)(2,1)S(1)}, bf16[16,128,128]{2,1,0:T(8,128)(2,1)}, u32[]{:S(2)}) copy-start(bf16[16,128,128]{2,1,0:T(8,128)(2,1)} %copy-done.3) | copy-start | bytes 1572868
  59.6 24.6 %copy-start = (f32[4096,128]{1,0:T(8,128)S(1)}, f32[4096,128]{1,0:T(8,128)}, u32[]{:S(2)}) copy-start(f32[4096,128]{1,0:T(8,128)} %get-tuple-element.24.dyn_ref) | copy-start | bytes 6291460
  59.6 24.6 %copy-start.1 = (s32[16,128]{1,0:T(8,128)S(1)}, s32[16,128]{1,0:T(8,128)}, u32[]{:S(2)}) copy-start(s32[16,128]{1,0:T(8,128)} %get-tuple-element.21.pos_ref) | copy-start | bytes 24580

commit v4 on v3

v4 whole, which is shorter than its diff:
```python
import functools

import jax
import jax.numpy as jnp
from jax import lax
from jax.experimental import pallas as pl
from jax.experimental.pallas import tpu as pltpu
from jax.sharding import Mesh
from jax.sharding import PartitionSpec as P

RIM_VMEM = 62
BULK_COST = 5
TURN_COST = 30
SLOTS = 48
DIFFUSE = 0.1
GROUP_AXES = ("lat", "lo")
LON_AXES = ("hi", "lo")

VMEM = pl.BlockSpec(memory_space=pltpu.VMEM)
ANY = pl.BlockSpec(memory_space=pltpu.HBM)
SMEM = pl.BlockSpec(memory_space=pltpu.SMEM)


def log2(n):
    return n.bit_length() - 1


def parities(place, lons):
    return place & 1, (place >> log2(lons)) & 1


def edge_kernel(
    lons, place_ref, q_hbm, u_hbm, v_hbm, lon_a, lon_b, lat_a, lat_b, q_side, u_side, wide, sems
):
    rows, cells, width = q_hbm.shape
    side = q_side.shape[2]
    odd_lon, odd_lat = parities(place_ref[0], lons)
    copies = []

    def copy(source, target):
        copies.append(pltpu.make_async_copy(source, target, sems.at[len(copies)]))
        copies[-1].start()

    for n, odd in enumerate((odd_lon, 1 - odd_lon)):
        near = pl.ds(pl.multiple_of(jnp.where(odd == 1, 0, cells - side), side), side)
        copy(q_hbm.at[:, near, :], q_side.at[n])
        copy(u_hbm.at[:, near, :], u_side.at[n])
    for ref, odd in ((lat_a, odd_lat), (lat_b, 1 - odd_lat)):
        i = jnp.where(odd == 1, 0, rows - 1)
        copy(q_hbm.at[i], ref.at[:, 0:width])
        copy(v_hbm.at[i], ref.at[:, width:])
    for c in copies[:4]:
        c.wait()
    for n, (ref, odd) in enumerate(((lon_a, odd_lon), (lon_b, 1 - odd_lon))):
        first = odd == 1
        for i in range(rows):
            q, u = q_side[n, i].astype(jnp.float32), u_side[n, i].astype(jnp.float32)
            wide[i : i + 1, 0:width] = jnp.where(first, q[0:1], q[side - 1 :])
            wide[i : i + 1, width:] = jnp.where(first, u[0:1], u[side - 1 :])
        ref[...] = wide[...].astype(jnp.bfloat16)
    for c in copies[4:]:
        c.wait()


def plan(place_ref, span_ref, slot_ref, send_ref, pos_ref, member, pos, cap, owned, lons, lows):
    rows, cells = span_ref.shape
    stored = cap + 1
    peers = send_ref.shape[0] // stored
    f32, bf16 = jnp.float32, jnp.bfloat16
    span, slot = span_ref[...], slot_ref[...]
    owner = span >> log2(owned)
    owner_lon = owner & (lons - 1)
    far = (owner_lon >> log2(lows)) != ((place_ref[0] >> log2(lows)) & 1)
    low = (owner_lon & (lows - 1)) ^ jnp.where(far, lows // 2, 0)
    peer = ((owner >> log2(lons)) << log2(lows)) + low
    local = (span & (owned - 1)) + jnp.where(far, owned, 0)
    iota = lambda shape, axis: lax.broadcasted_iota(jnp.int32, shape, axis)
    for i in range(rows):
        member[i * peers : (i + 1) * peers, :] = jnp.where(
            iota((peers, cells), 0) == peer[i : i + 1], 1.0, 0.0
        )
    hot = member[...].astype(bf16)
    dot = functools.partial(jnp.dot, preferred_element_type=f32)
    within = dot(hot, (iota((cells, cells), 0) < iota((cells, cells), 1)).astype(f32).astype(bf16))
    pairs = (rows * peers, rows * peers)
    to, of = iota(pairs, 0), iota(pairs, 1)
    same = (to & (peers - 1)) == (of & (peers - 1))
    lower = jnp.where(same & (of < (to & -peers)), 1.0, 0.0).astype(bf16)
    before = within + jnp.sum(dot(lower, hot), axis=1, keepdims=True)
    before = before * member[...]
    lists = jnp.zeros((3 * peers, 128), f32)
    for i in range(rows):
        block = slice(i * peers, (i + 1) * peers)
        rank = jnp.sum(before[block], axis=0, keepdims=True).astype(jnp.int32)
        pos[i : i + 1, 0:cells] = peer[i : i + 1] * stored + rank
        pos_ref[i : i + 1, 0:cells] = peer[i : i + 1] * cap + rank
        chosen = jnp.where(iota((128, cells), 0) == rank, 1.0, 0.0).astype(bf16)
        mine = member[block]
        values = jnp.concatenate(
            [mine * local[i : i + 1].astype(f32), mine * slot[i : i + 1].astype(f32), mine], axis=0
        )
        lists = lists + lax.dot_general(
            values.astype(bf16), chosen, (((1,), (1,)), ((), ())), preferred_element_type=f32
        )
    spans = jnp.where(lists[2 * peers :] > 0.5, lists[:peers], 2.0 * owned)
    slots = lists[peers : 2 * peers]
    tile = send_ref.shape[1:]
    for p in range(peers):
        send_ref[p * stored + cap] = jnp.where(
            iota(tile, 0) == 0,
            jnp.broadcast_to(spans[p : p + 1], tile),
            jnp.broadcast_to(slots[p : p + 1], tile),
        ).astype(bf16)


def bulk_kernel(cap, owned, lons, lows, place_ref, *refs):
    sources, outputs, held, rest = refs[:5], refs[5:11], refs[11:16], refs[16:]
    send_hbm, back_ref, pos_ref, dyn_hbm, rim_q, rim_dyn = outputs
    span_ref, slot_ref, q_ref, u_ref, v_ref = held
    sems, row_sems, member, pos_s, send_ref, dyn_ref, cell, wind_x, face_x, wind_y, face_y, flux_y = rest
    rows, cells, width = q_ref.shape
    levels = u_ref.shape[2]
    tracers = width // levels
    columns = rows * cells
    f32 = jnp.float32
    line = cells * tracers
    copies = [pltpu.make_async_copy(a, b, sems.at[n]) for n, (a, b) in enumerate(zip(sources, held))]
    for copy in copies:
        copy.start()
    copies[2].wait()

    def relayout(i, carry):
        for t in range(tracers):
            cell[pl.ds(i * line + t, cells, stride=tracers), :] = q_ref[
                i, :, t * levels : (t + 1) * levels
            ].astype(f32)
        return carry

    lax.fori_loop(0, rows, relayout, 0)
    for copy in copies[:2]:
        copy.wait()
    plan(place_ref, span_ref, slot_ref, send_ref, back_ref, member, pos_ref, cap, owned, lons, lows)
    pos_copy = pltpu.make_async_copy(pos_ref, pos_s, sems.at[5])
    pos_copy.start()
    for copy in copies[3:]:
        copy.wait()

    wind_x[0:columns, :] = u_ref[...].reshape(columns, levels).astype(f32)
    wind_y[...] = v_ref[...].reshape(columns, levels).astype(f32)
    face_x[...] = 0.25 * (wind_x[0:columns, :] + wind_x[1 : columns + 1, :])
    face_y[0 : columns - cells, :] = 0.25 * (wind_y[: columns - cells, :] + wind_y[cells:, :])
    face_y[columns - cells :, :] = jnp.zeros((cells, levels), f32)
    flux_y[...] = jnp.zeros_like(flux_y)

    def tile(i, j):
        return pl.ds(pl.multiple_of((i * cells + j) * tracers, tracers), tracers)

    def spread_row(ref, r):
        return jnp.broadcast_to(ref[pl.ds(r, 1), :], (tracers, levels))

    pos_copy.wait()

    def dyn_copy(i):
        rows_i = pl.ds(pl.multiple_of(i * line, tracers), line)
        return pltpu.make_async_copy(dyn_ref.at[rows_i], dyn_hbm.at[rows_i], row_sems.at[i])

    def row(i, carry):
        diffuse_y = jnp.where(i == rows - 1, 0.0, DIFFUSE)
        north = jnp.minimum(i + 1, rows - 1)
        here = cell[tile(i, 0), :]
        flux_w = jnp.zeros((tracers, levels), f32)
        for j in range(cells):
            column = i * cells + j
            if j < cells - 1:
                after = cell[tile(i, j + 1), :]
                flux_e = spread_row(face_x, column) * (here + after) - DIFFUSE * (after - here)
            else:
                flux_e = jnp.zeros((tracers, levels), f32)
            above = cell[tile(north, j), :]
            flux_n = spread_row(face_y, column) * (here + above) - diffuse_y * (above - here)
            flux_s = flux_y[j * tracers : (j + 1) * tracers, :]
            flux_y[j * tracers : (j + 1) * tracers, :] = flux_n
            dyn = (flux_w - flux_e) + (flux_s - flux_n)
            dyn_ref[tile(i, j), :] = dyn
            send_ref[pos_s[i, j]] = (here + dyn).astype(jnp.bfloat16)
            if j in (0, cells - 1):
                at = pl.multiple_of((2 * cells + (j > 0) * rows + i) * tracers, tracers)
                rim_q[pl.ds(at, tracers), :] = here
                rim_dyn[pl.ds(at, tracers), :] = dyn
            here, flux_w = after, flux_e
        dyn_copy(i).start()
        return carry

    lax.fori_loop(0, rows, row, 0)
    send_copy = pltpu.make_async_copy(send_ref, send_hbm, sems.at[6])
    send_copy.start()
    for n, i in enumerate((0, rows - 1)):
        rim_q[n * line : (n + 1) * line, :] = cell[i * line : (i + 1) * line, :]
        rim_dyn[n * line : (n + 1) * line, :] = dyn_ref[i * line : (i + 1) * line, :]
    send_copy.wait()

    def drain(i, carry):
        dyn_copy(i).wait()
        return carry

    lax.fori_loop(0, rows, drain, 0)


def rim_kernel(lats, lons, place_ref, *refs):
    sources, (send_in, send_hbm, rim_ref), rest = refs[:11], refs[11:14], refs[14:]
    own_lon, own_lat, far_lon, far_lat, pos_s, rim_q, rim_dyn, side, stage, sems = rest
    rows, cells = own_lon.shape[1], own_lat.shape[1]
    levels = side.shape[1]
    tracers = rim_q.shape[0] // (2 * (rows + cells))
    width = tracers * levels
    f32 = jnp.float32
    odd_lon, odd_lat = parities(place_ref[0], lons)
    targets = (
        own_lon.at[1 - odd_lon],
        own_lon.at[odd_lon],
        own_lat.at[1 - odd_lat],
        own_lat.at[odd_lat],
        far_lon.at[1 - odd_lon],
        far_lon.at[odd_lon],
        far_lat.at[1 - odd_lat],
        far_lat.at[odd_lat],
        pos_s,
        rim_q,
        rim_dyn,
    )
    copies = [pltpu.make_async_copy(a, b, sems.at[n]) for n, (a, b) in enumerate(zip(sources, targets))]
    for copy in copies:
        copy.start()
    for copy in copies[:8]:
        copy.wait()
    lat = place_ref[0] >> log2(lons)
    lat_open = (jnp.where(lat > 0, 1.0, 0.0), jnp.where(lat < lats - 1, 1.0, 0.0))
    first = 0
    for own, far, opens in ((own_lat, far_lat, lat_open), (own_lon, far_lon, (None, None))):
        for n, opened in enumerate(opens):
            sign, diffuse = (0.25, -0.25)[n], DIFFUSE
            if opened is not None:
                sign, diffuse = sign * opened, diffuse * opened
            count = own.shape[1]
            face = sign * (own[n, :, width:].astype(f32) + far[n, :, width:].astype(f32))
            for t in range(tracers):
                lanes = slice(t * levels, (t + 1) * levels)
                here, there = own[n, :, lanes].astype(f32), far[n, :, lanes].astype(f32)
                side[pl.ds(first * tracers + t, count, stride=tracers), :] = face * (
                    here + there
                ) + diffuse * (there - here)
            first += count
    for copy in copies[8:]:
        copy.wait()
    tile = lambda n: slice(n * tracers, (n + 1) * tracers)
    west, east = 2 * cells, 2 * cells + rows
    rim = []
    for n, i in enumerate((0, rows - 1)):
        for j in range(cells):
            extra = {0: (west + i,), cells - 1: (east + i,)}.get(j, ())
            rim.append((n * cells + j, i, j, extra))
    for i in range(1, rows - 1):
        rim += [(west + i, i, 0, ()), (east + i, i, cells - 1, ())]
    sent = sems.at[len(copies)]
    for m, (n, i, j, extra) in enumerate(rim):
        dyn = rim_dyn[tile(n), :] + side[tile(n), :]
        for e in extra:
            dyn = dyn + side[tile(e), :]
        rim_ref[tile(n), :] = dyn
        stage[m] = (rim_q[tile(n), :] + dyn).astype(jnp.bfloat16)
        pltpu.make_async_copy(stage.at[m], send_hbm.at[pos_s[i, j]], sent).start()
    pltpu.make_async_copy(stage, send_hbm.at[pl.ds(0, len(rim))], sent).wait()


def turn_kernel(lows, place_ref, own_ref, outer_ref, inner_ref, out_ref):
    owned = own_ref.shape[0]
    place = place_ref[0]
    is_outer = ((place >> log2(lows)) & 1) == ((place >> (log2(lows) - 1)) & 1)
    for k in range(owned):
        out_ref[k] = own_ref[k].T

    @pl.when(is_outer)
    def _():
        for k in range(owned):
            out_ref[owned + k] = outer_ref[k].T

    @pl.when(jnp.logical_not(is_outer))
    def _():
        for k in range(owned):
            out_ref[owned + k] = inner_ref[k].T


def relax_kernel(x_ref, w_ref, y_ref, pos, pos_s, sem, slots):
    tracers, levels = x_ref.shape[1:]
    peers, lanes = pos.shape
    stored = x_ref.shape[0] // peers
    cap = stored - 1
    f32 = jnp.float32
    for p in range(peers):
        listed = x_ref[p * stored + cap].astype(f32)
        pos[p : p + 1, :] = (listed[0:1] * SLOTS + listed[1:2]).astype(jnp.int32)
    copy = pltpu.make_async_copy(pos, pos_s, sem)
    copy.start()
    copy.wait()

    def place(at):
        return pl.ds(pl.multiple_of(at * tracers, tracers), tracers)

    def scatter(p, carry):
        for r in range(cap):
            slots[place(pos_s[p, r]), :] = x_ref[p * stored + r].astype(f32)
        return carry

    lax.fori_loop(0, peers, scatter, 0)
    block = SLOTS * tracers

    def span(k, carry):
        at = pl.ds(pl.multiple_of(k * block, block), block)
        x = slots[at, :]
        y = jnp.dot(x.astype(jnp.bfloat16), w_ref[k], preferred_element_type=f32)
        slots[at, :] = y - x
        return carry

    lax.fori_loop(0, w_ref.shape[0], span, 0, unroll=8)

    def gather(p, carry):
        for r in range(cap):
            y_ref[p * cap + r] = slots[place(pos_s[p, r]), :].astype(jnp.bfloat16)
        return carry

    lax.fori_loop(0, peers, gather, 0)


def finish_kernel(pos_ref, y_ref, dyn_ref, rim_ref, out_hbm, total, out, sems):
    rows, cells, width = out.shape
    tracers, levels = y_ref.shape[1:]

    def copy(i):
        return pltpu.make_async_copy(out.at[i], out_hbm.at[i], sems.at[i])

    def tile(n):
        return pl.ds(pl.multiple_of(n * tracers, tracers), tracers)

    def row(i, dyn):
        for j in range(cells):
            total[j * tracers : (j + 1) * tracers, :] = dyn(j) + y_ref[pos_ref[i, j]].astype(
                jnp.float32
            )
        for t in range(tracers):
            out[i, :, t * levels : (t + 1) * levels] = total[pl.ds(t, cells, stride=tracers), :]
        copy(i).start()

    def inner(i, carry):
        def dyn(j):
            if j in (0, cells - 1):
                return rim_ref[tile(2 * cells + (j > 0) * rows + i), :]
            return dyn_ref[tile(i * cells + j), :]

        row(i, dyn)
        return carry

    row(0, lambda j: rim_ref[tile(j), :])
    lax.fori_loop(1, rows - 1, inner, 0)
    row(rows - 1, lambda j: rim_ref[tile(cells + j), :])
    for i in range(rows):
        copy(i).wait()


def in_pairs(x, axis, first):
    count = lax.axis_size(axis)
    pairs = [(i % count, (i + 1) % count) for i in range(first, count + first, 2)]
    return lax.ppermute(x, axis, pairs + [(b, a) for a, b in pairs])


def shards(tracers, east_wind, north_wind, span_of, slot_of, inverses):
    levels = east_wind.shape[2]
    rows, cells, width = tracers.shape
    kinds = width // levels
    columns = rows * cells
    lats, lows = lax.axis_size("lat"), lax.axis_size("lo")
    lons = lax.axis_size("hi") * lows
    peers = lats * lows
    owned = inverses.shape[0]
    cap = 2 * (3 * columns // (2 * lats * lons))
    stored = cap + 1
    f32, bf16, i32 = jnp.float32, jnp.bfloat16, jnp.int32
    dma = pltpu.SemaphoreType.DMA
    params = lambda mib: pltpu.CompilerParams(vmem_limit_bytes=mib << 20)

    side = 8
    place = lax.axis_index(("lat", "hi", "lo")).astype(i32).reshape(1)
    lon_a, lon_b, lat_a, lat_b = pl.pallas_call(
        functools.partial(edge_kernel, lons),
        out_shape=(jax.ShapeDtypeStruct((rows, width + levels), bf16),) * 2
        + (jax.ShapeDtypeStruct((cells, width + levels), bf16),) * 2,
        in_specs=[SMEM] + [ANY] * 3,
        out_specs=(VMEM,) * 4,
        scratch_shapes=[
            pltpu.VMEM((2, rows, side, width), bf16),
            pltpu.VMEM((2, rows, side, levels), bf16),
            pltpu.VMEM((rows, width + levels), f32),
            dma((8,)),
        ],
        compiler_params=params(62),
        name="edges",
    )(place, tracers, east_wind, north_wind)
    edges = (lon_a, lon_b, lat_a, lat_b)
    far_edges = (
        in_pairs(lon_a, LON_AXES, 0),
        in_pairs(lon_b, LON_AXES, 1),
        in_pairs(lat_a, "lat", 0),
        in_pairs(lat_b, "lat", 1),
    )

    def opposite(start, stop):
        pairs = [(lo, lows + (lo ^ lows // 2)) for lo in range(start, stop)]
        return pairs + [(b, a) for a, b in pairs]

    outer = lax.ppermute(inverses, LON_AXES, opposite(0, lows // 2))
    cost = lambda us: pl.CostEstimate(
        flops=us * 1_000_000_000, bytes_accessed=1 << 20, transcendentals=0
    )
    fields = (span_of, slot_of, tracers, east_wind, north_wind)
    rim_shape = (2 * (rows + cells) * kinds, levels)
    block_shape = (columns * kinds, levels)
    send_shape = (peers * stored, kinds, levels)
    send, back, pos, dyn, rim_q, rim_dyn = pl.pallas_call(
        functools.partial(bulk_kernel, cap, owned, lons, lows),
        out_shape=(
            jax.ShapeDtypeStruct(send_shape, bf16),
            jax.ShapeDtypeStruct((rows, 128), i32),
            jax.ShapeDtypeStruct((rows, 128), i32),
            jax.ShapeDtypeStruct(block_shape, f32),
            jax.ShapeDtypeStruct(rim_shape, f32),
            jax.ShapeDtypeStruct(rim_shape, f32),
        ),
        in_specs=[SMEM] + [ANY] * 5,
        out_specs=(ANY, VMEM, VMEM, ANY, VMEM, VMEM),
        scratch_shapes=[pltpu.VMEM(x.shape, x.dtype) for x in fields]
        + [
            dma((7,)),
            dma((rows,)),
            pltpu.VMEM((rows * peers, cells), f32),
            pltpu.SMEM((rows, 128), i32),
            pltpu.VMEM(send_shape, bf16),
            pltpu.VMEM(block_shape, f32),
            pltpu.VMEM(block_shape, f32),
            pltpu.VMEM((columns + 8, levels), f32),
            pltpu.VMEM((columns, levels), f32),
            pltpu.VMEM((columns, levels), f32),
            pltpu.VMEM((columns, levels), f32),
            pltpu.VMEM((cells * kinds, levels), f32),
        ],
        compiler_params=params(62),
        cost_estimate=cost(BULK_COST),
        name="bulk",
    )(place, *fields)

    matrices, pos, *far_edges = lax.optimization_barrier((inverses, pos, *far_edges))
    inner = lax.ppermute(matrices, LON_AXES, opposite(lows // 2, lows))

    rim_args = (*edges, *far_edges, pos, rim_q, rim_dyn)
    both = lambda x: pltpu.VMEM((2,) + x.shape, x.dtype)
    send, rim = pl.pallas_call(
        functools.partial(rim_kernel, lats, lons),
        out_shape=(jax.ShapeDtypeStruct(send_shape, bf16), jax.ShapeDtypeStruct(rim_shape, f32)),
        in_specs=[SMEM] + [ANY] * 12,
        out_specs=(ANY, VMEM),
        scratch_shapes=[
            both(lon_a),
            both(lat_a),
            both(lon_a),
            both(lat_a),
            pltpu.SMEM((rows, 128), i32),
            pltpu.VMEM(rim_shape, f32),
            pltpu.VMEM(rim_shape, f32),
            pltpu.VMEM(rim_shape, f32),
            pltpu.VMEM((2 * (rows + cells) - 4, kinds, levels), bf16),
            dma((12,)),
        ],
        input_output_aliases={12: 0},
        compiler_params=params(RIM_VMEM),
        name="rim",
    )(place, *rim_args, send)

    def exchange(x):
        x = x.reshape(peers, -1, kinds, levels)
        x = lax.all_to_all(x, GROUP_AXES, split_axis=0, concat_axis=0, tiled=True)
        return x.reshape(-1, kinds, levels)

    arrived = exchange(send)
    turned = pl.pallas_call(
        functools.partial(turn_kernel, lows),
        out_shape=jax.ShapeDtypeStruct((2 * owned, levels, levels), bf16),
        in_specs=[SMEM] + [VMEM] * 3,
        out_specs=VMEM,
        compiler_params=params(16),
        cost_estimate=cost(TURN_COST),
        name="turn",
    )(place, inverses, outer, inner)
    physics = pl.pallas_call(
        relax_kernel,
        out_shape=jax.ShapeDtypeStruct((peers * cap, kinds, levels), bf16),
        in_specs=[VMEM] * 2,
        out_specs=VMEM,
        scratch_shapes=[
            pltpu.VMEM((peers, 128), i32),
            pltpu.SMEM((peers, 128), i32),
            dma,
            pltpu.VMEM(((2 * owned * SLOTS + 1) * kinds, levels), f32),
        ],
        compiler_params=params(24),
        name="relax",
    )(arrived, turned)

    returned = exchange(physics)
    return pl.pallas_call(
        finish_kernel,
        out_shape=jax.ShapeDtypeStruct((rows, cells, width), f32),
        in_specs=[SMEM, VMEM, VMEM, VMEM],
        out_specs=ANY,
        scratch_shapes=[
            pltpu.VMEM((cells * kinds, levels), f32),
            pltpu.VMEM((rows, cells, width), f32),
            dma((rows,)),
        ],
        compiler_params=params(16),
        name="finish",
    )(back, returned, dyn, rim)


def solution(mesh):
    lats, lons = mesh.devices.shape
    split = Mesh(mesh.devices.reshape(lats, 2, lons // 2), ("lat", "hi", "lo"))
    block = P("lat", LON_AXES, None)
    in_specs = (
        block,
        block,
        block,
        P("lat", LON_AXES),
        P("lat", LON_AXES),
        P(("lat", "hi", "lo"), None, None),
    )
    return jax.shard_map(shards, mesh=split, in_specs=in_specs, out_specs=block, check_vma=False)
```

time: 86.9 us -> 81.2 us (0.934)
  waiting for transfers between devices: 29.5 us -> 18.3 us
  Pallas kernels: 14.8 us -> 18.5 us
    ppermute x1 -> x2, waiting for transfers between devices: 11.1 us -> 0.01 us  [the longest x1 0.01 us: shards(): inner = lax.ppermute(matrices, LON_AXES, opposite(lows // 2, lows))]
    pallas_call x2 -> x3, Pallas kernels: 6.55 us -> 10.2 us  [the longest x1 6.66 us: shards(): pl.pallas_call(functools.partial(bulk_kernel, cap, owned, lons, lows), ou...]
    ppermute x1 -> x2, starting transfers between devices: 0.51 us -> 3.04 us  [the longest x1 2.35 us: shards(): outer = lax.ppermute(inverses, LON_AXES, opposite(0, lows // 2))]
    ppermute x4, waiting for transfers between devices: 1.96 us -> 0.01 us  [in_pairs(): return lax.ppermute(x, axis, pairs + [(b, a) for a, b in pairs])]
    all_to_all x1, starting transfers between devices: 5.66 us -> 3.72 us  [exchange(): x = lax.all_to_all(x, GROUP_AXES, split_axis=0, concat_axis=0, tiled=True)]
    all_to_all x1, waiting for transfers between devices: 16.4 us -> 18.2 us  [exchange(): x = lax.all_to_all(x, GROUP_AXES, split_axis=0, concat_axis=0, tiled=True)]
    unnamed x18 -> x24, local copies, waits for them, and re-layouts: 3.13 us -> 3.71 us
  transfers between devices with their start and end apart: 6 -> 7, of which waited for: 3 -> 1; matrix products, arithmetic and copies ran while one was open for 0% -> 0% of each run, Pallas kernels for 8% -> 13%
where the time goes in v4:
time: 81.2 us; the launch traced here: 80.8 us
  blocking collectives  25.2 us (31%)
  Pallas kernels  18.5 us (23%)
  waiting for transfers between devices  18.3 us (23%)
  starting transfers between devices  15 us (18%)
  local copies, waits for them, and re-layouts  3.71 us (5%)
    all_to_all x1, blocking collectives, exchange(): x = lax.all_to_all(x, GROUP_AXES, split_axis=0, concat_axis=0, tiled=True)  25.2 us
    all_to_all x1, waiting for transfers between devices, exchange(): x = lax.all_to_all(x, GROUP_AXES, split_axis=0, concat_axis=0, tiled=True)  18.2 us
    ppermute x4, starting transfers between devices, in_pairs(): return lax.ppermute(x, axis, pairs + [(b, a) for a, b in pairs])  8.21 us
    pallas_call x1, Pallas kernels, shards(): pl.pallas_call(functools.partial(bulk_kernel, cap, owned, lons, lows), ou...  6.66 us
    pallas_call x1, Pallas kernels, shards(): pl.pallas_call(relax_kernel, out_shape=jax.ShapeDtypeStruct((peers * cap,...  3.91 us
    all_to_all x1, starting transfers between devices, exchange(): x = lax.all_to_all(x, GROUP_AXES, split_axis=0, concat_axis=0, tiled=True)  3.72 us
    unnamed x24, local copies, waits for them, and re-layouts  3.71 us
    pallas_call x1, Pallas kernels, shards(): pl.pallas_call(functools.partial(rim_kernel, lats, lons), out_shape=(jax....  3.16 us
  transfers between devices with their start and end apart: 7, of which 1 were waited for; matrix products, arithmetic and copies ran while one was open for 0% of the time, Pallas kernels for 13%

profile of v4, /device:TPU:0, one launch (start us, length us, event | category | flops | bytes accessed | tf_op | source)
XLA Modules:
  0.0 80.8 jit_solution(13015842609836859778)
XLA Ops:
  0.0 2.0 %edges.1 = (bf16[16,1152]{1,0:T(8,128)(2,1)}, bf16[16,1152]{1,0:T(8,128)(2,1)}, bf16[32,1152]{1,0:T(8,128)(2,1)}, bf16[32,1152]{1,0:T(8,128)(2,1)}) custom-call(s32[1]{0:T(128)} %bitcast.place_ref, bf16[16,32,1024]{2,1,0:T(8,128)(2,1)} %q_hbm.1, bf16[16,32,128]{2,1,0:T(8,128)(2,1)} %u_hbm.1, bf16[16,32,128]{2,1,0:T(8,128)(2,1)} %v_hbm.1), custom_call_target="tpu_custom_call" | custom-call | tf_op jit(solution)/shard_map/edges/pallas_call | solution.py:392
  2.0 0.5 collective-permute-start
  2.5 4.7 %collective-permute-start.1 = (bf16[16,1152]{1,0:T(8,128)(2,1)}, bf16[16,1152]{1,0:T(8,128)(2,1)S(1)}, u32[]{:S(2)}, u32[]{:S(2)}) collective-permute-start(bf16[16,1152]{1,0:T(8,128)(2,1)} %get-tuple-element.25.refs_1_), channel_id=1, source_target_pairs={{1,2},{3,4},{5,6},{7,0},{2,1},{4,3},{6,5},{0,7},{9,10},{11,12},{13... | collective-permute-start | bytes 110600 | tf_op jit(solution)/shard_map/ppermute | solution.py:372
  7.2 1.5 %collective-permute-start.2 = (bf16[32,1152]{1,0:T(8,128)(2,1)}, bf16[32,1152]{1,0:T(8,128)(2,1)S(1)}, u32[]{:S(2)}, u32[]{:S(2)}) collective-permute-start(bf16[32,1152]{1,0:T(8,128)(2,1)} %get-tuple-element.26.refs_2_), channel_id=1, source_target_pairs={{0,8},{16,24},{8,0},{24,16},{1,9},{17,25},{9,1},{25,17},{2,10},{18... | collective-permute-start | bytes 221192 | tf_op jit(solution)/shard_map/ppermute | solution.py:372
  8.7 1.5 %collective-permute-start.3 = (bf16[32,1152]{1,0:T(8,128)(2,1)}, bf16[32,1152]{1,0:T(8,128)(2,1)S(1)}, u32[]{:S(2)}, u32[]{:S(2)}) collective-permute-start(bf16[32,1152]{1,0:T(8,128)(2,1)} %get-tuple-element.27.refs_3_), channel_id=1, source_target_pairs={{8,16},{24,0},{16,8},{0,24},{9,17},{25,1},{17,9},{1,25},{10,18},{2... | collective-permute-start | bytes 221192 | tf_op jit(solution)/shard_map/ppermute | solution.py:372
  10.2 2.3 %collective-permute-start.4 = (bf16[16,128,128]{2,1,0:T(8,128)(2,1)}, bf16[16,128,128]{2,1,0:T(8,128)(2,1)S(1)}, u32[]{:S(2)}, u32[]{:S(2)}) collective-permute-start(bf16[16,128,128]{2,1,0:T(8,128)(2,1)} %own_ref.1), channel_id=1, source_target_pairs={{0,6},{1,7},{6,0},{7,1},{8,14},{9,15},{14,8},{15,9},{16,22},{17,23... | collective-permute-start | bytes 1572872 | tf_op jit(solution)/shard_map/ppermute | solution.py:419
  12.6 6.7 %bulk.1 = (bf16[784,8,128]{2,1,0:T(8,128)(2,1)}, s32[16,128]{1,0:T(8,128)}, s32[16,128]{1,0:T(8,128)}, f32[4096,128]{1,0:T(8,128)}, f32[768,128]{1,0:T(8,128)}, /*index=5*/f32[768,128]{1,0:T(8,128)}) custom-call(s32[1]{0:T(128)} %bitcast.place_ref, s32[16,32]{1,0:T(8,128)} %refs_0_.1, s32[16,32]{1,0:T(8,128)} %refs_1_.1, bf16[16,32,1024]{2,1,0:T(8,128)(2,1)} %q_hbm.1, ...), custom_call_target="tpu_custom_call" | custom-call | flops 5000000000 | bytes 1048576 | tf_op jit(solution)/shard_map/bulk/pallas_call | solution.py:427
  19.3 0.0 collective-permute-done.refs_4_
  19.3 0.0 copy-start.10
  19.3 0.0 collective-permute-done.1.refs_5_
  19.3 0.0 copy-start.11
  19.3 0.0 collective-permute-done.2.refs_6_
  19.3 0.0 collective-permute-done.3.refs_7_
  19.3 0.7 collective-permute-start.5
  20.0 0.0 copy-done.10
  20.1 0.0 copy-done.11
  20.1 0.0 copy-done.8
  20.1 0.0 copy-done.9
  20.1 3.2 %rim.1 = (bf16[784,8,128]{2,1,0:T(8,128)(2,1)}, f32[768,128]{1,0:T(8,128)}) custom-call(s32[1]{0:T(128)} %bitcast.place_ref, bf16[16,1152]{1,0:T(8,128)(2,1)} %get-tuple-element.24.refs_0_, bf16[16,1152]{1,0:T(8,128)(2,1)} %get-tuple-element.25.refs_1_, bf16[32,1152]{1,0:T(8,128)(2,1)} %get-tuple-element.26.refs_2_, ...), custom_call_target="tpu_custom_call", output_to_operand_aliasing={{0}: (12, {})} | custom-call | tf_op jit(solution)/shard_map/rim/pallas_call | solution.py:464
  23.3 3.7 %all-to-all-start = ((bf16[16,49,8,128]{3,2,1,0:T(8,128)(2,1)}), bf16[16,49,8,128]{3,2,1,0:T(8,128)(2,1)S(1)}, u32[]{:S(2)}, u32[]{:S(2)}) async-start(bf16[16,49,8,128]{3,2,1,0:T(8,128)(2,1)} %bitcast.8), calls=%async_computation | async-start | bytes 3211264 | tf_op jit(solution)/shard_map/all_to_all | solution.py:488
  27.0 0.0 collective-permute-done.4.outer_ref
  27.0 0.8 copy-done.4
  27.8 0.0 collective-permute-done.5.inner_ref
  27.8 0.8 copy-done.6
  28.6 1.0 %copy-done.5 = bf16[16,128,128]{2,1,0:T(8,128)(2,1)S(1)} copy-done((bf16[16,128,128]{2,1,0:T(8,128)(2,1)S(1)}, bf16[16,128,128]{2,1,0:T(8,128)(2,1)}, u32[]{:S(2)}) %copy-start.5) | copy-done | bytes 524312
  29.6 1.0 %copy-done.7 = bf16[16,128,128]{2,1,0:T(8,128)(2,1)S(1)} copy-done((bf16[16,128,128]{2,1,0:T(8,128)(2,1)S(1)}, bf16[16,128,128]{2,1,0:T(8,128)(2,1)}, u32[]{:S(2)}) %copy-start.7) | copy-done | bytes 524312
  30.7 0.4 turn.1.w_ref
  31.1 18.2 %all-to-all-done = bf16[16,49,8,128]{3,2,1,0:T(8,128)(2,1)S(1)} async-done(((bf16[16,49,8,128]{3,2,1,0:T(8,128)(2,1)}), bf16[16,49,8,128]{3,2,1,0:T(8,128)(2,1)S(1)}, u32[]{:S(2)}, u32[]{:S(2)}) %all-to-all-start) | async-done | bytes 1605664 | tf_op jit(solution)/shard_map/all_to_all | solution.py:488
  49.3 3.9 %relax.1 = bf16[768,8,128]{2,1,0:T(8,128)(2,1)S(1)} custom-call(bf16[784,8,128]{2,1,0:T(8,128)(2,1)S(1)} %bitcast.5, bf16[32,128,128]{2,1,0:T(8,128)(2,1)S(1)} %turn.1.w_ref), custom_call_target="tpu_custom_call" | custom-call | tf_op jit(solution)/shard_map/relax/pallas_call | solution.py:501
  53.2 0.0 copy-start
  53.2 25.2 %all_to_all.10 = bf16[16,48,8,128]{3,2,1,0:T(8,128)(2,1)S(1)} all-to-all(bf16[16,48,8,128]{3,2,1,0:T(8,128)(2,1)S(1)} %bitcast.6), channel_id=1, replica_groups=mesh['lat'=4,'hi'=2,'lo'=4] {'lat','lo'}, dimensions={0} | all-to-all | bytes 3145728 | tf_op jit(solution)/shard_map/all_to_all | solution.py:488
  78.4 2.4 %finish.1 = f32[16,32,1024]{2,1,0:T(8,128)} custom-call(s32[16,128]{1,0:T(8,128)S(1)} %copy-done.2, bf16[768,8,128]{2,1,0:T(8,128)(2,1)S(1)} %bitcast.7, f32[4096,128]{1,0:T(8,128)S(1)} %copy-done, f32[768,128]{1,0:T(8,128)S(1)} %copy-done.1), custom_call_target="tpu_custom_call" | custom-call | tf_op jit(solution)/shard_map/finish/pallas_call | solution.py:517
  (13 shorter events, 0.0 us)
Async XLA Ops:
  2.0 17.2 %collective-permute-start = (bf16[16,1152]{1,0:T(8,128)(2,1)}, bf16[16,1152]{1,0:T(8,128)(2,1)S(1)}, u32[]{:S(2)}, u32[]{:S(2)}) collective-permute-start(bf16[16,1152]{1,0:T(8,128)(2,1)} %get-tuple-element.24.refs_0_), channel_id=1, source_target_pairs={{0,1},{2,3},{4,5},{6,7},{1,0},{3,2},{5,4},{7,6},{8,9},{10,11},{12,... | collective-permute-start | bytes 110600 | tf_op jit(solution)/shard_map/ppermute | solution.py:372
  2.5 16.7 %collective-permute-start.1 = (bf16[16,1152]{1,0:T(8,128)(2,1)}, bf16[16,1152]{1,0:T(8,128)(2,1)S(1)}, u32[]{:S(2)}, u32[]{:S(2)}) collective-permute-start(bf16[16,1152]{1,0:T(8,128)(2,1)} %get-tuple-element.25.refs_1_), channel_id=1, source_target_pairs={{1,2},{3,4},{5,6},{7,0},{2,1},{4,3},{6,5},{0,7},{9,10},{11,12},{13... | collective-permute-start | bytes 110600 | tf_op jit(solution)/shard_map/ppermute | solution.py:372
  7.2 12.1 %collective-permute-start.2 = (bf16[32,1152]{1,0:T(8,128)(2,1)}, bf16[32,1152]{1,0:T(8,128)(2,1)S(1)}, u32[]{:S(2)}, u32[]{:S(2)}) collective-permute-start(bf16[32,1152]{1,0:T(8,128)(2,1)} %get-tuple-element.26.refs_2_), channel_id=1, source_target_pairs={{0,8},{16,24},{8,0},{24,16},{1,9},{17,25},{9,1},{25,17},{2,10},{18... | collective-permute-start | bytes 221192 | tf_op jit(solution)/shard_map/ppermute | solution.py:372
  8.7 10.6 %copy-start.3 = (bf16[16,128,128]{2,1,0:T(8,128)(2,1)S(1)}, bf16[16,128,128]{2,1,0:T(8,128)(2,1)}, u32[]{:S(2)}) copy-start(bf16[16,128,128]{2,1,0:T(8,128)(2,1)} %own_ref.1) | copy-start | bytes 1572868
  8.7 10.6 %collective-permute-start.3 = (bf16[32,1152]{1,0:T(8,128)(2,1)}, bf16[32,1152]{1,0:T(8,128)(2,1)S(1)}, u32[]{:S(2)}, u32[]{:S(2)}) collective-permute-start(bf16[32,1152]{1,0:T(8,128)(2,1)} %get-tuple-element.27.refs_3_), channel_id=1, source_target_pairs={{8,16},{24,0},{16,8},{0,24},{9,17},{25,1},{17,9},{1,25},{10,18},{2... | collective-permute-start | bytes 221192 | tf_op jit(solution)/shard_map/ppermute | solution.py:372
  10.2 16.8 %collective-permute-start.4 = (bf16[16,128,128]{2,1,0:T(8,128)(2,1)}, bf16[16,128,128]{2,1,0:T(8,128)(2,1)S(1)}, u32[]{:S(2)}, u32[]{:S(2)}) collective-permute-start(bf16[16,128,128]{2,1,0:T(8,128)(2,1)} %own_ref.1), channel_id=1, source_target_pairs={{0,6},{1,7},{6,0},{7,1},{8,14},{9,15},{14,8},{15,9},{16,22},{17,23... | collective-permute-start | bytes 1572872 | tf_op jit(solution)/shard_map/ppermute | solution.py:419
  19.3 0.8 copy-start.10
  19.3 0.8 copy-start.11
  19.3 0.8 copy-start.8
  19.3 0.8 copy-start.9
  19.3 8.5 %collective-permute-start.5 = (bf16[16,128,128]{2,1,0:T(8,128)(2,1)S(1)}, bf16[16,128,128]{2,1,0:T(8,128)(2,1)S(1)}, u32[]{:S(2)}, u32[]{:S(2)}) collective-permute-start(bf16[16,128,128]{2,1,0:T(8,128)(2,1)S(1)} %copy-done.3), channel_id=1, source_target_pairs={{2,4},{3,5},{4,2},{5,3},{10,12},{11,13},{12,10},{13,11},{18,20},{1... | collective-permute-start | bytes 1572872 | tf_op jit(solution)/shard_map/ppermute | solution.py:460
  23.3 26.0 %all-to-all-start = ((bf16[16,49,8,128]{3,2,1,0:T(8,128)(2,1)}), bf16[16,49,8,128]{3,2,1,0:T(8,128)(2,1)S(1)}, u32[]{:S(2)}, u32[]{:S(2)}) async-start(bf16[16,49,8,128]{3,2,1,0:T(8,128)(2,1)} %bitcast.8), calls=%async_computation | async-start | bytes 3211264 | tf_op jit(solution)/shard_map/all_to_all | solution.py:488
  27.0 0.8 copy-start.4
  27.8 0.8 copy-start.6
  28.6 1.0 %copy-start.5 = (bf16[16,128,128]{2,1,0:T(8,128)(2,1)S(1)}, bf16[16,128,128]{2,1,0:T(8,128)(2,1)}, u32[]{:S(2)}) copy-start(bf16[16,128,128]{2,1,0:T(8,128)(2,1)} %copy-done.4) | copy-start | bytes 1572868
  29.6 1.0 %copy-start.7 = (bf16[16,128,128]{2,1,0:T(8,128)(2,1)S(1)}, bf16[16,128,128]{2,1,0:T(8,128)(2,1)}, u32[]{:S(2)}) copy-start(bf16[16,128,128]{2,1,0:T(8,128)(2,1)} %copy-done.6) | copy-start | bytes 1572868
  53.2 25.2 %copy-start = (f32[4096,128]{1,0:T(8,128)S(1)}, f32[4096,128]{1,0:T(8,128)}, u32[]{:S(2)}) copy-start(f32[4096,128]{1,0:T(8,128)} %get-tuple-element.39.dyn_ref) | copy-start | bytes 6291460
  53.2 25.2 %copy-start.1 = (f32[768,128]{1,0:T(8,128)S(1)}, f32[768,128]{1,0:T(8,128)}, u32[]{:S(2)}) copy-start(f32[768,128]{1,0:T(8,128)} %get-tuple-element.40.rim_ref) | copy-start | bytes 1179652
  53.2 25.2 %copy-start.2 = (s32[16,128]{1,0:T(8,128)S(1)}, s32[16,128]{1,0:T(8,128)}, u32[]{:S(2)}) copy-start(s32[16,128]{1,0:T(8,128)} %get-tuple-element.23.pos_ref) | copy-start | bytes 24580

commit v5 on v4

--- a/solution.py
+++ b/solution.py
@@ -8,9 +8,10 @@
 from jax.sharding import Mesh
 from jax.sharding import PartitionSpec as P
 
-RIM_VMEM = 62
+RIM_VMEM = 64
 BULK_COST = 5
 TURN_COST = 30
+INNER_COST = 1
 SLOTS = 48
 DIFFUSE = 0.1
 GROUP_AXES = ("lat", "lo")
@@ -114,10 +115,10 @@
 
 
 def bulk_kernel(cap, owned, lons, lows, place_ref, *refs):
-    sources, outputs, held, rest = refs[:5], refs[5:11], refs[11:16], refs[16:]
-    send_hbm, back_ref, pos_ref, dyn_hbm, rim_q, rim_dyn = outputs
+    sources, outputs, held, rest = refs[:5], refs[5:9], refs[9:14], refs[14:]
+    send_hbm, back_hbm, pos_hbm, dyn_hbm = outputs
     span_ref, slot_ref, q_ref, u_ref, v_ref = held
-    sems, row_sems, member, pos_s, send_ref, dyn_ref, cell, wind_x, face_x, wind_y, face_y, flux_y = rest
+    sems, row_sems, member, back_ref, pos_ref, pos_s, send_ref, dyn_ref, cell, wind_x, face_x, wind_y, face_y, flux_y = rest
     rows, cells, width = q_ref.shape
     levels = u_ref.shape[2]
     tracers = width // levels
@@ -127,6 +128,13 @@
     copies = [pltpu.make_async_copy(a, b, sems.at[n]) for n, (a, b) in enumerate(zip(sources, held))]
     for copy in copies:
         copy.start()
+    for copy in copies[:2]:
+        copy.wait()
+    plan(place_ref, span_ref, slot_ref, send_ref, back_ref, member, pos_ref, cap, owned, lons, lows)
+    places = [(pos_ref, pos_s), (pos_ref, pos_hbm), (back_ref, back_hbm)]
+    places = [pltpu.make_async_copy(a, b, sems.at[5 + n]) for n, (a, b) in enumerate(places)]
+    for copy in places:
+        copy.start()
     copies[2].wait()
 
     def relayout(i, carry):
@@ -137,11 +145,6 @@
         return carry
 
     lax.fori_loop(0, rows, relayout, 0)
-    for copy in copies[:2]:
-        copy.wait()
-    plan(place_ref, span_ref, slot_ref, send_ref, back_ref, member, pos_ref, cap, owned, lons, lows)
-    pos_copy = pltpu.make_async_copy(pos_ref, pos_s, sems.at[5])
-    pos_copy.start()
     for copy in copies[3:]:
         copy.wait()
 
@@ -158,11 +161,10 @@
     def spread_row(ref, r):
         return jnp.broadcast_to(ref[pl.ds(r, 1), :], (tracers, levels))
 
-    pos_copy.wait()
+    places[0].wait()
 
     def dyn_copy(i):
-        rows_i = pl.ds(pl.multiple_of(i * line, tracers), line)
-        return pltpu.make_async_copy(dyn_ref.at[rows_i], dyn_hbm.at[rows_i], row_sems.at[i])
+        return pltpu.make_async_copy(dyn_ref.at[i], dyn_hbm.at[i], row_sems.at[i])
 
     def row(i, carry):
         diffuse_y = jnp.where(i == rows - 1, 0.0, DIFFUSE)
@@ -181,37 +183,31 @@
             flux_s = flux_y[j * tracers : (j + 1) * tracers, :]
             flux_y[j * tracers : (j + 1) * tracers, :] = flux_n
             dyn = (flux_w - flux_e) + (flux_s - flux_n)
-            dyn_ref[tile(i, j), :] = dyn
+            dyn_ref[i, j * tracers : (j + 1) * tracers, :] = dyn
             send_ref[pos_s[i, j]] = (here + dyn).astype(jnp.bfloat16)
-            if j in (0, cells - 1):
-                at = pl.multiple_of((2 * cells + (j > 0) * rows + i) * tracers, tracers)
-                rim_q[pl.ds(at, tracers), :] = here
-                rim_dyn[pl.ds(at, tracers), :] = dyn
             here, flux_w = after, flux_e
         dyn_copy(i).start()
         return carry
 
     lax.fori_loop(0, rows, row, 0)
-    send_copy = pltpu.make_async_copy(send_ref, send_hbm, sems.at[6])
+    send_copy = pltpu.make_async_copy(send_ref, send_hbm, sems.at[8])
     send_copy.start()
-    for n, i in enumerate((0, rows - 1)):
-        rim_q[n * line : (n + 1) * line, :] = cell[i * line : (i + 1) * line, :]
-        rim_dyn[n * line : (n + 1) * line, :] = dyn_ref[i * line : (i + 1) * line, :]
-    send_copy.wait()
-
+    for copy in places[1:]:
+        copy.wait()
     def drain(i, carry):
         dyn_copy(i).wait()
         return carry
 
     lax.fori_loop(0, rows, drain, 0)
+    send_copy.wait()
 
 
 def rim_kernel(lats, lons, place_ref, *refs):
-    sources, (send_in, send_hbm, rim_ref), rest = refs[:11], refs[11:14], refs[14:]
-    own_lon, own_lat, far_lon, far_lat, pos_s, rim_q, rim_dyn, side, stage, sems = rest
+    sources, dyn_hbm, (send_in, send_hbm, rim_ref), rest = refs[:9], refs[9], refs[10:13], refs[13:]
+    own_lon, own_lat, far_lon, far_lat, pos_s, row_dyn, side_dyn, rim_q, side, stage, sems = rest
     rows, cells = own_lon.shape[1], own_lat.shape[1]
     levels = side.shape[1]
-    tracers = rim_q.shape[0] // (2 * (rows + cells))
+    tracers = row_dyn.shape[1] // cells
     width = tracers * levels
     f32 = jnp.float32
     odd_lon, odd_lat = parities(place_ref[0], lons)
@@ -225,10 +221,15 @@
         far_lat.at[1 - odd_lat],
         far_lat.at[odd_lat],
         pos_s,
-        rim_q,
-        rim_dyn,
     )
-    copies = [pltpu.make_async_copy(a, b, sems.at[n]) for n, (a, b) in enumerate(zip(sources, targets))]
+    pairs = list(zip(sources, targets))
+    line = cells * tracers
+    west, east = 2 * cells, 2 * cells + rows
+    for n, i in enumerate((0, rows - 1)):
+        pairs.append((dyn_hbm.at[i], row_dyn.at[n]))
+    for n, j in enumerate((0, cells - 1)):
+        pairs.append((dyn_hbm.at[:, j * tracers : (j + 1) * tracers, :], side_dyn.at[n]))
+    copies = [pltpu.make_async_copy(a, b, sems.at[n]) for n, (a, b) in enumerate(pairs)]
     for copy in copies:
         copy.start()
     for copy in copies[:8]:
@@ -246,14 +247,13 @@
             for t in range(tracers):
                 lanes = slice(t * levels, (t + 1) * levels)
                 here, there = own[n, :, lanes].astype(f32), far[n, :, lanes].astype(f32)
-                side[pl.ds(first * tracers + t, count, stride=tracers), :] = face * (
-                    here + there
-                ) + diffuse * (there - here)
+                at = pl.ds(first * tracers + t, count, stride=tracers)
+                rim_q[at, :] = here
+                side[at, :] = face * (here + there) + diffuse * (there - here)
             first += count
     for copy in copies[8:]:
         copy.wait()
     tile = lambda n: slice(n * tracers, (n + 1) * tracers)
-    west, east = 2 * cells, 2 * cells + rows
     rim = []
     for n, i in enumerate((0, rows - 1)):
         for j in range(cells):
@@ -263,7 +263,11 @@
         rim += [(west + i, i, 0, ()), (east + i, i, cells - 1, ())]
     sent = sems.at[len(copies)]
     for m, (n, i, j, extra) in enumerate(rim):
-        dyn = rim_dyn[tile(n), :] + side[tile(n), :]
+        if n < west:
+            dyn = row_dyn[n // cells, tile(n % cells), :]
+        else:
+            dyn = side_dyn[(n - west) // rows, (n - west) % rows]
+        dyn = dyn + side[tile(n), :]
         for e in extra:
             dyn = dyn + side[tile(e), :]
         rim_ref[tile(n), :] = dyn
@@ -272,25 +276,14 @@
     pltpu.make_async_copy(stage, send_hbm.at[pl.ds(0, len(rim))], sent).wait()
 
 
-def turn_kernel(lows, place_ref, own_ref, outer_ref, inner_ref, out_ref):
-    owned = own_ref.shape[0]
-    place = place_ref[0]
-    is_outer = ((place >> log2(lows)) & 1) == ((place >> (log2(lows) - 1)) & 1)
-    for k in range(owned):
-        out_ref[k] = own_ref[k].T
-
-    @pl.when(is_outer)
-    def _():
-        for k in range(owned):
-            out_ref[owned + k] = outer_ref[k].T
-
-    @pl.when(jnp.logical_not(is_outer))
-    def _():
-        for k in range(owned):
-            out_ref[owned + k] = inner_ref[k].T
-
-
-def relax_kernel(x_ref, w_ref, y_ref, pos, pos_s, sem, slots):
+def turn_kernel(*refs):
+    refs, out_ref = refs[:-1], refs[-1]
+    for n, ref in enumerate(refs):
+        for k in range(ref.shape[0]):
+            out_ref[n * ref.shape[0] + k] = ref[k].T
+
+
+def relax_kernel(lows, place_ref, x_ref, outer_ref, inner_ref, y_ref, pos, pos_s, sem, slots):
     tracers, levels = x_ref.shape[1:]
     peers, lanes = pos.shape
     stored = x_ref.shape[0] // peers
@@ -303,29 +296,43 @@
     copy.start()
     copy.wait()
 
-    def place(at):
+    def tile(at):
         return pl.ds(pl.multiple_of(at * tracers, tracers), tracers)
 
     def scatter(p, carry):
         for r in range(cap):
-            slots[place(pos_s[p, r]), :] = x_ref[p * stored + r].astype(f32)
+            slots[tile(pos_s[p, r]), :] = x_ref[p * stored + r].astype(f32)
         return carry
 
     lax.fori_loop(0, peers, scatter, 0)
     block = SLOTS * tracers
 
-    def span(k, carry):
-        at = pl.ds(pl.multiple_of(k * block, block), block)
-        x = slots[at, :]
-        y = jnp.dot(x.astype(jnp.bfloat16), w_ref[k], preferred_element_type=f32)
-        slots[at, :] = y - x
-        return carry
-
-    lax.fori_loop(0, w_ref.shape[0], span, 0, unroll=8)
+    def relax(first, count, w_ref, w_first):
+        def span(k, carry):
+            at = pl.ds(pl.multiple_of((first + k) * block, block), block)
+            x = slots[at, :]
+            y = jnp.dot(x.astype(jnp.bfloat16), w_ref[w_first + k], preferred_element_type=f32)
+            slots[at, :] = y - x
+            return carry
+
+        lax.fori_loop(0, count, span, 0, unroll=8)
+
+    owned = inner_ref.shape[0]
+    place = place_ref[0]
+    is_outer = ((place >> log2(lows)) & 1) == ((place >> (log2(lows) - 1)) & 1)
+    relax(0, owned, outer_ref, 0)
+
+    @pl.when(is_outer)
+    def _():
+        relax(owned, owned, outer_ref, owned)
+
+    @pl.when(jnp.logical_not(is_outer))
+    def _():
+        relax(owned, owned, inner_ref, 0)
 
     def gather(p, carry):
         for r in range(cap):
-            y_ref[p * cap + r] = slots[place(pos_s[p, r]), :].astype(jnp.bfloat16)
+            y_ref[p * cap + r] = slots[tile(pos_s[p, r]), :].astype(jnp.bfloat16)
         return carry
 
     lax.fori_loop(0, peers, gather, 0)
@@ -354,7 +361,7 @@
         def dyn(j):
             if j in (0, cells - 1):
                 return rim_ref[tile(2 * cells + (j > 0) * rows + i), :]
-            return dyn_ref[tile(i * cells + j), :]
+            return dyn_ref[i, j * tracers : (j + 1) * tracers, :]
 
         row(i, dyn)
         return carry
@@ -401,7 +408,7 @@
             pltpu.VMEM((rows, width + levels), f32),
             dma((8,)),
         ],
-        compiler_params=params(62),
+        compiler_params=params(64),
         name="edges",
     )(place, tracers, east_wind, north_wind)
     edges = (lon_a, lon_b, lat_a, lat_b)
@@ -423,27 +430,28 @@
     fields = (span_of, slot_of, tracers, east_wind, north_wind)
     rim_shape = (2 * (rows + cells) * kinds, levels)
     block_shape = (columns * kinds, levels)
+    dyn_shape = (rows, cells * kinds, levels)
     send_shape = (peers * stored, kinds, levels)
-    send, back, pos, dyn, rim_q, rim_dyn = pl.pallas_call(
+    send, back, pos, dyn = pl.pallas_call(
         functools.partial(bulk_kernel, cap, owned, lons, lows),
         out_shape=(
             jax.ShapeDtypeStruct(send_shape, bf16),
             jax.ShapeDtypeStruct((rows, 128), i32),
             jax.ShapeDtypeStruct((rows, 128), i32),
-            jax.ShapeDtypeStruct(block_shape, f32),
-            jax.ShapeDtypeStruct(rim_shape, f32),
-            jax.ShapeDtypeStruct(rim_shape, f32),
+            jax.ShapeDtypeStruct(dyn_shape, f32),
         ),
         in_specs=[SMEM] + [ANY] * 5,
-        out_specs=(ANY, VMEM, VMEM, ANY, VMEM, VMEM),
+        out_specs=(ANY,) * 4,
         scratch_shapes=[pltpu.VMEM(x.shape, x.dtype) for x in fields]
         + [
-            dma((7,)),
+            dma((9,)),
             dma((rows,)),
             pltpu.VMEM((rows * peers, cells), f32),
+            pltpu.VMEM((rows, 128), i32),
+            pltpu.VMEM((rows, 128), i32),
             pltpu.SMEM((rows, 128), i32),
             pltpu.VMEM(send_shape, bf16),
-            pltpu.VMEM(block_shape, f32),
+            pltpu.VMEM(dyn_shape, f32),
             pltpu.VMEM(block_shape, f32),
             pltpu.VMEM((columns + 8, levels), f32),
             pltpu.VMEM((columns, levels), f32),
@@ -451,20 +459,18 @@
             pltpu.VMEM((columns, levels), f32),
             pltpu.VMEM((cells * kinds, levels), f32),
         ],
-        compiler_params=params(62),
+        compiler_params=params(64),
         cost_estimate=cost(BULK_COST),
         name="bulk",
     )(place, *fields)
 
-    matrices, pos, *far_edges = lax.optimization_barrier((inverses, pos, *far_edges))
-    inner = lax.ppermute(matrices, LON_AXES, opposite(lows // 2, lows))
-
-    rim_args = (*edges, *far_edges, pos, rim_q, rim_dyn)
+
+    rim_args = (*edges, *far_edges, pos, dyn)
     both = lambda x: pltpu.VMEM((2,) + x.shape, x.dtype)
     send, rim = pl.pallas_call(
         functools.partial(rim_kernel, lats, lons),
         out_shape=(jax.ShapeDtypeStruct(send_shape, bf16), jax.ShapeDtypeStruct(rim_shape, f32)),
-        in_specs=[SMEM] + [ANY] * 12,
+        in_specs=[SMEM] + [ANY] * 11,
         out_specs=(ANY, VMEM),
         scratch_shapes=[
             both(lon_a),
@@ -472,16 +478,20 @@
             both(lon_a),
             both(lat_a),
             pltpu.SMEM((rows, 128), i32),
-            pltpu.VMEM(rim_shape, f32),
+            pltpu.VMEM((2,) + dyn_shape[1:], f32),
+            pltpu.VMEM((2, rows, kinds, levels), f32),
             pltpu.VMEM(rim_shape, f32),
             pltpu.VMEM(rim_shape, f32),
             pltpu.VMEM((2 * (rows + cells) - 4, kinds, levels), bf16),
-            dma((12,)),
+            dma((14,)),
         ],
-        input_output_aliases={12: 0},
+        input_output_aliases={11: 0},
         compiler_params=params(RIM_VMEM),
         name="rim",
     )(place, *rim_args, send)
+
+    matrices, send = lax.optimization_barrier((inverses, send))
+    inner = lax.ppermute(matrices, LON_AXES, opposite(lows // 2, lows))
 
     def exchange(x):
         x = x.reshape(peers, -1, kinds, levels)
@@ -489,19 +499,21 @@
         return x.reshape(-1, kinds, levels)
 
     arrived = exchange(send)
-    turned = pl.pallas_call(
-        functools.partial(turn_kernel, lows),
-        out_shape=jax.ShapeDtypeStruct((2 * owned, levels, levels), bf16),
+    def turned(us, *arrays):
+        return pl.pallas_call(
+            turn_kernel,
+            out_shape=jax.ShapeDtypeStruct((len(arrays) * owned, levels, levels), bf16),
+            in_specs=[VMEM] * len(arrays),
+            out_specs=VMEM,
+            compiler_params=params(16),
+            cost_estimate=cost(us),
+            name="turn",
+        )(*arrays)
+
+    physics = pl.pallas_call(
+        functools.partial(relax_kernel, lows),
+        out_shape=jax.ShapeDtypeStruct((peers * cap, kinds, levels), bf16),
         in_specs=[SMEM] + [VMEM] * 3,
-        out_specs=VMEM,
-        compiler_params=params(16),
-        cost_estimate=cost(TURN_COST),
-        name="turn",
-    )(place, inverses, outer, inner)
-    physics = pl.pallas_call(
-        relax_kernel,
-        out_shape=jax.ShapeDtypeStruct((peers * cap, kinds, levels), bf16),
-        in_specs=[VMEM] * 2,
         out_specs=VMEM,
         scratch_shapes=[
             pltpu.VMEM((peers, 128), i32),
@@ -511,7 +523,7 @@
         ],
         compiler_params=params(24),
         name="relax",
-    )(arrived, turned)
+    )(place, arrived, turned(TURN_COST, inverses, outer), turned(INNER_COST, inner))
 
     returned = exchange(physics)
     return pl.pallas_call(

time: 81.2 us -> 78.7 us (0.969)
  local copies, waits for them, and re-layouts: 3.71 us -> 0.02 us
  waiting for transfers between devices: 18.3 us -> 20 us
    unnamed x24 -> x8, local copies, waits for them, and re-layouts: 3.71 us -> 0.02 us
    pallas_call x1, Pallas kernels: 6.66 us -> 4.93 us  [shards(): pl.pallas_call(functools.partial(bulk_kernel, cap, owned, lons, lows), ou...]
    all_to_all x1, waiting for transfers between devices: 18.2 us -> 19.6 us  [exchange(): x = lax.all_to_all(x, GROUP_AXES, split_axis=0, concat_axis=0, tiled=True)]
    pallas_call x2 -> x3, Pallas kernels: 4.27 us -> 5.47 us  [the longest x1 3.92 us: shards(): pl.pallas_call(functools.partial(relax_kernel, lows), out_shape=jax.Shape...]
  transfers between devices with their start and end apart: 7 -> 7, of which waited for: 1 -> 2; matrix products, arithmetic and copies ran while one was open for 0% -> 0% of each run, Pallas kernels for 13% -> 12%
where the time goes in v5:
time: 78.7 us; the launch traced here: 78.3 us
  blocking collectives  25.2 us (32%)
  waiting for transfers between devices  20 us (25%)
  Pallas kernels  17.8 us (23%)
  starting transfers between devices  15.1 us (19%)
    all_to_all x1, blocking collectives, exchange(): x = lax.all_to_all(x, GROUP_AXES, split_axis=0, concat_axis=0, tiled=True)  25.2 us
    all_to_all x1, waiting for transfers between devices, exchange(): x = lax.all_to_all(x, GROUP_AXES, split_axis=0, concat_axis=0, tiled=True)  19.6 us
    ppermute x4, starting transfers between devices, in_pairs(): return lax.ppermute(x, axis, pairs + [(b, a) for a, b in pairs])  8.21 us
    pallas_call x1, Pallas kernels, shards(): pl.pallas_call(functools.partial(bulk_kernel, cap, owned, lons, lows), ou...  4.93 us
    pallas_call x1, Pallas kernels, shards(): pl.pallas_call(functools.partial(relax_kernel, lows), out_shape=jax.Shape...  3.92 us
    all_to_all x1, starting transfers between devices, exchange(): x = lax.all_to_all(x, GROUP_AXES, split_axis=0, concat_axis=0, tiled=True)  3.85 us
    pallas_call x1, Pallas kernels, shards(): pl.pallas_call(functools.partial(rim_kernel, lats, lons), out_shape=(jax....  3.01 us
    pallas_call x1, Pallas kernels, shards(): pl.pallas_call(finish_kernel, out_shape=jax.ShapeDtypeStruct((rows, cells...  2.37 us
  transfers between devices with their start and end apart: 7, of which 2 were waited for; matrix products, arithmetic and copies ran while one was open for 0% of the time, Pallas kernels for 12%

profile of v5, /device:TPU:0, one launch (start us, length us, event | category | flops | bytes accessed | tf_op | source)
XLA Modules:
  0.0 78.3 jit_solution(12761007332786461812)
XLA Ops:
  0.0 2.0 %edges.1 = (bf16[16,1152]{1,0:T(8,128)(2,1)}, bf16[16,1152]{1,0:T(8,128)(2,1)}, bf16[32,1152]{1,0:T(8,128)(2,1)}, bf16[32,1152]{1,0:T(8,128)(2,1)}) custom-call(s32[1]{0:T(128)} %bitcast.place_ref, bf16[16,32,1024]{2,1,0:T(8,128)(2,1)} %q_hbm.1, bf16[16,32,128]{2,1,0:T(8,128)(2,1)} %u_hbm.1, bf16[16,32,128]{2,1,0:T(8,128)(2,1)} %v_hbm.1), custom_call_target="tpu_custom_call" | custom-call | tf_op jit(solution)/shard_map/edges/pallas_call | solution.py:399
  2.0 0.5 collective-permute-start
  2.5 4.7 %collective-permute-start.1 = (bf16[16,1152]{1,0:T(8,128)(2,1)}, bf16[16,1152]{1,0:T(8,128)(2,1)}, u32[]{:S(2)}, u32[]{:S(2)}) collective-permute-start(bf16[16,1152]{1,0:T(8,128)(2,1)} %get-tuple-element.19.refs_1_), channel_id=1, source_target_pairs={{1,2},{3,4},{5,6},{7,0},{2,1},{4,3},{6,5},{0,7},{9,10},{11,12},{13... | collective-permute-start | bytes 110600 | tf_op jit(solution)/shard_map/ppermute | solution.py:379
  7.2 1.5 %collective-permute-start.2 = (bf16[32,1152]{1,0:T(8,128)(2,1)}, bf16[32,1152]{1,0:T(8,128)(2,1)}, u32[]{:S(2)}, u32[]{:S(2)}) collective-permute-start(bf16[32,1152]{1,0:T(8,128)(2,1)} %get-tuple-element.20.refs_2_), channel_id=1, source_target_pairs={{0,8},{16,24},{8,0},{24,16},{1,9},{17,25},{9,1},{25,17},{2,10},{18... | collective-permute-start | bytes 221192 | tf_op jit(solution)/shard_map/ppermute | solution.py:379
  8.7 1.5 %collective-permute-start.3 = (bf16[32,1152]{1,0:T(8,128)(2,1)}, bf16[32,1152]{1,0:T(8,128)(2,1)}, u32[]{:S(2)}, u32[]{:S(2)}) collective-permute-start(bf16[32,1152]{1,0:T(8,128)(2,1)} %get-tuple-element.21.refs_3_), channel_id=1, source_target_pairs={{8,16},{24,0},{16,8},{0,24},{9,17},{25,1},{17,9},{1,25},{10,18},{2... | collective-permute-start | bytes 221192 | tf_op jit(solution)/shard_map/ppermute | solution.py:379
  10.2 2.3 %collective-permute-start.4 = (bf16[16,128,128]{2,1,0:T(8,128)(2,1)}, bf16[16,128,128]{2,1,0:T(8,128)(2,1)}, u32[]{:S(2)}, u32[]{:S(2)}) collective-permute-start(bf16[16,128,128]{2,1,0:T(8,128)(2,1)} %refs_0_.3), channel_id=1, source_target_pairs={{0,6},{1,7},{6,0},{7,1},{8,14},{9,15},{14,8},{15,9},{16,22},{17,23... | collective-permute-start | bytes 1572872 | tf_op jit(solution)/shard_map/ppermute | solution.py:426
  12.6 4.9 %bulk.1 = (bf16[784,8,128]{2,1,0:T(8,128)(2,1)}, s32[16,128]{1,0:T(8,128)}, s32[16,128]{1,0:T(8,128)}, f32[16,256,128]{2,1,0:T(8,128)}) custom-call(s32[1]{0:T(128)} %bitcast.place_ref, s32[16,32]{1,0:T(8,128)} %refs_0_.2, s32[16,32]{1,0:T(8,128)} %refs_1_.1, bf16[16,32,1024]{2,1,0:T(8,128)(2,1)} %q_hbm.1, bf16[16,32,128]{2,1,0:T(8,128)(2,1)} %u_hbm.1, ...), custom_call_target="tpu_custom_call" | custom-call | flops 5000000000 | bytes 1048576 | tf_op jit(solution)/shard_map/bulk/pallas_call | solution.py:435
  17.5 0.0 collective-permute-done.refs_4_
  17.5 0.0 collective-permute-done.1.refs_5_
  17.5 0.0 collective-permute-done.2.refs_6_
  17.5 0.0 collective-permute-done.3.refs_7_
  17.6 3.0 %rim.1 = (bf16[784,8,128]{2,1,0:T(8,128)(2,1)}, f32[768,128]{1,0:T(8,128)}) custom-call(s32[1]{0:T(128)} %bitcast.place_ref, bf16[16,1152]{1,0:T(8,128)(2,1)} %get-tuple-element.18.refs_0_, bf16[16,1152]{1,0:T(8,128)(2,1)} %get-tuple-element.19.refs_1_, bf16[32,1152]{1,0:T(8,128)(2,1)} %get-tuple-element.20.refs_2_, ...), custom_call_target="tpu_custom_call", output_to_operand_aliasing={{0}: (11, {})} | custom-call | tf_op jit(solution)/shard_map/rim/pallas_call | solution.py:470
  20.6 0.0 copy-start.3
  20.6 3.9 %all-to-all-start = ((bf16[16,49,8,128]{3,2,1,0:T(8,128)(2,1)}), bf16[16,49,8,128]{3,2,1,0:T(8,128)(2,1)S(1)}, u32[]{:S(2)}, u32[]{:S(2)}) async-start(bf16[16,49,8,128]{3,2,1,0:T(8,128)(2,1)} %bitcast.8), calls=%async_computation | async-start | bytes 3211264 | tf_op jit(solution)/shard_map/all_to_all | solution.py:498
  24.4 0.0 copy-done.3
  24.5 0.7 collective-permute-start.5
  25.2 0.4 collective-permute-done.4.refs_1_
  25.5 1.4 %turn.2.outer_ref = bf16[32,128,128]{2,1,0:T(8,128)(2,1)S(1)} custom-call(bf16[16,128,128]{2,1,0:T(8,128)(2,1)S(1)} %copy-done.3, bf16[16,128,128]{2,1,0:T(8,128)(2,1)} %collective-permute-done.4.refs_1_), custom_call_target="tpu_custom_call" | custom-call | flops 30000001024 | bytes 1048576 | tf_op jit(solution)/shard_map/turn/pallas_call | solution.py:503
  26.9 0.0 collective-permute-done.5.refs_0_
  26.9 0.2 turn.3.inner_ref
  27.1 19.6 %all-to-all-done = bf16[16,49,8,128]{3,2,1,0:T(8,128)(2,1)S(1)} async-done(((bf16[16,49,8,128]{3,2,1,0:T(8,128)(2,1)}), bf16[16,49,8,128]{3,2,1,0:T(8,128)(2,1)S(1)}, u32[]{:S(2)}, u32[]{:S(2)}) %all-to-all-start) | async-done | bytes 1605664 | tf_op jit(solution)/shard_map/all_to_all | solution.py:498
  46.8 3.9 %relax.1 = bf16[768,8,128]{2,1,0:T(8,128)(2,1)S(1)} custom-call(s32[1]{0:T(128)} %bitcast.place_ref, bf16[784,8,128]{2,1,0:T(8,128)(2,1)S(1)} %bitcast.5, bf16[32,128,128]{2,1,0:T(8,128)(2,1)S(1)} %turn.2.outer_ref, bf16[16,128,128]{2,1,0:T(8,128)(2,1)S(1)} %turn.3.inner_ref), custom_call_target="tpu_custom_call" | custom-call | tf_op jit(solution)/shard_map/relax/pallas_call | solution.py:513
  50.7 0.0 copy-start
  50.7 0.0 copy-start.1
  50.7 0.0 copy-start.2
  50.7 25.2 %all_to_all.10 = bf16[16,48,8,128]{3,2,1,0:T(8,128)(2,1)S(1)} all-to-all(bf16[16,48,8,128]{3,2,1,0:T(8,128)(2,1)S(1)} %bitcast.6), channel_id=1, replica_groups=mesh['lat'=4,'hi'=2,'lo'=4] {'lat','lo'}, dimensions={0} | all-to-all | bytes 3145728 | tf_op jit(solution)/shard_map/all_to_all | solution.py:498
  75.9 0.0 copy-done
  75.9 0.0 copy-done.1
  75.9 0.0 copy-done.2
  75.9 2.4 %finish.1 = f32[16,32,1024]{2,1,0:T(8,128)} custom-call(s32[16,128]{1,0:T(8,128)S(1)} %copy-done.2, bf16[768,8,128]{2,1,0:T(8,128)(2,1)S(1)} %bitcast.7, f32[16,256,128]{2,1,0:T(8,128)S(1)} %copy-done, f32[768,128]{1,0:T(8,128)S(1)} %copy-done.1), custom_call_target="tpu_custom_call" | custom-call | tf_op jit(solution)/shard_map/finish/pallas_call | solution.py:529
Async XLA Ops:
  2.0 15.5 %collective-permute-start = (bf16[16,1152]{1,0:T(8,128)(2,1)}, bf16[16,1152]{1,0:T(8,128)(2,1)}, u32[]{:S(2)}, u32[]{:S(2)}) collective-permute-start(bf16[16,1152]{1,0:T(8,128)(2,1)} %get-tuple-element.18.refs_0_), channel_id=1, source_target_pairs={{0,1},{2,3},{4,5},{6,7},{1,0},{3,2},{5,4},{7,6},{8,9},{10,11},{12,... | collective-permute-start | bytes 110600 | tf_op jit(solution)/shard_map/ppermute | solution.py:379
  2.5 15.0 %collective-permute-start.1 = (bf16[16,1152]{1,0:T(8,128)(2,1)}, bf16[16,1152]{1,0:T(8,128)(2,1)}, u32[]{:S(2)}, u32[]{:S(2)}) collective-permute-start(bf16[16,1152]{1,0:T(8,128)(2,1)} %get-tuple-element.19.refs_1_), channel_id=1, source_target_pairs={{1,2},{3,4},{5,6},{7,0},{2,1},{4,3},{6,5},{0,7},{9,10},{11,12},{13... | collective-permute-start | bytes 110600 | tf_op jit(solution)/shard_map/ppermute | solution.py:379
  7.2 10.3 %collective-permute-start.2 = (bf16[32,1152]{1,0:T(8,128)(2,1)}, bf16[32,1152]{1,0:T(8,128)(2,1)}, u32[]{:S(2)}, u32[]{:S(2)}) collective-permute-start(bf16[32,1152]{1,0:T(8,128)(2,1)} %get-tuple-element.20.refs_2_), channel_id=1, source_target_pairs={{0,8},{16,24},{8,0},{24,16},{1,9},{17,25},{9,1},{25,17},{2,10},{18... | collective-permute-start | bytes 221192 | tf_op jit(solution)/shard_map/ppermute | solution.py:379
  8.7 8.8 %collective-permute-start.3 = (bf16[32,1152]{1,0:T(8,128)(2,1)}, bf16[32,1152]{1,0:T(8,128)(2,1)}, u32[]{:S(2)}, u32[]{:S(2)}) collective-permute-start(bf16[32,1152]{1,0:T(8,128)(2,1)} %get-tuple-element.21.refs_3_), channel_id=1, source_target_pairs={{8,16},{24,0},{16,8},{0,24},{9,17},{25,1},{17,9},{1,25},{10,18},{2... | collective-permute-start | bytes 221192 | tf_op jit(solution)/shard_map/ppermute | solution.py:379
  10.2 15.3 %collective-permute-start.4 = (bf16[16,128,128]{2,1,0:T(8,128)(2,1)}, bf16[16,128,128]{2,1,0:T(8,128)(2,1)}, u32[]{:S(2)}, u32[]{:S(2)}) collective-permute-start(bf16[16,128,128]{2,1,0:T(8,128)(2,1)} %refs_0_.3), channel_id=1, source_target_pairs={{0,6},{1,7},{6,0},{7,1},{8,14},{9,15},{14,8},{15,9},{16,22},{17,23... | collective-permute-start | bytes 1572872 | tf_op jit(solution)/shard_map/ppermute | solution.py:426
  20.6 3.9 %copy-start.3 = (bf16[16,128,128]{2,1,0:T(8,128)(2,1)S(1)}, bf16[16,128,128]{2,1,0:T(8,128)(2,1)}, u32[]{:S(2)}) copy-start(bf16[16,128,128]{2,1,0:T(8,128)(2,1)} %refs_0_.3) | copy-start | bytes 1572868
  20.6 26.2 %all-to-all-start = ((bf16[16,49,8,128]{3,2,1,0:T(8,128)(2,1)}), bf16[16,49,8,128]{3,2,1,0:T(8,128)(2,1)S(1)}, u32[]{:S(2)}, u32[]{:S(2)}) async-start(bf16[16,49,8,128]{3,2,1,0:T(8,128)(2,1)} %bitcast.8), calls=%async_computation | async-start | bytes 3211264 | tf_op jit(solution)/shard_map/all_to_all | solution.py:498
  24.5 2.5 %collective-permute-start.5 = (bf16[16,128,128]{2,1,0:T(8,128)(2,1)S(1)}, bf16[16,128,128]{2,1,0:T(8,128)(2,1)S(1)}, u32[]{:S(2)}, u32[]{:S(2)}) collective-permute-start(bf16[16,128,128]{2,1,0:T(8,128)(2,1)S(1)} %copy-done.3), channel_id=1, source_target_pairs={{2,4},{3,5},{4,2},{5,3},{10,12},{11,13},{12,10},{13,11},{18,20},{1... | collective-permute-start | bytes 1572872 | tf_op jit(solution)/shard_map/ppermute | solution.py:494
  50.7 25.2 %copy-start = (f32[16,256,128]{2,1,0:T(8,128)S(1)}, f32[16,256,128]{2,1,0:T(8,128)}, u32[]{:S(2)}) copy-start(f32[16,256,128]{2,1,0:T(8,128)} %get-tuple-element.23.refs_9_.dyn_ref) | copy-start | bytes 6291460
  50.7 25.2 %copy-start.1 = (f32[768,128]{1,0:T(8,128)S(1)}, f32[768,128]{1,0:T(8,128)}, u32[]{:S(2)}) copy-start(f32[768,128]{1,0:T(8,128)} %get-tuple-element.28.rim_ref) | copy-start | bytes 1179652
  50.7 25.2 %copy-start.2 = (s32[16,128]{1,0:T(8,128)S(1)}, s32[16,128]{1,0:T(8,128)}, u32[]{:S(2)}) copy-start(s32[16,128]{1,0:T(8,128)} %get-tuple-element.17.pos_ref) | copy-start | bytes 24580

commit v6 on v3

--- a/solution.py
+++ b/solution.py
@@ -10,6 +10,7 @@
 
 FLUX_COST = 10
 TURN_COST = 30
+INNER_COST = 1
 SLOTS = 48
 DIFFUSE = 0.1
 GROUP_AXES = ("lat", "lo")
@@ -69,8 +70,9 @@
     span, slot = span_ref[...], slot_ref[...]
     owner = span >> log2(owned)
     owner_lon = owner & (lons - 1)
-    peer = ((owner >> log2(lons)) << log2(lows)) + (owner_lon & (lows - 1))
     far = (owner_lon >> log2(lows)) != ((place_ref[0] >> log2(lows)) & 1)
+    low = (owner_lon & (lows - 1)) ^ jnp.where(far, lows // 2, 0)
+    peer = ((owner >> log2(lons)) << log2(lows)) + low
     local = (span & (owned - 1)) + jnp.where(far, owned, 0)
     iota = lambda shape, axis: lax.broadcasted_iota(jnp.int32, shape, axis)
     for i in range(rows):
@@ -120,14 +122,16 @@
     place_ref,
     *refs,
 ):
-    sources, (send_ref, pos_ref, dyn_hbm), rest = refs[:9], refs[9:12], refs[12:]
+    sources, (send_hbm, back_hbm, dyn_hbm), rest = refs[:9], refs[9:12], refs[12:]
     held, rest = rest[:7], rest[7:]
     (
         sems,
         row_sems,
         member,
+        back,
         pos,
         pos_s,
+        send_ref,
         dyn_ref,
         cell,
         wind,
@@ -161,6 +165,13 @@
             cell[pl.ds(first + t, count, stride=stride), :] = block(t).astype(f32)
 
     lanes = lambda t: slice(t * levels, (t + 1) * levels)
+    for copy in copies[:2]:
+        copy.wait()
+    plan(place_ref, span_ref, slot_ref, send_ref, back, member, pos, cap, owned, lons, lows)
+    pos_copy = pltpu.make_async_copy(pos, pos_s, sems.at[len(copies)])
+    pos_copy.start()
+    back_copy = pltpu.make_async_copy(back, back_hbm, sems.at[len(copies) + 1])
+    back_copy.start()
     copies[2].wait()
 
     def relayout(i, carry):
@@ -170,11 +181,6 @@
         return carry
 
     lax.fori_loop(0, rows, relayout, 0)
-    for copy in copies[:2]:
-        copy.wait()
-    plan(place_ref, span_ref, slot_ref, send_ref, pos_ref, member, pos, cap, owned, lons, lows)
-    pos_copy = pltpu.make_async_copy(pos, pos_s, sems.at[len(copies)])
-    pos_copy.start()
     for copy in copies[3:]:
         copy.wait()
     spread(lambda t: south_ref[:, lanes(t)], tracers, cells, tracers)
@@ -222,8 +228,7 @@
     pos_copy.wait()
 
     def dyn_copy(i):
-        rows_i = pl.ds(pl.multiple_of(i * cells * tracers, tracers), cells * tracers)
-        return pltpu.make_async_copy(dyn_ref.at[rows_i], dyn_hbm.at[rows_i], row_sems.at[i])
+        return pltpu.make_async_copy(dyn_ref.at[i], dyn_hbm.at[i], row_sems.at[i])
 
     def row(i, carry):
         diffuse_y = DIFFUSE * jnp.where(i == rows - 1, north_open, 1.0)
@@ -242,8 +247,7 @@
             flux_s = flux_y[j * tracers : (j + 1) * tracers, :]
             flux_y[j * tracers : (j + 1) * tracers, :] = flux_n
             dyn = (flux_w - flux_e) + (flux_s - flux_n)
-            column = i * cells + j
-            dyn_ref[pl.ds(pl.multiple_of(column * tracers, tracers), tracers), :] = dyn
+            dyn_ref[i, j * tracers : (j + 1) * tracers, :] = dyn
             send_ref[pos_s[i, j]] = (here + dyn).astype(jnp.bfloat16)
             here, flux_w = after, flux_e
         dyn_copy(i).start()
@@ -251,21 +255,26 @@
 
     lax.fori_loop(0, rows, row, 0)
 
+    send_copy = pltpu.make_async_copy(send_ref, send_hbm, sems.at[len(copies) + 2])
+    send_copy.start()
+    back_copy.wait()
+
     def drain(i, carry):
         dyn_copy(i).wait()
         return carry
 
     lax.fori_loop(0, rows, drain, 0)
-
-
-def turn_kernel(own_ref, pair_ref, out_ref):
-    owned = own_ref.shape[0]
-    for k in range(owned):
-        out_ref[k] = own_ref[k].T
-        out_ref[owned + k] = pair_ref[k].T
-
-
-def relax_kernel(x_ref, w_ref, y_ref, pos, pos_s, sem, slots):
+    send_copy.wait()
+
+
+def turn_kernel(*refs):
+    refs, out_ref = refs[:-1], refs[-1]
+    for n, ref in enumerate(refs):
+        for k in range(ref.shape[0]):
+            out_ref[n * ref.shape[0] + k] = ref[k].T
+
+
+def relax_kernel(lows, place_ref, x_ref, outer_ref, inner_ref, y_ref, pos, pos_s, sem, slots):
     tracers, levels = x_ref.shape[1:]
     peers, lanes = pos.shape
     stored = x_ref.shape[0] // peers
@@ -278,29 +287,43 @@
     copy.start()
     copy.wait()
 
-    def place(at):
+    def tile(at):
         return pl.ds(pl.multiple_of(at * tracers, tracers), tracers)
 
     def scatter(p, carry):
         for r in range(cap):
-            slots[place(pos_s[p, r]), :] = x_ref[p * stored + r].astype(f32)
+            slots[tile(pos_s[p, r]), :] = x_ref[p * stored + r].astype(f32)
         return carry
 
     lax.fori_loop(0, peers, scatter, 0)
     block = SLOTS * tracers
 
-    def span(k, carry):
-        at = pl.ds(pl.multiple_of(k * block, block), block)
-        x = slots[at, :]
-        y = jnp.dot(x.astype(jnp.bfloat16), w_ref[k], preferred_element_type=f32)
-        slots[at, :] = y - x
-        return carry
-
-    lax.fori_loop(0, w_ref.shape[0], span, 0, unroll=8)
+    def relax(first, count, w_ref, w_first):
+        def span(k, carry):
+            at = pl.ds(pl.multiple_of((first + k) * block, block), block)
+            x = slots[at, :]
+            y = jnp.dot(x.astype(jnp.bfloat16), w_ref[w_first + k], preferred_element_type=f32)
+            slots[at, :] = y - x
+            return carry
+
+        lax.fori_loop(0, count, span, 0, unroll=8)
+
+    owned = inner_ref.shape[0]
+    place = place_ref[0]
+    is_outer = ((place >> log2(lows)) & 1) == ((place >> (log2(lows) - 1)) & 1)
+    relax(0, owned, outer_ref, 0)
+
+    @pl.when(is_outer)
+    def _():
+        relax(owned, owned, outer_ref, owned)
+
+    @pl.when(jnp.logical_not(is_outer))
+    def _():
+        relax(owned, owned, inner_ref, 0)
 
     def gather(p, carry):
         for r in range(cap):
-            y_ref[p * cap + r] = slots[place(pos_s[p, r]), :].astype(jnp.bfloat16)
+            y_ref[p * cap + r] = slots[tile(pos_s[p, r]), :].astype(jnp.bfloat16)
         return carry
 
     lax.fori_loop(0, peers, gather, 0)
@@ -315,22 +338,16 @@
 
     def row(i, carry):
         for j in range(cells):
-            at = pl.multiple_of((i * cells + j) * tracers, tracers)
-            total[j * tracers : (j + 1) * tracers, :] = dyn_ref[pl.ds(at, tracers), :] + y_ref[
-                pos_ref[i, j]
-            ].astype(jnp.float32)
+            tile = slice(j * tracers, (j + 1) * tracers)
+            total[tile, :] = dyn_ref[i, tile, :] + y_ref[pos_ref[i, j]].astype(jnp.float32)
         for t in range(tracers):
             out[i, :, t * levels : (t + 1) * levels] = total[pl.ds(t, cells, stride=tracers), :]
         copy(i).start()
         return carry
 
     lax.fori_loop(0, rows, row, 0)
-
-    def drain(i, carry):
+    for i in range(rows):
         copy(i).wait()
-        return carry
-
-    lax.fori_loop(0, rows, drain, 0)
 
 
 def in_pairs(x, axis, first):
@@ -368,35 +385,49 @@
             pltpu.VMEM((rows, width + levels), f32),
             dma((8,)),
         ],
-        compiler_params=params(62),
+        compiler_params=params(64),
         name="edges",
     )(place, tracers, east_wind, north_wind)
-    lon_a, lon_b = in_pairs(lon_a, LON_AXES, 0), in_pairs(lon_b, LON_AXES, 1)
-    lat_a, lat_b = in_pairs(lat_a, "lat", 0), in_pairs(lat_b, "lat", 1)
-    matrices, lon_a, lon_b = lax.optimization_barrier((inverses, lon_a, lon_b))
-    pair = lax.ppermute(matrices, "hi", [(0, 1), (1, 0)])
-
+    far_edges = (
+        in_pairs(lon_a, LON_AXES, 0),
+        in_pairs(lon_b, LON_AXES, 1),
+        in_pairs(lat_a, "lat", 0),
+        in_pairs(lat_b, "lat", 1),
+    )
+
+    def opposite(start, stop):
+        pairs = [(lo, lows + (lo ^ lows // 2)) for lo in range(start, stop)]
+        return pairs + [(b, a) for a, b in pairs]
+
+    outer = lax.ppermute(inverses, LON_AXES, opposite(0, lows // 2))
+    cost = lambda us: pl.CostEstimate(
+        flops=us * 1_000_000_000, bytes_accessed=1 << 20, transcendentals=0
+    )
+    fields = (span_of, slot_of, tracers, east_wind, north_wind, *far_edges)
+    held = [(x.shape, x.dtype) for x in fields[:5]]
+    held += [((2,) + x.shape, x.dtype) for x in (lon_a, lat_a)]
     stride = (cells + 1 + 7) // 8 * 8
-    fields = (span_of, slot_of, tracers, east_wind, north_wind, lon_a, lon_b, lat_a, lat_b)
-    held = [(x.shape, x.dtype) for x in fields[:5]] + [((2,) + x.shape, x.dtype) for x in (lon_a, lat_a)]
-    cost = lambda us: pl.CostEstimate(flops=us * 1_000_000_000, bytes_accessed=1 << 20, transcendentals=0)
-    send, pos, dyn = pl.pallas_call(
+    dyn_shape = (rows, cells * kinds, levels)
+    send_shape = (peers * stored, kinds, levels)
+    send, back, dyn = pl.pallas_call(
         functools.partial(flux_kernel, cap, owned, lats, lons, lows),
         out_shape=(
-            jax.ShapeDtypeStruct((peers * stored, kinds, levels), bf16),
+            jax.ShapeDtypeStruct(send_shape, bf16),
             jax.ShapeDtypeStruct((rows, 128), i32),
-            jax.ShapeDtypeStruct((columns * kinds, levels), f32),
+            jax.ShapeDtypeStruct(dyn_shape, f32),
         ),
         in_specs=[SMEM] + [ANY] * 9,
-        out_specs=(VMEM, VMEM, ANY),
+        out_specs=(ANY,) * 3,
         scratch_shapes=[pltpu.VMEM(*x) for x in held]
         + [
-            dma((10,)),
+            dma((12,)),
             dma((rows,)),
             pltpu.VMEM((rows * peers, cells), f32),
             pltpu.VMEM((rows, 128), i32),
+            pltpu.VMEM((rows, 128), i32),
             pltpu.SMEM((rows, 128), i32),
-            pltpu.VMEM((columns * kinds, levels), f32),
+            pltpu.VMEM(send_shape, bf16),
+            pltpu.VMEM(dyn_shape, f32),
             pltpu.VMEM(((rows + 2) * (cells + 2) * kinds, levels), f32),
             pltpu.VMEM((stride + 8, levels), f32),
             pltpu.VMEM((rows * stride, levels), f32),
@@ -405,10 +436,13 @@
             pltpu.VMEM((2 * rows, levels), f32),
             pltpu.VMEM((cells * kinds, levels), f32),
         ],
-        compiler_params=params(62),
+        compiler_params=params(64),
         cost_estimate=cost(FLUX_COST),
         name="flux",
     )(place, *fields)
+
+    matrices, send = lax.optimization_barrier((inverses, send))
+    inner = lax.ppermute(matrices, LON_AXES, opposite(lows // 2, lows))
 
     def exchange(x):
         x = x.reshape(peers, -1, kinds, levels)
@@ -416,19 +450,21 @@
         return x.reshape(-1, kinds, levels)
 
     arrived = exchange(send)
-    turned = pl.pallas_call(
-        turn_kernel,
-        out_shape=jax.ShapeDtypeStruct((2 * owned, levels, levels), bf16),
-        in_specs=[VMEM] * 2,
-        out_specs=VMEM,
-        compiler_params=params(16),
-        cost_estimate=cost(TURN_COST),
-        name="turn",
-    )(inverses, pair)
+    def turned(us, *arrays):
+        return pl.pallas_call(
+            turn_kernel,
+            out_shape=jax.ShapeDtypeStruct((len(arrays) * owned, levels, levels), bf16),
+            in_specs=[VMEM] * len(arrays),
+            out_specs=VMEM,
+            compiler_params=params(16),
+            cost_estimate=cost(us),
+            name="turn",
+        )(*arrays)
+
     physics = pl.pallas_call(
-        relax_kernel,
+        functools.partial(relax_kernel, lows),
         out_shape=jax.ShapeDtypeStruct((peers * cap, kinds, levels), bf16),
-        in_specs=[VMEM] * 2,
+        in_specs=[SMEM] + [VMEM] * 3,
         out_specs=VMEM,
         scratch_shapes=[
             pltpu.VMEM((peers, 128), i32),
@@ -438,7 +474,7 @@
         ],
         compiler_params=params(24),
         name="relax",
-    )(arrived, turned)
+    )(place, arrived, turned(TURN_COST, inverses, outer), turned(INNER_COST, inner))
 
     returned = exchange(physics)
     return pl.pallas_call(
@@ -453,7 +489,7 @@
         ],
         compiler_params=params(16),
         name="finish",
-    )(pos, returned, dyn)
+    )(back, returned, dyn)
 
 
 def solution(mesh):

time: 86.9 us -> 77 us (0.89)
  waiting for transfers between devices: 29.5 us -> 20.8 us
  local copies, waits for them, and re-layouts: 3.13 us -> 0.02 us
  blocking collectives: 24.5 us -> 25.7 us
    ppermute x1 -> x2, waiting for transfers between devices: 11.1 us -> 3.86 us  [the longest x1 3.86 us: shards(): outer = lax.ppermute(inverses, LON_AXES, opposite(0, lows // 2))]
    unnamed x18 -> x6, local copies, waits for them, and re-layouts: 3.13 us -> 0.02 us
    ppermute x1 -> x2, starting transfers between devices: 0.51 us -> 3.04 us  [the longest x1 2.35 us: shards(): outer = lax.ppermute(inverses, LON_AXES, opposite(0, lows // 2))]
    ppermute x4, waiting for transfers between devices: 1.96 us -> 0.01 us  [in_pairs(): return lax.ppermute(x, axis, pairs + [(b, a) for a, b in pairs])]
    all_to_all x1, starting transfers between devices: 5.66 us -> 3.85 us  [exchange(): x = lax.all_to_all(x, GROUP_AXES, split_axis=0, concat_axis=0, tiled=True)]
    pallas_call x2 -> x3, Pallas kernels: 4.23 us -> 5.46 us  [the longest x1 3.92 us: shards(): pl.pallas_call(functools.partial(relax_kernel, lows), out_shape=jax.Shape...]
    all_to_all x1, blocking collectives: 24.5 us -> 25.7 us  [exchange(): x = lax.all_to_all(x, GROUP_AXES, split_axis=0, concat_axis=0, tiled=True)]
    pallas_call x1, Pallas kernels: 6.23 us -> 5.06 us  [shards(): pl.pallas_call(functools.partial(flux_kernel, cap, owned, lats, lons, low...]
  transfers between devices with their start and end apart: 6 -> 7, of which waited for: 3 -> 2; matrix products, arithmetic and copies ran while one was open for 0% -> 0% of each run, Pallas kernels for 8% -> 9%
where the time goes in v6:
time: 77 us; the launch traced here: 76.7 us
  blocking collectives  25.7 us (33%)
  waiting for transfers between devices  20.8 us (27%)
  starting transfers between devices  15.1 us (20%)
  Pallas kernels  14.9 us (19%)
    all_to_all x1, blocking collectives, exchange(): x = lax.all_to_all(x, GROUP_AXES, split_axis=0, concat_axis=0, tiled=True)  25.7 us
    all_to_all x1, waiting for transfers between devices, exchange(): x = lax.all_to_all(x, GROUP_AXES, split_axis=0, concat_axis=0, tiled=True)  16.9 us
    ppermute x4, starting transfers between devices, in_pairs(): return lax.ppermute(x, axis, pairs + [(b, a) for a, b in pairs])  8.21 us
    pallas_call x1, Pallas kernels, shards(): pl.pallas_call(functools.partial(flux_kernel, cap, owned, lats, lons, low...  5.06 us
    pallas_call x1, Pallas kernels, shards(): pl.pallas_call(functools.partial(relax_kernel, lows), out_shape=jax.Shape...  3.92 us
    ppermute x1, waiting for transfers between devices, shards(): outer = lax.ppermute(inverses, LON_AXES, opposite(0, lows // 2))  3.86 us
    all_to_all x1, starting transfers between devices, exchange(): x = lax.all_to_all(x, GROUP_AXES, split_axis=0, concat_axis=0, tiled=True)  3.85 us
    pallas_call x1, Pallas kernels, shards(): pl.pallas_call(finish_kernel, out_shape=jax.ShapeDtypeStruct((rows, cells...  2.39 us
  transfers between devices with their start and end apart: 7, of which 2 were waited for; matrix products, arithmetic and copies ran while one was open for 0% of the time, Pallas kernels for 9%

profile of v6, /device:TPU:0, one launch (start us, length us, event | category | flops | bytes accessed | tf_op | source)
XLA Modules:
  0.0 76.7 jit_solution(15568031819602051766)
XLA Ops:
  0.0 2.0 %edges.1 = (bf16[16,1152]{1,0:T(8,128)(2,1)}, bf16[16,1152]{1,0:T(8,128)(2,1)}, bf16[32,1152]{1,0:T(8,128)(2,1)}, bf16[32,1152]{1,0:T(8,128)(2,1)}) custom-call(s32[1]{0:T(128)} %bitcast.place_ref, bf16[16,32,1024]{2,1,0:T(8,128)(2,1)} %refs_2_.1, bf16[16,32,128]{2,1,0:T(8,128)(2,1)} %refs_3_.1, bf16[16,32,128]{2,1,0:T(8,128)(2,1)} %refs_4_.1), custom_call_target="tpu_custom_call" | custom-call | tf_op jit(solution)/shard_map/edges/pallas_call | solution.py:376
  2.0 3.0 %collective-permute-start.2 = (bf16[32,1152]{1,0:T(8,128)(2,1)}, bf16[32,1152]{1,0:T(8,128)(2,1)}, u32[]{:S(2)}, u32[]{:S(2)}) collective-permute-start(bf16[32,1152]{1,0:T(8,128)(2,1)} %get-tuple-element.16), channel_id=1, source_target_pairs={{0,8},{16,24},{8,0},{24,16},{1,9},{17,25},{9,1},{25,17},{2,10},{18... | collective-permute-start | bytes 221192 | tf_op jit(solution)/shard_map/ppermute | solution.py:356
  5.0 1.5 %collective-permute-start.3 = (bf16[32,1152]{1,0:T(8,128)(2,1)}, bf16[32,1152]{1,0:T(8,128)(2,1)}, u32[]{:S(2)}, u32[]{:S(2)}) collective-permute-start(bf16[32,1152]{1,0:T(8,128)(2,1)} %get-tuple-element.17), channel_id=1, source_target_pairs={{8,16},{24,0},{16,8},{0,24},{9,17},{25,1},{17,9},{1,25},{10,18},{2... | collective-permute-start | bytes 221192 | tf_op jit(solution)/shard_map/ppermute | solution.py:356
  6.5 0.0 collective-permute-start
  6.5 3.7 %collective-permute-start.1 = (bf16[16,1152]{1,0:T(8,128)(2,1)}, bf16[16,1152]{1,0:T(8,128)(2,1)}, u32[]{:S(2)}, u32[]{:S(2)}) collective-permute-start(bf16[16,1152]{1,0:T(8,128)(2,1)} %get-tuple-element.15), channel_id=1, source_target_pairs={{1,2},{3,4},{5,6},{7,0},{2,1},{4,3},{6,5},{0,7},{9,10},{11,12},{13... | collective-permute-start | bytes 110600 | tf_op jit(solution)/shard_map/ppermute | solution.py:356
  10.2 2.3 %collective-permute-start.4 = (bf16[16,128,128]{2,1,0:T(8,128)(2,1)}, bf16[16,128,128]{2,1,0:T(8,128)(2,1)}, u32[]{:S(2)}, u32[]{:S(2)}) collective-permute-start(bf16[16,128,128]{2,1,0:T(8,128)(2,1)} %refs_0_.3), channel_id=1, source_target_pairs={{0,6},{1,7},{6,0},{7,1},{8,14},{9,15},{14,8},{15,9},{16,22},{17,23... | collective-permute-start | bytes 1572872 | tf_op jit(solution)/shard_map/ppermute | solution.py:402
  12.6 0.0 collective-permute-done.refs_5_
  12.6 0.0 collective-permute-done.1.refs_6_
  12.6 0.0 collective-permute-done.2.refs_7_
  12.6 0.0 collective-permute-done.3.refs_8_
  12.6 5.1 %flux.1 = (bf16[784,8,128]{2,1,0:T(8,128)(2,1)}, s32[16,128]{1,0:T(8,128)}, f32[16,256,128]{2,1,0:T(8,128)}) custom-call(s32[1]{0:T(128)} %bitcast.place_ref, s32[16,32]{1,0:T(8,128)} %refs_0_.2, s32[16,32]{1,0:T(8,128)} %refs_1_.1, bf16[16,32,1024]{2,1,0:T(8,128)(2,1)} %refs_2_.1, bf16[16,32,128]{2,1,0:T(8,128)(2,1)} %refs_3_.1, ...), custom_call_target="tpu_custom_call" | custom-call | flops 10000000000 | bytes 1048576 | tf_op jit(solution)/shard_map/flux/pallas_call | solution.py:412
  17.7 0.0 copy-start.2
  17.7 3.9 %all-to-all-start = ((bf16[16,49,8,128]{3,2,1,0:T(8,128)(2,1)}), bf16[16,49,8,128]{3,2,1,0:T(8,128)(2,1)S(1)}, u32[]{:S(2)}, u32[]{:S(2)}) async-start(bf16[16,49,8,128]{3,2,1,0:T(8,128)(2,1)} %bitcast.8), calls=%async_computation | async-start | bytes 3211264 | tf_op jit(solution)/shard_map/all_to_all | solution.py:449
  21.5 0.0 copy-done.2
  21.6 0.7 collective-permute-start.5
  22.3 3.9 %collective-permute-done.4.refs_1_ = bf16[16,128,128]{2,1,0:T(8,128)(2,1)} collective-permute-done((bf16[16,128,128]{2,1,0:T(8,128)(2,1)}, bf16[16,128,128]{2,1,0:T(8,128)(2,1)}, u32[]{:S(2)}, u32[]{:S(2)}) %collective-permute-start.4) | collective-permute-done | bytes 524320 | tf_op jit(solution)/shard_map/ppermute | solution.py:402
  26.1 1.4 %turn.2.outer_ref = bf16[32,128,128]{2,1,0:T(8,128)(2,1)S(1)} custom-call(bf16[16,128,128]{2,1,0:T(8,128)(2,1)S(1)} %copy-done.2, bf16[16,128,128]{2,1,0:T(8,128)(2,1)} %collective-permute-done.4.refs_1_), custom_call_target="tpu_custom_call" | custom-call | flops 30000001024 | bytes 1048576 | tf_op jit(solution)/shard_map/turn/pallas_call | solution.py:454
  27.5 0.0 collective-permute-done.5.refs_0_
  27.5 0.2 turn.3.inner_ref
  27.7 16.9 %all-to-all-done = bf16[16,49,8,128]{3,2,1,0:T(8,128)(2,1)S(1)} async-done(((bf16[16,49,8,128]{3,2,1,0:T(8,128)(2,1)}), bf16[16,49,8,128]{3,2,1,0:T(8,128)(2,1)S(1)}, u32[]{:S(2)}, u32[]{:S(2)}) %all-to-all-start) | async-done | bytes 1605664 | tf_op jit(solution)/shard_map/all_to_all | solution.py:449
  44.6 3.9 %relax.1 = bf16[768,8,128]{2,1,0:T(8,128)(2,1)S(1)} custom-call(s32[1]{0:T(128)} %bitcast.place_ref, bf16[784,8,128]{2,1,0:T(8,128)(2,1)S(1)} %bitcast.5, bf16[32,128,128]{2,1,0:T(8,128)(2,1)S(1)} %turn.2.outer_ref, bf16[16,128,128]{2,1,0:T(8,128)(2,1)S(1)} %turn.3.inner_ref), custom_call_target="tpu_custom_call" | custom-call | tf_op jit(solution)/shard_map/relax/pallas_call | solution.py:464
  48.5 0.0 copy-start
  48.5 0.0 copy-start.1
  48.5 25.7 %all_to_all.10 = bf16[16,48,8,128]{3,2,1,0:T(8,128)(2,1)S(1)} all-to-all(bf16[16,48,8,128]{3,2,1,0:T(8,128)(2,1)S(1)} %bitcast.6), channel_id=1, replica_groups=mesh['lat'=4,'hi'=2,'lo'=4] {'lat','lo'}, dimensions={0} | all-to-all | bytes 3145728 | tf_op jit(solution)/shard_map/all_to_all | solution.py:449
  74.3 0.0 copy-done
  74.3 0.0 copy-done.1
  74.3 2.4 %finish.1 = f32[16,32,1024]{2,1,0:T(8,128)} custom-call(s32[16,128]{1,0:T(8,128)S(1)} %copy-done.1, bf16[768,8,128]{2,1,0:T(8,128)(2,1)S(1)} %bitcast.7, f32[16,256,128]{2,1,0:T(8,128)S(1)} %copy-done), custom_call_target="tpu_custom_call" | custom-call | tf_op jit(solution)/shard_map/finish/pallas_call | solution.py:480
Async XLA Ops:
  2.0 10.6 %collective-permute-start.2 = (bf16[32,1152]{1,0:T(8,128)(2,1)}, bf16[32,1152]{1,0:T(8,128)(2,1)}, u32[]{:S(2)}, u32[]{:S(2)}) collective-permute-start(bf16[32,1152]{1,0:T(8,128)(2,1)} %get-tuple-element.16), channel_id=1, source_target_pairs={{0,8},{16,24},{8,0},{24,16},{1,9},{17,25},{9,1},{25,17},{2,10},{18... | collective-permute-start | bytes 221192 | tf_op jit(solution)/shard_map/ppermute | solution.py:356
  5.0 7.6 %collective-permute-start.3 = (bf16[32,1152]{1,0:T(8,128)(2,1)}, bf16[32,1152]{1,0:T(8,128)(2,1)}, u32[]{:S(2)}, u32[]{:S(2)}) collective-permute-start(bf16[32,1152]{1,0:T(8,128)(2,1)} %get-tuple-element.17), channel_id=1, source_target_pairs={{8,16},{24,0},{16,8},{0,24},{9,17},{25,1},{17,9},{1,25},{10,18},{2... | collective-permute-start | bytes 221192 | tf_op jit(solution)/shard_map/ppermute | solution.py:356
  6.5 6.1 %collective-permute-start = (bf16[16,1152]{1,0:T(8,128)(2,1)}, bf16[16,1152]{1,0:T(8,128)(2,1)}, u32[]{:S(2)}, u32[]{:S(2)}) collective-permute-start(bf16[16,1152]{1,0:T(8,128)(2,1)} %get-tuple-element.14), channel_id=1, source_target_pairs={{0,1},{2,3},{4,5},{6,7},{1,0},{3,2},{5,4},{7,6},{8,9},{10,11},{12,... | collective-permute-start | bytes 110600 | tf_op jit(solution)/shard_map/ppermute | solution.py:356
  6.5 6.1 %collective-permute-start.1 = (bf16[16,1152]{1,0:T(8,128)(2,1)}, bf16[16,1152]{1,0:T(8,128)(2,1)}, u32[]{:S(2)}, u32[]{:S(2)}) collective-permute-start(bf16[16,1152]{1,0:T(8,128)(2,1)} %get-tuple-element.15), channel_id=1, source_target_pairs={{1,2},{3,4},{5,6},{7,0},{2,1},{4,3},{6,5},{0,7},{9,10},{11,12},{13... | collective-permute-start | bytes 110600 | tf_op jit(solution)/shard_map/ppermute | solution.py:356
  10.2 15.9 %collective-permute-start.4 = (bf16[16,128,128]{2,1,0:T(8,128)(2,1)}, bf16[16,128,128]{2,1,0:T(8,128)(2,1)}, u32[]{:S(2)}, u32[]{:S(2)}) collective-permute-start(bf16[16,128,128]{2,1,0:T(8,128)(2,1)} %refs_0_.3), channel_id=1, source_target_pairs={{0,6},{1,7},{6,0},{7,1},{8,14},{9,15},{14,8},{15,9},{16,22},{17,23... | collective-permute-start | bytes 1572872 | tf_op jit(solution)/shard_map/ppermute | solution.py:402
  17.7 3.9 %copy-start.2 = (bf16[16,128,128]{2,1,0:T(8,128)(2,1)S(1)}, bf16[16,128,128]{2,1,0:T(8,128)(2,1)}, u32[]{:S(2)}) copy-start(bf16[16,128,128]{2,1,0:T(8,128)(2,1)} %refs_0_.3) | copy-start | bytes 1572868
  17.7 26.9 %all-to-all-start = ((bf16[16,49,8,128]{3,2,1,0:T(8,128)(2,1)}), bf16[16,49,8,128]{3,2,1,0:T(8,128)(2,1)S(1)}, u32[]{:S(2)}, u32[]{:S(2)}) async-start(bf16[16,49,8,128]{3,2,1,0:T(8,128)(2,1)} %bitcast.8), calls=%async_computation | async-start | bytes 3211264 | tf_op jit(solution)/shard_map/all_to_all | solution.py:449
  21.6 5.9 %collective-permute-start.5 = (bf16[16,128,128]{2,1,0:T(8,128)(2,1)S(1)}, bf16[16,128,128]{2,1,0:T(8,128)(2,1)S(1)}, u32[]{:S(2)}, u32[]{:S(2)}) collective-permute-start(bf16[16,128,128]{2,1,0:T(8,128)(2,1)S(1)} %copy-done.2), channel_id=1, source_target_pairs={{2,4},{3,5},{4,2},{5,3},{10,12},{11,13},{12,10},{13,11},{18,20},{1... | collective-permute-start | bytes 1572872 | tf_op jit(solution)/shard_map/ppermute | solution.py:445
  48.5 25.8 %copy-start = (f32[16,256,128]{2,1,0:T(8,128)S(1)}, f32[16,256,128]{2,1,0:T(8,128)}, u32[]{:S(2)}) copy-start(f32[16,256,128]{2,1,0:T(8,128)} %get-tuple-element.22.dyn_ref) | copy-start | bytes 6291460
  48.5 25.8 %copy-start.1 = (s32[16,128]{1,0:T(8,128)S(1)}, s32[16,128]{1,0:T(8,128)}, u32[]{:S(2)}) copy-start(s32[16,128]{1,0:T(8,128)} %get-tuple-element.18.pos_ref) | copy-start | bytes 24580

commit v7 on v6

--- a/solution.py
+++ b/solution.py
@@ -30,7 +30,7 @@
 
 
 def edge_kernel(
-    lons, place_ref, q_hbm, u_hbm, v_hbm, lon_a, lon_b, lat_a, lat_b, q_side, u_side, wide, sems
+    lons, place_ref, q_hbm, u_hbm, v_hbm, lon_a, lon_b, lat_a, lat_b, q_side, u_side, wide, ready, row, sems
 ):
     rows, cells, width = q_hbm.shape
     side = q_side.shape[2]
@@ -45,10 +45,14 @@
         near = pl.ds(pl.multiple_of(jnp.where(odd == 1, 0, cells - side), side), side)
         copy(q_hbm.at[:, near, :], q_side.at[n])
         copy(u_hbm.at[:, near, :], u_side.at[n])
-    for ref, odd in ((lat_a, odd_lat), (lat_b, 1 - odd_lat)):
+    for n, odd in enumerate((odd_lat, 1 - odd_lat)):
         i = jnp.where(odd == 1, 0, rows - 1)
-        copy(q_hbm.at[i], ref.at[:, 0:width])
-        copy(v_hbm.at[i], ref.at[:, width:])
+        copy(q_hbm.at[i], row.at[n, :, 0:width])
+        copy(v_hbm.at[i], row.at[n, :, width:])
+    for c in copies[4:]:
+        c.wait()
+    copy(row.at[0], lat_a)
+    copy(row.at[1], lat_b)
     for c in copies[:4]:
         c.wait()
     for n, (ref, odd) in enumerate(((lon_a, odd_lon), (lon_b, 1 - odd_lon))):
@@ -57,8 +61,9 @@
             q, u = q_side[n, i].astype(jnp.float32), u_side[n, i].astype(jnp.float32)
             wide[i : i + 1, 0:width] = jnp.where(first, q[0:1], q[side - 1 :])
             wide[i : i + 1, width:] = jnp.where(first, u[0:1], u[side - 1 :])
-        ref[...] = wide[...].astype(jnp.bfloat16)
-    for c in copies[4:]:
+        ready[n] = wide[...].astype(jnp.bfloat16)
+        copy(ready.at[n], ref)
+    for c in copies[8:]:
         c.wait()
 
 
@@ -295,7 +300,7 @@
             slots[tile(pos_s[p, r]), :] = x_ref[p * stored + r].astype(f32)
         return carry
 
-    lax.fori_loop(0, peers, scatter, 0)
+    lax.fori_loop(0, peers, scatter, 0, unroll=4)
     block = SLOTS * tracers
 
     def relax(first, count, w_ref, w_first):
@@ -306,7 +311,7 @@
             slots[at, :] = y - x
             return carry
 
-        lax.fori_loop(0, count, span, 0, unroll=8)
+        lax.fori_loop(0, count, span, 0, unroll=16)
 
     owned = inner_ref.shape[0]
     place = place_ref[0]
@@ -326,7 +331,7 @@
             y_ref[p * cap + r] = slots[tile(pos_s[p, r]), :].astype(jnp.bfloat16)
         return carry
 
-    lax.fori_loop(0, peers, gather, 0)
+    lax.fori_loop(0, peers, gather, 0, unroll=4)
 
 
 def finish_kernel(pos_ref, y_ref, dyn_ref, out_hbm, total, out, sems):
@@ -378,12 +383,14 @@
         out_shape=(jax.ShapeDtypeStruct((rows, width + levels), bf16),) * 2
         + (jax.ShapeDtypeStruct((cells, width + levels), bf16),) * 2,
         in_specs=[SMEM] + [ANY] * 3,
-        out_specs=(VMEM,) * 4,
+        out_specs=(ANY,) * 4,
         scratch_shapes=[
             pltpu.VMEM((2, rows, side, width), bf16),
             pltpu.VMEM((2, rows, side, levels), bf16),
             pltpu.VMEM((rows, width + levels), f32),
-            dma((8,)),
+            pltpu.VMEM((2, rows, width + levels), bf16),
+            pltpu.VMEM((2, cells, width + levels), bf16),
+            dma((12,)),
         ],
         compiler_params=params(64),
         name="edges",

time: 77 us -> 76.5 us (level)
  no operation moved by 1% of the time
where the time goes in v7:
time: 76.5 us; the launch traced here: 76.2 us
  blocking collectives  25.7 us (34%)
  waiting for transfers between devices  20.8 us (27%)
  starting transfers between devices  15.1 us (20%)
  Pallas kernels  14.4 us (19%)
    all_to_all x1, blocking collectives, exchange(): x = lax.all_to_all(x, GROUP_AXES, split_axis=0, concat_axis=0, tiled=True)  25.7 us
    all_to_all x1, waiting for transfers between devices, exchange(): x = lax.all_to_all(x, GROUP_AXES, split_axis=0, concat_axis=0, tiled=True)  16.9 us
    ppermute x4, starting transfers between devices, in_pairs(): return lax.ppermute(x, axis, pairs + [(b, a) for a, b in pairs])  8.21 us
    pallas_call x1, Pallas kernels, shards(): pl.pallas_call(functools.partial(flux_kernel, cap, owned, lats, lons, low...  5.06 us
    ppermute x1, waiting for transfers between devices, shards(): outer = lax.ppermute(inverses, LON_AXES, opposite(0, lows // 2))  3.86 us
    all_to_all x1, starting transfers between devices, exchange(): x = lax.all_to_all(x, GROUP_AXES, split_axis=0, concat_axis=0, tiled=True)  3.85 us
    pallas_call x1, Pallas kernels, shards(): pl.pallas_call(functools.partial(relax_kernel, lows), out_shape=jax.Shape...  3.44 us
    pallas_call x1, Pallas kernels, shards(): pl.pallas_call(finish_kernel, out_shape=jax.ShapeDtypeStruct((rows, cells...  2.39 us
  transfers between devices with their start and end apart: 7, of which 2 were waited for; matrix products, arithmetic and copies ran while one was open for 0% of the time, Pallas kernels for 9%

profile of v7, /device:TPU:0, one launch (start us, length us, event | category | flops | bytes accessed | tf_op | source)
XLA Modules:
  0.0 76.2 jit_solution(13032634412243110295)
XLA Ops:
  0.0 2.0 %edges.1 = (bf16[16,1152]{1,0:T(8,128)(2,1)}, bf16[16,1152]{1,0:T(8,128)(2,1)}, bf16[32,1152]{1,0:T(8,128)(2,1)}, bf16[32,1152]{1,0:T(8,128)(2,1)}) custom-call(s32[1]{0:T(128)} %bitcast.place_ref, bf16[16,32,1024]{2,1,0:T(8,128)(2,1)} %refs_2_.1, bf16[16,32,128]{2,1,0:T(8,128)(2,1)} %refs_3_.1, bf16[16,32,128]{2,1,0:T(8,128)(2,1)} %refs_4_.1), custom_call_target="tpu_custom_call" | custom-call | tf_op jit(solution)/shard_map/edges/pallas_call | solution.py:381
  2.0 3.0 %collective-permute-start.2 = (bf16[32,1152]{1,0:T(8,128)(2,1)}, bf16[32,1152]{1,0:T(8,128)(2,1)}, u32[]{:S(2)}, u32[]{:S(2)}) collective-permute-start(bf16[32,1152]{1,0:T(8,128)(2,1)} %get-tuple-element.16), channel_id=1, source_target_pairs={{0,8},{16,24},{8,0},{24,16},{1,9},{17,25},{9,1},{25,17},{2,10},{18... | collective-permute-start | bytes 221192 | tf_op jit(solution)/shard_map/ppermute | solution.py:361
  5.0 1.5 %collective-permute-start.3 = (bf16[32,1152]{1,0:T(8,128)(2,1)}, bf16[32,1152]{1,0:T(8,128)(2,1)}, u32[]{:S(2)}, u32[]{:S(2)}) collective-permute-start(bf16[32,1152]{1,0:T(8,128)(2,1)} %get-tuple-element.17), channel_id=1, source_target_pairs={{8,16},{24,0},{16,8},{0,24},{9,17},{25,1},{17,9},{1,25},{10,18},{2... | collective-permute-start | bytes 221192 | tf_op jit(solution)/shard_map/ppermute | solution.py:361
  6.5 0.0 collective-permute-start
  6.5 3.7 %collective-permute-start.1 = (bf16[16,1152]{1,0:T(8,128)(2,1)}, bf16[16,1152]{1,0:T(8,128)(2,1)}, u32[]{:S(2)}, u32[]{:S(2)}) collective-permute-start(bf16[16,1152]{1,0:T(8,128)(2,1)} %get-tuple-element.15), channel_id=1, source_target_pairs={{1,2},{3,4},{5,6},{7,0},{2,1},{4,3},{6,5},{0,7},{9,10},{11,12},{13... | collective-permute-start | bytes 110600 | tf_op jit(solution)/shard_map/ppermute | solution.py:361
  10.2 2.3 %collective-permute-start.4 = (bf16[16,128,128]{2,1,0:T(8,128)(2,1)}, bf16[16,128,128]{2,1,0:T(8,128)(2,1)}, u32[]{:S(2)}, u32[]{:S(2)}) collective-permute-start(bf16[16,128,128]{2,1,0:T(8,128)(2,1)} %refs_0_.3), channel_id=1, source_target_pairs={{0,6},{1,7},{6,0},{7,1},{8,14},{9,15},{14,8},{15,9},{16,22},{17,23... | collective-permute-start | bytes 1572872 | tf_op jit(solution)/shard_map/ppermute | solution.py:409
  12.5 0.0 collective-permute-done.refs_5_
  12.6 0.0 collective-permute-done.1.refs_6_
  12.6 0.0 collective-permute-done.2.refs_7_
  12.6 0.0 collective-permute-done.3.refs_8_
  12.6 5.1 %flux.1 = (bf16[784,8,128]{2,1,0:T(8,128)(2,1)}, s32[16,128]{1,0:T(8,128)}, f32[16,256,128]{2,1,0:T(8,128)}) custom-call(s32[1]{0:T(128)} %bitcast.place_ref, s32[16,32]{1,0:T(8,128)} %refs_0_.2, s32[16,32]{1,0:T(8,128)} %refs_1_.1, bf16[16,32,1024]{2,1,0:T(8,128)(2,1)} %refs_2_.1, bf16[16,32,128]{2,1,0:T(8,128)(2,1)} %refs_3_.1, ...), custom_call_target="tpu_custom_call" | custom-call | flops 10000000000 | bytes 1048576 | tf_op jit(solution)/shard_map/flux/pallas_call | solution.py:419
  17.7 0.0 copy-start.2
  17.7 3.9 %all-to-all-start = ((bf16[16,49,8,128]{3,2,1,0:T(8,128)(2,1)}), bf16[16,49,8,128]{3,2,1,0:T(8,128)(2,1)S(1)}, u32[]{:S(2)}, u32[]{:S(2)}) async-start(bf16[16,49,8,128]{3,2,1,0:T(8,128)(2,1)} %bitcast.8), calls=%async_computation | async-start | bytes 3211264 | tf_op jit(solution)/shard_map/all_to_all | solution.py:456
  21.5 0.0 copy-done.2
  21.5 0.7 collective-permute-start.5
  22.2 3.9 %collective-permute-done.4.refs_1_ = bf16[16,128,128]{2,1,0:T(8,128)(2,1)} collective-permute-done((bf16[16,128,128]{2,1,0:T(8,128)(2,1)}, bf16[16,128,128]{2,1,0:T(8,128)(2,1)}, u32[]{:S(2)}, u32[]{:S(2)}) %collective-permute-start.4) | collective-permute-done | bytes 524320 | tf_op jit(solution)/shard_map/ppermute | solution.py:409
  26.1 1.4 %turn.2.outer_ref = bf16[32,128,128]{2,1,0:T(8,128)(2,1)S(1)} custom-call(bf16[16,128,128]{2,1,0:T(8,128)(2,1)S(1)} %copy-done.2, bf16[16,128,128]{2,1,0:T(8,128)(2,1)} %collective-permute-done.4.refs_1_), custom_call_target="tpu_custom_call" | custom-call | flops 30000001024 | bytes 1048576 | tf_op jit(solution)/shard_map/turn/pallas_call | solution.py:461
  27.5 0.0 collective-permute-done.5.refs_0_
  27.5 0.2 turn.3.inner_ref
  27.7 16.9 %all-to-all-done = bf16[16,49,8,128]{3,2,1,0:T(8,128)(2,1)S(1)} async-done(((bf16[16,49,8,128]{3,2,1,0:T(8,128)(2,1)}), bf16[16,49,8,128]{3,2,1,0:T(8,128)(2,1)S(1)}, u32[]{:S(2)}, u32[]{:S(2)}) %all-to-all-start) | async-done | bytes 1605664 | tf_op jit(solution)/shard_map/all_to_all | solution.py:456
  44.6 3.4 %relax.1 = bf16[768,8,128]{2,1,0:T(8,128)(2,1)S(1)} custom-call(s32[1]{0:T(128)} %bitcast.place_ref, bf16[784,8,128]{2,1,0:T(8,128)(2,1)S(1)} %bitcast.5, bf16[32,128,128]{2,1,0:T(8,128)(2,1)S(1)} %turn.2.outer_ref, bf16[16,128,128]{2,1,0:T(8,128)(2,1)S(1)} %turn.3.inner_ref), custom_call_target="tpu_custom_call" | custom-call | tf_op jit(solution)/shard_map/relax/pallas_call | solution.py:471
  48.0 0.0 copy-start
  48.0 0.0 copy-start.1
  48.0 25.7 %all_to_all.10 = bf16[16,48,8,128]{3,2,1,0:T(8,128)(2,1)S(1)} all-to-all(bf16[16,48,8,128]{3,2,1,0:T(8,128)(2,1)S(1)} %bitcast.6), channel_id=1, replica_groups=mesh['lat'=4,'hi'=2,'lo'=4] {'lat','lo'}, dimensions={0} | all-to-all | bytes 3145728 | tf_op jit(solution)/shard_map/all_to_all | solution.py:456
  73.8 0.0 copy-done
  73.8 0.0 copy-done.1
  73.8 2.4 %finish.1 = f32[16,32,1024]{2,1,0:T(8,128)} custom-call(s32[16,128]{1,0:T(8,128)S(1)} %copy-done.1, bf16[768,8,128]{2,1,0:T(8,128)(2,1)S(1)} %bitcast.7, f32[16,256,128]{2,1,0:T(8,128)S(1)} %copy-done), custom_call_target="tpu_custom_call" | custom-call | tf_op jit(solution)/shard_map/finish/pallas_call | solution.py:487
Async XLA Ops:
  2.0 10.6 %collective-permute-start.2 = (bf16[32,1152]{1,0:T(8,128)(2,1)}, bf16[32,1152]{1,0:T(8,128)(2,1)}, u32[]{:S(2)}, u32[]{:S(2)}) collective-permute-start(bf16[32,1152]{1,0:T(8,128)(2,1)} %get-tuple-element.16), channel_id=1, source_target_pairs={{0,8},{16,24},{8,0},{24,16},{1,9},{17,25},{9,1},{25,17},{2,10},{18... | collective-permute-start | bytes 221192 | tf_op jit(solution)/shard_map/ppermute | solution.py:361
  5.0 7.6 %collective-permute-start.3 = (bf16[32,1152]{1,0:T(8,128)(2,1)}, bf16[32,1152]{1,0:T(8,128)(2,1)}, u32[]{:S(2)}, u32[]{:S(2)}) collective-permute-start(bf16[32,1152]{1,0:T(8,128)(2,1)} %get-tuple-element.17), channel_id=1, source_target_pairs={{8,16},{24,0},{16,8},{0,24},{9,17},{25,1},{17,9},{1,25},{10,18},{2... | collective-permute-start | bytes 221192 | tf_op jit(solution)/shard_map/ppermute | solution.py:361
  6.5 6.1 %collective-permute-start = (bf16[16,1152]{1,0:T(8,128)(2,1)}, bf16[16,1152]{1,0:T(8,128)(2,1)}, u32[]{:S(2)}, u32[]{:S(2)}) collective-permute-start(bf16[16,1152]{1,0:T(8,128)(2,1)} %get-tuple-element.14), channel_id=1, source_target_pairs={{0,1},{2,3},{4,5},{6,7},{1,0},{3,2},{5,4},{7,6},{8,9},{10,11},{12,... | collective-permute-start | bytes 110600 | tf_op jit(solution)/shard_map/ppermute | solution.py:361
  6.5 6.1 %collective-permute-start.1 = (bf16[16,1152]{1,0:T(8,128)(2,1)}, bf16[16,1152]{1,0:T(8,128)(2,1)}, u32[]{:S(2)}, u32[]{:S(2)}) collective-permute-start(bf16[16,1152]{1,0:T(8,128)(2,1)} %get-tuple-element.15), channel_id=1, source_target_pairs={{1,2},{3,4},{5,6},{7,0},{2,1},{4,3},{6,5},{0,7},{9,10},{11,12},{13... | collective-permute-start | bytes 110600 | tf_op jit(solution)/shard_map/ppermute | solution.py:361
  10.2 15.9 %collective-permute-start.4 = (bf16[16,128,128]{2,1,0:T(8,128)(2,1)}, bf16[16,128,128]{2,1,0:T(8,128)(2,1)}, u32[]{:S(2)}, u32[]{:S(2)}) collective-permute-start(bf16[16,128,128]{2,1,0:T(8,128)(2,1)} %refs_0_.3), channel_id=1, source_target_pairs={{0,6},{1,7},{6,0},{7,1},{8,14},{9,15},{14,8},{15,9},{16,22},{17,23... | collective-permute-start | bytes 1572872 | tf_op jit(solution)/shard_map/ppermute | solution.py:409
  17.7 3.9 %copy-start.2 = (bf16[16,128,128]{2,1,0:T(8,128)(2,1)S(1)}, bf16[16,128,128]{2,1,0:T(8,128)(2,1)}, u32[]{:S(2)}) copy-start(bf16[16,128,128]{2,1,0:T(8,128)(2,1)} %refs_0_.3) | copy-start | bytes 1572868
  17.7 26.9 %all-to-all-start = ((bf16[16,49,8,128]{3,2,1,0:T(8,128)(2,1)}), bf16[16,49,8,128]{3,2,1,0:T(8,128)(2,1)S(1)}, u32[]{:S(2)}, u32[]{:S(2)}) async-start(bf16[16,49,8,128]{3,2,1,0:T(8,128)(2,1)} %bitcast.8), calls=%async_computation | async-start | bytes 3211264 | tf_op jit(solution)/shard_map/all_to_all | solution.py:456
  21.5 5.9 %collective-permute-start.5 = (bf16[16,128,128]{2,1,0:T(8,128)(2,1)S(1)}, bf16[16,128,128]{2,1,0:T(8,128)(2,1)S(1)}, u32[]{:S(2)}, u32[]{:S(2)}) collective-permute-start(bf16[16,128,128]{2,1,0:T(8,128)(2,1)S(1)} %copy-done.2), channel_id=1, source_target_pairs={{2,4},{3,5},{4,2},{5,3},{10,12},{11,13},{12,10},{13,11},{18,20},{1... | collective-permute-start | bytes 1572872 | tf_op jit(solution)/shard_map/ppermute | solution.py:452
  48.0 25.8 %copy-start = (f32[16,256,128]{2,1,0:T(8,128)S(1)}, f32[16,256,128]{2,1,0:T(8,128)}, u32[]{:S(2)}) copy-start(f32[16,256,128]{2,1,0:T(8,128)} %get-tuple-element.22.dyn_ref) | copy-start | bytes 6291460
  48.0 25.7 %copy-start.1 = (s32[16,128]{1,0:T(8,128)S(1)}, s32[16,128]{1,0:T(8,128)}, u32[]{:S(2)}) copy-start(s32[16,128]{1,0:T(8,128)} %get-tuple-element.18.pos_ref) | copy-start | bytes 24580

commit v8 on v7

--- a/solution.py
+++ b/solution.py
@@ -300,7 +300,7 @@
             slots[tile(pos_s[p, r]), :] = x_ref[p * stored + r].astype(f32)
         return carry
 
-    lax.fori_loop(0, peers, scatter, 0, unroll=4)
+    lax.fori_loop(0, peers, scatter, 0, unroll=16)
     block = SLOTS * tracers
 
     def relax(first, count, w_ref, w_first):
@@ -331,7 +331,7 @@
             y_ref[p * cap + r] = slots[tile(pos_s[p, r]), :].astype(jnp.bfloat16)
         return carry
 
-    lax.fori_loop(0, peers, gather, 0, unroll=4)
+    lax.fori_loop(0, peers, gather, 0, unroll=16)
 
 
 def finish_kernel(pos_ref, y_ref, dyn_ref, out_hbm, total, out, sems):

time: 76.5 us -> 76.1 us (level)
  no operation moved by 1% of the time
where the time goes in v8:
time: 76.1 us; the launch traced here: 75.7 us
  blocking collectives  25.7 us (34%)
  waiting for transfers between devices  20.8 us (27%)
  starting transfers between devices  15.1 us (20%)
  Pallas kernels  14 us (18%)
    all_to_all x1, blocking collectives, exchange(): x = lax.all_to_all(x, GROUP_AXES, split_axis=0, concat_axis=0, tiled=True)  25.7 us
    all_to_all x1, waiting for transfers between devices, exchange(): x = lax.all_to_all(x, GROUP_AXES, split_axis=0, concat_axis=0, tiled=True)  16.9 us
    ppermute x4, starting transfers between devices, in_pairs(): return lax.ppermute(x, axis, pairs + [(b, a) for a, b in pairs])  8.21 us
    pallas_call x1, Pallas kernels, shards(): pl.pallas_call(functools.partial(flux_kernel, cap, owned, lats, lons, low...  5.06 us
    ppermute x1, waiting for transfers between devices, shards(): outer = lax.ppermute(inverses, LON_AXES, opposite(0, lows // 2))  3.86 us
    all_to_all x1, starting transfers between devices, exchange(): x = lax.all_to_all(x, GROUP_AXES, split_axis=0, concat_axis=0, tiled=True)  3.85 us
    pallas_call x1, Pallas kernels, shards(): pl.pallas_call(functools.partial(relax_kernel, lows), out_shape=jax.Shape...  3 us
    pallas_call x1, Pallas kernels, shards(): pl.pallas_call(finish_kernel, out_shape=jax.ShapeDtypeStruct((rows, cells...  2.4 us
  transfers between devices with their start and end apart: 7, of which 2 were waited for; matrix products, arithmetic and copies ran while one was open for 0% of the time, Pallas kernels for 9%

profile of v8, /device:TPU:0, one launch (start us, length us, event | category | flops | bytes accessed | tf_op | source)
XLA Modules:
  0.0 75.7 jit_solution(12134724956403607247)
XLA Ops:
  0.0 2.0 %edges.1 = (bf16[16,1152]{1,0:T(8,128)(2,1)}, bf16[16,1152]{1,0:T(8,128)(2,1)}, bf16[32,1152]{1,0:T(8,128)(2,1)}, bf16[32,1152]{1,0:T(8,128)(2,1)}) custom-call(s32[1]{0:T(128)} %bitcast.place_ref, bf16[16,32,1024]{2,1,0:T(8,128)(2,1)} %refs_2_.1, bf16[16,32,128]{2,1,0:T(8,128)(2,1)} %refs_3_.1, bf16[16,32,128]{2,1,0:T(8,128)(2,1)} %refs_4_.1), custom_call_target="tpu_custom_call" | custom-call | tf_op jit(solution)/shard_map/edges/pallas_call | solution.py:381
  2.0 3.0 %collective-permute-start.2 = (bf16[32,1152]{1,0:T(8,128)(2,1)}, bf16[32,1152]{1,0:T(8,128)(2,1)}, u32[]{:S(2)}, u32[]{:S(2)}) collective-permute-start(bf16[32,1152]{1,0:T(8,128)(2,1)} %get-tuple-element.16), channel_id=1, source_target_pairs={{0,8},{16,24},{8,0},{24,16},{1,9},{17,25},{9,1},{25,17},{2,10},{18... | collective-permute-start | bytes 221192 | tf_op jit(solution)/shard_map/ppermute | solution.py:361
  5.0 1.5 %collective-permute-start.3 = (bf16[32,1152]{1,0:T(8,128)(2,1)}, bf16[32,1152]{1,0:T(8,128)(2,1)}, u32[]{:S(2)}, u32[]{:S(2)}) collective-permute-start(bf16[32,1152]{1,0:T(8,128)(2,1)} %get-tuple-element.17), channel_id=1, source_target_pairs={{8,16},{24,0},{16,8},{0,24},{9,17},{25,1},{17,9},{1,25},{10,18},{2... | collective-permute-start | bytes 221192 | tf_op jit(solution)/shard_map/ppermute | solution.py:361
  6.5 0.0 collective-permute-start
  6.5 3.7 %collective-permute-start.1 = (bf16[16,1152]{1,0:T(8,128)(2,1)}, bf16[16,1152]{1,0:T(8,128)(2,1)}, u32[]{:S(2)}, u32[]{:S(2)}) collective-permute-start(bf16[16,1152]{1,0:T(8,128)(2,1)} %get-tuple-element.15), channel_id=1, source_target_pairs={{1,2},{3,4},{5,6},{7,0},{2,1},{4,3},{6,5},{0,7},{9,10},{11,12},{13... | collective-permute-start | bytes 110600 | tf_op jit(solution)/shard_map/ppermute | solution.py:361
  10.2 2.3 %collective-permute-start.4 = (bf16[16,128,128]{2,1,0:T(8,128)(2,1)}, bf16[16,128,128]{2,1,0:T(8,128)(2,1)}, u32[]{:S(2)}, u32[]{:S(2)}) collective-permute-start(bf16[16,128,128]{2,1,0:T(8,128)(2,1)} %refs_0_.3), channel_id=1, source_target_pairs={{0,6},{1,7},{6,0},{7,1},{8,14},{9,15},{14,8},{15,9},{16,22},{17,23... | collective-permute-start | bytes 1572872 | tf_op jit(solution)/shard_map/ppermute | solution.py:409
  12.5 0.0 collective-permute-done.refs_5_
  12.6 0.0 collective-permute-done.1.refs_6_
  12.6 0.0 collective-permute-done.2.refs_7_
  12.6 0.0 collective-permute-done.3.refs_8_
  12.6 5.1 %flux.1 = (bf16[784,8,128]{2,1,0:T(8,128)(2,1)}, s32[16,128]{1,0:T(8,128)}, f32[16,256,128]{2,1,0:T(8,128)}) custom-call(s32[1]{0:T(128)} %bitcast.place_ref, s32[16,32]{1,0:T(8,128)} %refs_0_.2, s32[16,32]{1,0:T(8,128)} %refs_1_.1, bf16[16,32,1024]{2,1,0:T(8,128)(2,1)} %refs_2_.1, bf16[16,32,128]{2,1,0:T(8,128)(2,1)} %refs_3_.1, ...), custom_call_target="tpu_custom_call" | custom-call | flops 10000000000 | bytes 1048576 | tf_op jit(solution)/shard_map/flux/pallas_call | solution.py:419
  17.7 0.0 copy-start.2
  17.7 3.9 %all-to-all-start = ((bf16[16,49,8,128]{3,2,1,0:T(8,128)(2,1)}), bf16[16,49,8,128]{3,2,1,0:T(8,128)(2,1)S(1)}, u32[]{:S(2)}, u32[]{:S(2)}) async-start(bf16[16,49,8,128]{3,2,1,0:T(8,128)(2,1)} %bitcast.8), calls=%async_computation | async-start | bytes 3211264 | tf_op jit(solution)/shard_map/all_to_all | solution.py:456
  21.5 0.0 copy-done.2
  21.5 0.7 collective-permute-start.5
  22.2 3.9 %collective-permute-done.4.refs_1_ = bf16[16,128,128]{2,1,0:T(8,128)(2,1)} collective-permute-done((bf16[16,128,128]{2,1,0:T(8,128)(2,1)}, bf16[16,128,128]{2,1,0:T(8,128)(2,1)}, u32[]{:S(2)}, u32[]{:S(2)}) %collective-permute-start.4) | collective-permute-done | bytes 524320 | tf_op jit(solution)/shard_map/ppermute | solution.py:409
  26.1 1.4 %turn.2.outer_ref = bf16[32,128,128]{2,1,0:T(8,128)(2,1)S(1)} custom-call(bf16[16,128,128]{2,1,0:T(8,128)(2,1)S(1)} %copy-done.2, bf16[16,128,128]{2,1,0:T(8,128)(2,1)} %collective-permute-done.4.refs_1_), custom_call_target="tpu_custom_call" | custom-call | flops 30000001024 | bytes 1048576 | tf_op jit(solution)/shard_map/turn/pallas_call | solution.py:461
  27.5 0.0 collective-permute-done.5.refs_0_
  27.5 0.2 turn.3.inner_ref
  27.7 16.9 %all-to-all-done = bf16[16,49,8,128]{3,2,1,0:T(8,128)(2,1)S(1)} async-done(((bf16[16,49,8,128]{3,2,1,0:T(8,128)(2,1)}), bf16[16,49,8,128]{3,2,1,0:T(8,128)(2,1)S(1)}, u32[]{:S(2)}, u32[]{:S(2)}) %all-to-all-start) | async-done | bytes 1605664 | tf_op jit(solution)/shard_map/all_to_all | solution.py:456
  44.6 3.0 %relax.1 = bf16[768,8,128]{2,1,0:T(8,128)(2,1)S(1)} custom-call(s32[1]{0:T(128)} %bitcast.place_ref, bf16[784,8,128]{2,1,0:T(8,128)(2,1)S(1)} %bitcast.5, bf16[32,128,128]{2,1,0:T(8,128)(2,1)S(1)} %turn.2.outer_ref, bf16[16,128,128]{2,1,0:T(8,128)(2,1)S(1)} %turn.3.inner_ref), custom_call_target="tpu_custom_call" | custom-call | tf_op jit(solution)/shard_map/relax/pallas_call | solution.py:471
  47.6 0.0 copy-start
  47.6 0.0 copy-start.1
  47.6 25.7 %all_to_all.10 = bf16[16,48,8,128]{3,2,1,0:T(8,128)(2,1)S(1)} all-to-all(bf16[16,48,8,128]{3,2,1,0:T(8,128)(2,1)S(1)} %bitcast.6), channel_id=1, replica_groups=mesh['lat'=4,'hi'=2,'lo'=4] {'lat','lo'}, dimensions={0} | all-to-all | bytes 3145728 | tf_op jit(solution)/shard_map/all_to_all | solution.py:456
  73.3 0.0 copy-done
  73.3 0.0 copy-done.1
  73.3 2.4 %finish.1 = f32[16,32,1024]{2,1,0:T(8,128)} custom-call(s32[16,128]{1,0:T(8,128)S(1)} %copy-done.1, bf16[768,8,128]{2,1,0:T(8,128)(2,1)S(1)} %bitcast.7, f32[16,256,128]{2,1,0:T(8,128)S(1)} %copy-done), custom_call_target="tpu_custom_call" | custom-call | tf_op jit(solution)/shard_map/finish/pallas_call | solution.py:487
Async XLA Ops:
  2.0 10.6 %collective-permute-start.2 = (bf16[32,1152]{1,0:T(8,128)(2,1)}, bf16[32,1152]{1,0:T(8,128)(2,1)}, u32[]{:S(2)}, u32[]{:S(2)}) collective-permute-start(bf16[32,1152]{1,0:T(8,128)(2,1)} %get-tuple-element.16), channel_id=1, source_target_pairs={{0,8},{16,24},{8,0},{24,16},{1,9},{17,25},{9,1},{25,17},{2,10},{18... | collective-permute-start | bytes 221192 | tf_op jit(solution)/shard_map/ppermute | solution.py:361
  5.0 7.6 %collective-permute-start.3 = (bf16[32,1152]{1,0:T(8,128)(2,1)}, bf16[32,1152]{1,0:T(8,128)(2,1)}, u32[]{:S(2)}, u32[]{:S(2)}) collective-permute-start(bf16[32,1152]{1,0:T(8,128)(2,1)} %get-tuple-element.17), channel_id=1, source_target_pairs={{8,16},{24,0},{16,8},{0,24},{9,17},{25,1},{17,9},{1,25},{10,18},{2... | collective-permute-start | bytes 221192 | tf_op jit(solution)/shard_map/ppermute | solution.py:361
  6.5 6.1 %collective-permute-start = (bf16[16,1152]{1,0:T(8,128)(2,1)}, bf16[16,1152]{1,0:T(8,128)(2,1)}, u32[]{:S(2)}, u32[]{:S(2)}) collective-permute-start(bf16[16,1152]{1,0:T(8,128)(2,1)} %get-tuple-element.14), channel_id=1, source_target_pairs={{0,1},{2,3},{4,5},{6,7},{1,0},{3,2},{5,4},{7,6},{8,9},{10,11},{12,... | collective-permute-start | bytes 110600 | tf_op jit(solution)/shard_map/ppermute | solution.py:361
  6.5 6.1 %collective-permute-start.1 = (bf16[16,1152]{1,0:T(8,128)(2,1)}, bf16[16,1152]{1,0:T(8,128)(2,1)}, u32[]{:S(2)}, u32[]{:S(2)}) collective-permute-start(bf16[16,1152]{1,0:T(8,128)(2,1)} %get-tuple-element.15), channel_id=1, source_target_pairs={{1,2},{3,4},{5,6},{7,0},{2,1},{4,3},{6,5},{0,7},{9,10},{11,12},{13... | collective-permute-start | bytes 110600 | tf_op jit(solution)/shard_map/ppermute | solution.py:361
  10.2 15.9 %collective-permute-start.4 = (bf16[16,128,128]{2,1,0:T(8,128)(2,1)}, bf16[16,128,128]{2,1,0:T(8,128)(2,1)}, u32[]{:S(2)}, u32[]{:S(2)}) collective-permute-start(bf16[16,128,128]{2,1,0:T(8,128)(2,1)} %refs_0_.3), channel_id=1, source_target_pairs={{0,6},{1,7},{6,0},{7,1},{8,14},{9,15},{14,8},{15,9},{16,22},{17,23... | collective-permute-start | bytes 1572872 | tf_op jit(solution)/shard_map/ppermute | solution.py:409
  17.7 3.9 %copy-start.2 = (bf16[16,128,128]{2,1,0:T(8,128)(2,1)S(1)}, bf16[16,128,128]{2,1,0:T(8,128)(2,1)}, u32[]{:S(2)}) copy-start(bf16[16,128,128]{2,1,0:T(8,128)(2,1)} %refs_0_.3) | copy-start | bytes 1572868
  17.7 26.9 %all-to-all-start = ((bf16[16,49,8,128]{3,2,1,0:T(8,128)(2,1)}), bf16[16,49,8,128]{3,2,1,0:T(8,128)(2,1)S(1)}, u32[]{:S(2)}, u32[]{:S(2)}) async-start(bf16[16,49,8,128]{3,2,1,0:T(8,128)(2,1)} %bitcast.8), calls=%async_computation | async-start | bytes 3211264 | tf_op jit(solution)/shard_map/all_to_all | solution.py:456
  21.5 5.9 %collective-permute-start.5 = (bf16[16,128,128]{2,1,0:T(8,128)(2,1)S(1)}, bf16[16,128,128]{2,1,0:T(8,128)(2,1)S(1)}, u32[]{:S(2)}, u32[]{:S(2)}) collective-permute-start(bf16[16,128,128]{2,1,0:T(8,128)(2,1)S(1)} %copy-done.2), channel_id=1, source_target_pairs={{2,4},{3,5},{4,2},{5,3},{10,12},{11,13},{12,10},{13,11},{18,20},{1... | collective-permute-start | bytes 1572872 | tf_op jit(solution)/shard_map/ppermute | solution.py:452
  47.6 25.8 %copy-start = (f32[16,256,128]{2,1,0:T(8,128)S(1)}, f32[16,256,128]{2,1,0:T(8,128)}, u32[]{:S(2)}) copy-start(f32[16,256,128]{2,1,0:T(8,128)} %get-tuple-element.22.dyn_ref) | copy-start | bytes 6291460
  47.6 25.7 %copy-start.1 = (s32[16,128]{1,0:T(8,128)S(1)}, s32[16,128]{1,0:T(8,128)}, u32[]{:S(2)}) copy-start(s32[16,128]{1,0:T(8,128)} %get-tuple-element.18.pos_ref) | copy-start | bytes 24580

commit v9 on v8

--- a/solution.py
+++ b/solution.py
@@ -185,7 +185,7 @@
         )
         return carry
 
-    lax.fori_loop(0, rows, relayout, 0)
+    lax.fori_loop(0, rows, relayout, 0, unroll=4)
     for copy in copies[3:]:
         copy.wait()
     spread(lambda t: south_ref[:, lanes(t)], tracers, cells, tracers)
@@ -206,7 +206,7 @@
         )
         return carry
 
-    lax.fori_loop(0, rows, faces, 0)
+    lax.fori_loop(0, rows, faces, 0, unroll=4)
     wind_y[0:cells, :] = south_ref[:, width:].astype(f32)
     wind_y[cells : (rows + 1) * cells, :] = v_ref[...].reshape(rows * cells, levels).astype(f32)
     wind_y[(rows + 1) * cells :, :] = north_ref[:, width:].astype(f32)
@@ -258,7 +258,7 @@
         dyn_copy(i).start()
         return carry
 
-    lax.fori_loop(0, rows, row, 0)
+    lax.fori_loop(0, rows, row, 0, unroll=2)
 
     send_copy = pltpu.make_async_copy(send_ref, send_hbm, sems.at[len(copies) + 2])
     send_copy.start()

time: 76.1 us -> 75.9 us (level)
  transfers between devices with their start and end apart: 7 -> 7, of which waited for: 2 -> 2; matrix products, arithmetic and copies ran while one was open for 0% -> 0% of each run, Pallas kernels for 9% -> 8%
where the time goes in v9:
time: 75.9 us; the launch traced here: 75.6 us
  blocking collectives  25.4 us (33%)
  waiting for transfers between devices  21.2 us (28%)
  starting transfers between devices  15.1 us (20%)
  Pallas kernels  13.8 us (18%)
    all_to_all x1, blocking collectives, exchange(): x = lax.all_to_all(x, GROUP_AXES, split_axis=0, concat_axis=0, tiled=True)  25.4 us
    all_to_all x1, waiting for transfers between devices, exchange(): x = lax.all_to_all(x, GROUP_AXES, split_axis=0, concat_axis=0, tiled=True)  17.1 us
    ppermute x4, starting transfers between devices, in_pairs(): return lax.ppermute(x, axis, pairs + [(b, a) for a, b in pairs])  8.21 us
    pallas_call x1, Pallas kernels, shards(): pl.pallas_call(functools.partial(flux_kernel, cap, owned, lats, lons, low...  4.84 us
    ppermute x1, waiting for transfers between devices, shards(): outer = lax.ppermute(inverses, LON_AXES, opposite(0, lows // 2))  4.07 us
    all_to_all x1, starting transfers between devices, exchange(): x = lax.all_to_all(x, GROUP_AXES, split_axis=0, concat_axis=0, tiled=True)  3.85 us
    pallas_call x1, Pallas kernels, shards(): pl.pallas_call(functools.partial(relax_kernel, lows), out_shape=jax.Shape...  3 us
    pallas_call x1, Pallas kernels, shards(): pl.pallas_call(finish_kernel, out_shape=jax.ShapeDtypeStruct((rows, cells...  2.39 us
  transfers between devices with their start and end apart: 7, of which 2 were waited for; matrix products, arithmetic and copies ran while one was open for 0% of the time, Pallas kernels for 8%

profile of v9, /device:TPU:0, one launch (start us, length us, event | category | flops | bytes accessed | tf_op | source)
XLA Modules:
  0.0 75.6 jit_solution(8830346371678152310)
XLA Ops:
  0.0 2.0 %edges.1 = (bf16[16,1152]{1,0:T(8,128)(2,1)}, bf16[16,1152]{1,0:T(8,128)(2,1)}, bf16[32,1152]{1,0:T(8,128)(2,1)}, bf16[32,1152]{1,0:T(8,128)(2,1)}) custom-call(s32[1]{0:T(128)} %bitcast.place_ref, bf16[16,32,1024]{2,1,0:T(8,128)(2,1)} %refs_2_.1, bf16[16,32,128]{2,1,0:T(8,128)(2,1)} %refs_3_.1, bf16[16,32,128]{2,1,0:T(8,128)(2,1)} %refs_4_.1), custom_call_target="tpu_custom_call" | custom-call | tf_op jit(solution)/shard_map/edges/pallas_call | solution.py:381
  2.0 3.0 %collective-permute-start.2 = (bf16[32,1152]{1,0:T(8,128)(2,1)}, bf16[32,1152]{1,0:T(8,128)(2,1)}, u32[]{:S(2)}, u32[]{:S(2)}) collective-permute-start(bf16[32,1152]{1,0:T(8,128)(2,1)} %get-tuple-element.16), channel_id=1, source_target_pairs={{0,8},{16,24},{8,0},{24,16},{1,9},{17,25},{9,1},{25,17},{2,10},{18... | collective-permute-start | bytes 221192 | tf_op jit(solution)/shard_map/ppermute | solution.py:361
  5.0 1.5 %collective-permute-start.3 = (bf16[32,1152]{1,0:T(8,128)(2,1)}, bf16[32,1152]{1,0:T(8,128)(2,1)}, u32[]{:S(2)}, u32[]{:S(2)}) collective-permute-start(bf16[32,1152]{1,0:T(8,128)(2,1)} %get-tuple-element.17), channel_id=1, source_target_pairs={{8,16},{24,0},{16,8},{0,24},{9,17},{25,1},{17,9},{1,25},{10,18},{2... | collective-permute-start | bytes 221192 | tf_op jit(solution)/shard_map/ppermute | solution.py:361
  6.5 0.0 collective-permute-start
  6.5 3.7 %collective-permute-start.1 = (bf16[16,1152]{1,0:T(8,128)(2,1)}, bf16[16,1152]{1,0:T(8,128)(2,1)}, u32[]{:S(2)}, u32[]{:S(2)}) collective-permute-start(bf16[16,1152]{1,0:T(8,128)(2,1)} %get-tuple-element.15), channel_id=1, source_target_pairs={{1,2},{3,4},{5,6},{7,0},{2,1},{4,3},{6,5},{0,7},{9,10},{11,12},{13... | collective-permute-start | bytes 110600 | tf_op jit(solution)/shard_map/ppermute | solution.py:361
  10.2 2.3 %collective-permute-start.4 = (bf16[16,128,128]{2,1,0:T(8,128)(2,1)}, bf16[16,128,128]{2,1,0:T(8,128)(2,1)}, u32[]{:S(2)}, u32[]{:S(2)}) collective-permute-start(bf16[16,128,128]{2,1,0:T(8,128)(2,1)} %refs_0_.3), channel_id=1, source_target_pairs={{0,6},{1,7},{6,0},{7,1},{8,14},{9,15},{14,8},{15,9},{16,22},{17,23... | collective-permute-start | bytes 1572872 | tf_op jit(solution)/shard_map/ppermute | solution.py:409
  12.5 0.0 collective-permute-done.refs_5_
  12.6 0.0 collective-permute-done.1.refs_6_
  12.6 0.0 collective-permute-done.2.refs_7_
  12.6 0.0 collective-permute-done.3.refs_8_
  12.6 4.8 %flux.1 = (bf16[784,8,128]{2,1,0:T(8,128)(2,1)}, s32[16,128]{1,0:T(8,128)}, f32[16,256,128]{2,1,0:T(8,128)}) custom-call(s32[1]{0:T(128)} %bitcast.place_ref, s32[16,32]{1,0:T(8,128)} %refs_0_.2, s32[16,32]{1,0:T(8,128)} %refs_1_.1, bf16[16,32,1024]{2,1,0:T(8,128)(2,1)} %refs_2_.1, bf16[16,32,128]{2,1,0:T(8,128)(2,1)} %refs_3_.1, ...), custom_call_target="tpu_custom_call" | custom-call | flops 10000000000 | bytes 1048576 | tf_op jit(solution)/shard_map/flux/pallas_call | solution.py:419
  17.4 0.0 copy-start.2
  17.5 3.9 %all-to-all-start = ((bf16[16,49,8,128]{3,2,1,0:T(8,128)(2,1)}), bf16[16,49,8,128]{3,2,1,0:T(8,128)(2,1)S(1)}, u32[]{:S(2)}, u32[]{:S(2)}) async-start(bf16[16,49,8,128]{3,2,1,0:T(8,128)(2,1)} %bitcast.8), calls=%async_computation | async-start | bytes 3211264 | tf_op jit(solution)/shard_map/all_to_all | solution.py:456
  21.3 0.0 copy-done.2
  21.3 0.7 collective-permute-start.5
  22.0 4.1 %collective-permute-done.4.refs_1_ = bf16[16,128,128]{2,1,0:T(8,128)(2,1)} collective-permute-done((bf16[16,128,128]{2,1,0:T(8,128)(2,1)}, bf16[16,128,128]{2,1,0:T(8,128)(2,1)}, u32[]{:S(2)}, u32[]{:S(2)}) %collective-permute-start.4) | collective-permute-done | bytes 524320 | tf_op jit(solution)/shard_map/ppermute | solution.py:409
  26.1 1.4 %turn.2.outer_ref = bf16[32,128,128]{2,1,0:T(8,128)(2,1)S(1)} custom-call(bf16[16,128,128]{2,1,0:T(8,128)(2,1)S(1)} %copy-done.2, bf16[16,128,128]{2,1,0:T(8,128)(2,1)} %collective-permute-done.4.refs_1_), custom_call_target="tpu_custom_call" | custom-call | flops 30000001024 | bytes 1048576 | tf_op jit(solution)/shard_map/turn/pallas_call | solution.py:461
  27.5 0.0 collective-permute-done.5.refs_0_
  27.5 0.2 turn.3.inner_ref
  27.7 17.1 %all-to-all-done = bf16[16,49,8,128]{3,2,1,0:T(8,128)(2,1)S(1)} async-done(((bf16[16,49,8,128]{3,2,1,0:T(8,128)(2,1)}), bf16[16,49,8,128]{3,2,1,0:T(8,128)(2,1)S(1)}, u32[]{:S(2)}, u32[]{:S(2)}) %all-to-all-start) | async-done | bytes 1605664 | tf_op jit(solution)/shard_map/all_to_all | solution.py:456
  44.8 3.0 %relax.1 = bf16[768,8,128]{2,1,0:T(8,128)(2,1)S(1)} custom-call(s32[1]{0:T(128)} %bitcast.place_ref, bf16[784,8,128]{2,1,0:T(8,128)(2,1)S(1)} %bitcast.5, bf16[32,128,128]{2,1,0:T(8,128)(2,1)S(1)} %turn.2.outer_ref, bf16[16,128,128]{2,1,0:T(8,128)(2,1)S(1)} %turn.3.inner_ref), custom_call_target="tpu_custom_call" | custom-call | tf_op jit(solution)/shard_map/relax/pallas_call | solution.py:471
  47.8 0.0 copy-start
  47.8 0.0 copy-start.1
  47.8 25.4 %all_to_all.10 = bf16[16,48,8,128]{3,2,1,0:T(8,128)(2,1)S(1)} all-to-all(bf16[16,48,8,128]{3,2,1,0:T(8,128)(2,1)S(1)} %bitcast.6), channel_id=1, replica_groups=mesh['lat'=4,'hi'=2,'lo'=4] {'lat','lo'}, dimensions={0} | all-to-all | bytes 3145728 | tf_op jit(solution)/shard_map/all_to_all | solution.py:456
  73.2 0.0 copy-done
  73.2 0.0 copy-done.1
  73.2 2.4 %finish.1 = f32[16,32,1024]{2,1,0:T(8,128)} custom-call(s32[16,128]{1,0:T(8,128)S(1)} %copy-done.1, bf16[768,8,128]{2,1,0:T(8,128)(2,1)S(1)} %bitcast.7, f32[16,256,128]{2,1,0:T(8,128)S(1)} %copy-done), custom_call_target="tpu_custom_call" | custom-call | tf_op jit(solution)/shard_map/finish/pallas_call | solution.py:487
Async XLA Ops:
  2.0 10.6 %collective-permute-start.2 = (bf16[32,1152]{1,0:T(8,128)(2,1)}, bf16[32,1152]{1,0:T(8,128)(2,1)}, u32[]{:S(2)}, u32[]{:S(2)}) collective-permute-start(bf16[32,1152]{1,0:T(8,128)(2,1)} %get-tuple-element.16), channel_id=1, source_target_pairs={{0,8},{16,24},{8,0},{24,16},{1,9},{17,25},{9,1},{25,17},{2,10},{18... | collective-permute-start | bytes 221192 | tf_op jit(solution)/shard_map/ppermute | solution.py:361
  5.0 7.6 %collective-permute-start.3 = (bf16[32,1152]{1,0:T(8,128)(2,1)}, bf16[32,1152]{1,0:T(8,128)(2,1)}, u32[]{:S(2)}, u32[]{:S(2)}) collective-permute-start(bf16[32,1152]{1,0:T(8,128)(2,1)} %get-tuple-element.17), channel_id=1, source_target_pairs={{8,16},{24,0},{16,8},{0,24},{9,17},{25,1},{17,9},{1,25},{10,18},{2... | collective-permute-start | bytes 221192 | tf_op jit(solution)/shard_map/ppermute | solution.py:361
  6.5 6.1 %collective-permute-start = (bf16[16,1152]{1,0:T(8,128)(2,1)}, bf16[16,1152]{1,0:T(8,128)(2,1)}, u32[]{:S(2)}, u32[]{:S(2)}) collective-permute-start(bf16[16,1152]{1,0:T(8,128)(2,1)} %get-tuple-element.14), channel_id=1, source_target_pairs={{0,1},{2,3},{4,5},{6,7},{1,0},{3,2},{5,4},{7,6},{8,9},{10,11},{12,... | collective-permute-start | bytes 110600 | tf_op jit(solution)/shard_map/ppermute | solution.py:361
  6.5 6.1 %collective-permute-start.1 = (bf16[16,1152]{1,0:T(8,128)(2,1)}, bf16[16,1152]{1,0:T(8,128)(2,1)}, u32[]{:S(2)}, u32[]{:S(2)}) collective-permute-start(bf16[16,1152]{1,0:T(8,128)(2,1)} %get-tuple-element.15), channel_id=1, source_target_pairs={{1,2},{3,4},{5,6},{7,0},{2,1},{4,3},{6,5},{0,7},{9,10},{11,12},{13... | collective-permute-start | bytes 110600 | tf_op jit(solution)/shard_map/ppermute | solution.py:361
  10.2 15.9 %collective-permute-start.4 = (bf16[16,128,128]{2,1,0:T(8,128)(2,1)}, bf16[16,128,128]{2,1,0:T(8,128)(2,1)}, u32[]{:S(2)}, u32[]{:S(2)}) collective-permute-start(bf16[16,128,128]{2,1,0:T(8,128)(2,1)} %refs_0_.3), channel_id=1, source_target_pairs={{0,6},{1,7},{6,0},{7,1},{8,14},{9,15},{14,8},{15,9},{16,22},{17,23... | collective-permute-start | bytes 1572872 | tf_op jit(solution)/shard_map/ppermute | solution.py:409
  17.4 3.9 %copy-start.2 = (bf16[16,128,128]{2,1,0:T(8,128)(2,1)S(1)}, bf16[16,128,128]{2,1,0:T(8,128)(2,1)}, u32[]{:S(2)}) copy-start(bf16[16,128,128]{2,1,0:T(8,128)(2,1)} %refs_0_.3) | copy-start | bytes 1572868
  17.5 27.3 %all-to-all-start = ((bf16[16,49,8,128]{3,2,1,0:T(8,128)(2,1)}), bf16[16,49,8,128]{3,2,1,0:T(8,128)(2,1)S(1)}, u32[]{:S(2)}, u32[]{:S(2)}) async-start(bf16[16,49,8,128]{3,2,1,0:T(8,128)(2,1)} %bitcast.8), calls=%async_computation | async-start | bytes 3211264 | tf_op jit(solution)/shard_map/all_to_all | solution.py:456
  21.3 6.1 %collective-permute-start.5 = (bf16[16,128,128]{2,1,0:T(8,128)(2,1)S(1)}, bf16[16,128,128]{2,1,0:T(8,128)(2,1)S(1)}, u32[]{:S(2)}, u32[]{:S(2)}) collective-permute-start(bf16[16,128,128]{2,1,0:T(8,128)(2,1)S(1)} %copy-done.2), channel_id=1, source_target_pairs={{2,4},{3,5},{4,2},{5,3},{10,12},{11,13},{12,10},{13,11},{18,20},{1... | collective-permute-start | bytes 1572872 | tf_op jit(solution)/shard_map/ppermute | solution.py:452
  47.8 25.4 %copy-start = (f32[16,256,128]{2,1,0:T(8,128)S(1)}, f32[16,256,128]{2,1,0:T(8,128)}, u32[]{:S(2)}) copy-start(f32[16,256,128]{2,1,0:T(8,128)} %get-tuple-element.22.dyn_ref) | copy-start | bytes 6291460
  47.8 25.4 %copy-start.1 = (s32[16,128]{1,0:T(8,128)S(1)}, s32[16,128]{1,0:T(8,128)}, u32[]{:S(2)}) copy-start(s32[16,128]{1,0:T(8,128)} %get-tuple-element.18.pos_ref) | copy-start | bytes 24580

commit v10 on v9

--- a/solution.py
+++ b/solution.py
@@ -272,14 +272,29 @@
     send_copy.wait()
 
 
-def turn_kernel(*refs):
-    refs, out_ref = refs[:-1], refs[-1]
-    for n, ref in enumerate(refs):
+def turn_kernel(own_ref, outer_ref, out_ref):
+    for n, ref in enumerate((own_ref, outer_ref)):
         for k in range(ref.shape[0]):
             out_ref[n * ref.shape[0] + k] = ref[k].T
 
 
-def relax_kernel(lows, place_ref, x_ref, outer_ref, inner_ref, y_ref, pos, pos_s, sem, slots):
+def inner_kernel(lows, place_ref, inner_ref, turned_ref, out_ref):
+    owned = inner_ref.shape[0]
+    place = place_ref[0]
+    is_outer = ((place >> log2(lows)) & 1) == ((place >> (log2(lows) - 1)) & 1)
+    out_ref[0:owned] = turned_ref[0:owned]
+
+    @pl.when(is_outer)
+    def _():
+        out_ref[owned:] = turned_ref[owned:]
+
+    @pl.when(jnp.logical_not(is_outer))
+    def _():
+        for k in range(owned):
+            out_ref[owned + k] = inner_ref[k].T
+
+
+def relax_kernel(x_ref, w_ref, y_ref, pos, pos_s, sem, slots):
     tracers, levels = x_ref.shape[1:]
     peers, lanes = pos.shape
     stored = x_ref.shape[0] // peers
@@ -303,28 +318,14 @@
     lax.fori_loop(0, peers, scatter, 0, unroll=16)
     block = SLOTS * tracers
 
-    def relax(first, count, w_ref, w_first):
-        def span(k, carry):
-            at = pl.ds(pl.multiple_of((first + k) * block, block), block)
-            x = slots[at, :]
-            y = jnp.dot(x.astype(jnp.bfloat16), w_ref[w_first + k], preferred_element_type=f32)
-            slots[at, :] = y - x
-            return carry
-
-        lax.fori_loop(0, count, span, 0, unroll=16)
-
-    owned = inner_ref.shape[0]
-    place = place_ref[0]
-    is_outer = ((place >> log2(lows)) & 1) == ((place >> (log2(lows) - 1)) & 1)
-    relax(0, owned, outer_ref, 0)
-
-    @pl.when(is_outer)
-    def _():
-        relax(owned, owned, outer_ref, owned)
-
-    @pl.when(jnp.logical_not(is_outer))
-    def _():
-        relax(owned, owned, inner_ref, 0)
+    def span(k, carry):
+        at = pl.ds(pl.multiple_of(k * block, block), block)
+        x = slots[at, :]
+        y = jnp.dot(x.astype(jnp.bfloat16), w_ref[k], preferred_element_type=f32)
+        slots[at, :] = y - x
+        return carry
+
+    lax.fori_loop(0, w_ref.shape[0], span, 0, unroll=32)
 
     def gather(p, carry):
         for r in range(cap):
@@ -350,7 +351,7 @@
         copy(i).start()
         return carry
 
-    lax.fori_loop(0, rows, row, 0)
+    lax.fori_loop(0, rows, row, 0, unroll=2)
     for i in range(rows):
         copy(i).wait()
 
@@ -457,21 +458,29 @@
         return x.reshape(-1, kinds, levels)
 
     arrived = exchange(send)
-    def turned(us, *arrays):
-        return pl.pallas_call(
-            turn_kernel,
-            out_shape=jax.ShapeDtypeStruct((len(arrays) * owned, levels, levels), bf16),
-            in_specs=[VMEM] * len(arrays),
-            out_specs=VMEM,
-            compiler_params=params(16),
-            cost_estimate=cost(us),
-            name="turn",
-        )(*arrays)
-
+    turned_shape = jax.ShapeDtypeStruct((2 * owned, levels, levels), bf16)
+    turned = pl.pallas_call(
+        turn_kernel,
+        out_shape=turned_shape,
+        in_specs=[VMEM] * 2,
+        out_specs=VMEM,
+        compiler_params=params(16),
+        cost_estimate=cost(TURN_COST),
+        name="turn",
+    )(inverses, outer)
+    turned = pl.pallas_call(
+        functools.partial(inner_kernel, lows),
+        out_shape=turned_shape,
+        in_specs=[SMEM] + [VMEM] * 2,
+        out_specs=VMEM,
+        compiler_params=params(16),
+        cost_estimate=cost(INNER_COST),
+        name="inner",
+    )(place, inner, turned)
     physics = pl.pallas_call(
-        functools.partial(relax_kernel, lows),
+        relax_kernel,
         out_shape=jax.ShapeDtypeStruct((peers * cap, kinds, levels), bf16),
-        in_specs=[SMEM] + [VMEM] * 3,
+        in_specs=[VMEM] * 2,
         out_specs=VMEM,
         scratch_shapes=[
             pltpu.VMEM((peers, 128), i32),
@@ -481,7 +490,7 @@
         ],
         compiler_params=params(24),
         name="relax",
-    )(place, arrived, turned(TURN_COST, inverses, outer), turned(INNER_COST, inner))
+    )(arrived, turned)
 
     returned = exchange(physics)
     return pl.pallas_call(

time: 75.9 us -> 75.8 us (level)
  no operation moved by 1% of the time
where the time goes in v10:
time: 75.8 us; the launch traced here: 75.4 us
  blocking collectives  25.4 us (34%)
  waiting for transfers between devices  21.3 us (28%)
  starting transfers between devices  15.1 us (20%)
  Pallas kernels  13.5 us (18%)
    all_to_all x1, blocking collectives, exchange(): x = lax.all_to_all(x, GROUP_AXES, split_axis=0, concat_axis=0, tiled=True)  25.4 us
    all_to_all x1, waiting for transfers between devices, exchange(): x = lax.all_to_all(x, GROUP_AXES, split_axis=0, concat_axis=0, tiled=True)  17.2 us
    ppermute x4, starting transfers between devices, in_pairs(): return lax.ppermute(x, axis, pairs + [(b, a) for a, b in pairs])  8.21 us
    pallas_call x1, Pallas kernels, shards(): pl.pallas_call(functools.partial(flux_kernel, cap, owned, lats, lons, low...  4.84 us
    ppermute x1, waiting for transfers between devices, shards(): outer = lax.ppermute(inverses, LON_AXES, opposite(0, lows // 2))  4.07 us
    all_to_all x1, starting transfers between devices, exchange(): x = lax.all_to_all(x, GROUP_AXES, split_axis=0, concat_axis=0, tiled=True)  3.85 us
    pallas_call x1, Pallas kernels, shards(): pl.pallas_call(relax_kernel, out_shape=jax.ShapeDtypeStruct((peers * cap,...  2.84 us
    pallas_call x1, Pallas kernels, shards(): pl.pallas_call(finish_kernel, out_shape=jax.ShapeDtypeStruct((rows, cells...  2.37 us
  transfers between devices with their start and end apart: 7, of which 2 were waited for; matrix products, arithmetic and copies ran while one was open for 0% of the time, Pallas kernels for 8%

profile of v10, /device:TPU:0, one launch (start us, length us, event | category | flops | bytes accessed | tf_op | source)
XLA Modules:
  0.0 75.4 jit_solution(9963614003637849023)
XLA Ops:
  0.0 2.0 %edges.1 = (bf16[16,1152]{1,0:T(8,128)(2,1)}, bf16[16,1152]{1,0:T(8,128)(2,1)}, bf16[32,1152]{1,0:T(8,128)(2,1)}, bf16[32,1152]{1,0:T(8,128)(2,1)}) custom-call(s32[1]{0:T(128)} %bitcast.place_ref, bf16[16,32,1024]{2,1,0:T(8,128)(2,1)} %refs_2_.1, bf16[16,32,128]{2,1,0:T(8,128)(2,1)} %refs_3_.1, bf16[16,32,128]{2,1,0:T(8,128)(2,1)} %refs_4_.1), custom_call_target="tpu_custom_call" | custom-call | tf_op jit(solution)/shard_map/edges/pallas_call | solution.py:382
  2.0 3.0 %collective-permute-start.2 = (bf16[32,1152]{1,0:T(8,128)(2,1)}, bf16[32,1152]{1,0:T(8,128)(2,1)}, u32[]{:S(2)}, u32[]{:S(2)}) collective-permute-start(bf16[32,1152]{1,0:T(8,128)(2,1)} %get-tuple-element.16), channel_id=1, source_target_pairs={{0,8},{16,24},{8,0},{24,16},{1,9},{17,25},{9,1},{25,17},{2,10},{18... | collective-permute-start | bytes 221192 | tf_op jit(solution)/shard_map/ppermute | solution.py:362
  5.0 1.5 %collective-permute-start.3 = (bf16[32,1152]{1,0:T(8,128)(2,1)}, bf16[32,1152]{1,0:T(8,128)(2,1)}, u32[]{:S(2)}, u32[]{:S(2)}) collective-permute-start(bf16[32,1152]{1,0:T(8,128)(2,1)} %get-tuple-element.17), channel_id=1, source_target_pairs={{8,16},{24,0},{16,8},{0,24},{9,17},{25,1},{17,9},{1,25},{10,18},{2... | collective-permute-start | bytes 221192 | tf_op jit(solution)/shard_map/ppermute | solution.py:362
  6.5 0.0 collective-permute-start
  6.5 3.7 %collective-permute-start.1 = (bf16[16,1152]{1,0:T(8,128)(2,1)}, bf16[16,1152]{1,0:T(8,128)(2,1)}, u32[]{:S(2)}, u32[]{:S(2)}) collective-permute-start(bf16[16,1152]{1,0:T(8,128)(2,1)} %get-tuple-element.15), channel_id=1, source_target_pairs={{1,2},{3,4},{5,6},{7,0},{2,1},{4,3},{6,5},{0,7},{9,10},{11,12},{13... | collective-permute-start | bytes 110600 | tf_op jit(solution)/shard_map/ppermute | solution.py:362
  10.2 2.3 %collective-permute-start.5 = (bf16[16,128,128]{2,1,0:T(8,128)(2,1)}, bf16[16,128,128]{2,1,0:T(8,128)(2,1)}, u32[]{:S(2)}, u32[]{:S(2)}) collective-permute-start(bf16[16,128,128]{2,1,0:T(8,128)(2,1)} %own_ref.1), channel_id=1, source_target_pairs={{0,6},{1,7},{6,0},{7,1},{8,14},{9,15},{14,8},{15,9},{16,22},{17,23... | collective-permute-start | bytes 1572872 | tf_op jit(solution)/shard_map/ppermute | solution.py:410
  12.5 0.0 collective-permute-done.refs_5_
  12.6 0.0 collective-permute-done.1.refs_6_
  12.6 0.0 collective-permute-done.2.refs_7_
  12.6 0.0 collective-permute-done.3.refs_8_
  12.6 4.8 %flux.1 = (bf16[784,8,128]{2,1,0:T(8,128)(2,1)}, s32[16,128]{1,0:T(8,128)}, f32[16,256,128]{2,1,0:T(8,128)}) custom-call(s32[1]{0:T(128)} %bitcast.place_ref, s32[16,32]{1,0:T(8,128)} %refs_0_.1, s32[16,32]{1,0:T(8,128)} %refs_1_.1, bf16[16,32,1024]{2,1,0:T(8,128)(2,1)} %refs_2_.1, bf16[16,32,128]{2,1,0:T(8,128)(2,1)} %refs_3_.1, ...), custom_call_target="tpu_custom_call" | custom-call | flops 10000000000 | bytes 1048576 | tf_op jit(solution)/shard_map/flux/pallas_call | solution.py:420
  17.4 0.0 copy-start.2
  17.5 3.9 %all-to-all-start = ((bf16[16,49,8,128]{3,2,1,0:T(8,128)(2,1)}), bf16[16,49,8,128]{3,2,1,0:T(8,128)(2,1)S(1)}, u32[]{:S(2)}, u32[]{:S(2)}) async-start(bf16[16,49,8,128]{3,2,1,0:T(8,128)(2,1)} %bitcast.8), calls=%async_computation | async-start | bytes 3211264 | tf_op jit(solution)/shard_map/all_to_all | solution.py:457
  21.3 0.0 copy-done.2
  21.3 0.7 collective-permute-start.4
  22.0 4.1 %collective-permute-done.5.outer_ref = bf16[16,128,128]{2,1,0:T(8,128)(2,1)} collective-permute-done((bf16[16,128,128]{2,1,0:T(8,128)(2,1)}, bf16[16,128,128]{2,1,0:T(8,128)(2,1)}, u32[]{:S(2)}, u32[]{:S(2)}) %collective-permute-start.5) | collective-permute-done | bytes 524320 | tf_op jit(solution)/shard_map/ppermute | solution.py:410
  26.1 1.4 %turn.1.turned_ref = bf16[32,128,128]{2,1,0:T(8,128)(2,1)S(1)} custom-call(bf16[16,128,128]{2,1,0:T(8,128)(2,1)S(1)} %copy-done.2, bf16[16,128,128]{2,1,0:T(8,128)(2,1)} %collective-permute-done.5.outer_ref), custom_call_target="tpu_custom_call" | custom-call | flops 30000001024 | bytes 1048576 | tf_op jit(solution)/shard_map/turn/pallas_call | solution.py:462
  27.5 0.0 collective-permute-done.4.inner_ref
  27.5 0.1 inner.1.w_ref
  27.6 17.2 %all-to-all-done = bf16[16,49,8,128]{3,2,1,0:T(8,128)(2,1)S(1)} async-done(((bf16[16,49,8,128]{3,2,1,0:T(8,128)(2,1)}), bf16[16,49,8,128]{3,2,1,0:T(8,128)(2,1)S(1)}, u32[]{:S(2)}, u32[]{:S(2)}) %all-to-all-start) | async-done | bytes 1605664 | tf_op jit(solution)/shard_map/all_to_all | solution.py:457
  44.8 2.8 %relax.1 = bf16[768,8,128]{2,1,0:T(8,128)(2,1)S(1)} custom-call(bf16[784,8,128]{2,1,0:T(8,128)(2,1)S(1)} %bitcast.5, bf16[32,128,128]{2,1,0:T(8,128)(2,1)S(1)} %inner.1.w_ref), custom_call_target="tpu_custom_call" | custom-call | tf_op jit(solution)/shard_map/relax/pallas_call | solution.py:480
  47.6 0.0 copy-start
  47.6 0.0 copy-start.1
  47.6 25.4 %all_to_all.10 = bf16[16,48,8,128]{3,2,1,0:T(8,128)(2,1)S(1)} all-to-all(bf16[16,48,8,128]{3,2,1,0:T(8,128)(2,1)S(1)} %bitcast.6), channel_id=1, replica_groups=mesh['lat'=4,'hi'=2,'lo'=4] {'lat','lo'}, dimensions={0} | all-to-all | bytes 3145728 | tf_op jit(solution)/shard_map/all_to_all | solution.py:457
  73.0 0.0 copy-done
  73.0 0.0 copy-done.1
  73.0 2.4 %finish.1 = f32[16,32,1024]{2,1,0:T(8,128)} custom-call(s32[16,128]{1,0:T(8,128)S(1)} %copy-done.1, bf16[768,8,128]{2,1,0:T(8,128)(2,1)S(1)} %bitcast.7, f32[16,256,128]{2,1,0:T(8,128)S(1)} %copy-done), custom_call_target="tpu_custom_call" | custom-call | tf_op jit(solution)/shard_map/finish/pallas_call | solution.py:496
Async XLA Ops:
  2.0 10.6 %collective-permute-start.2 = (bf16[32,1152]{1,0:T(8,128)(2,1)}, bf16[32,1152]{1,0:T(8,128)(2,1)}, u32[]{:S(2)}, u32[]{:S(2)}) collective-permute-start(bf16[32,1152]{1,0:T(8,128)(2,1)} %get-tuple-element.16), channel_id=1, source_target_pairs={{0,8},{16,24},{8,0},{24,16},{1,9},{17,25},{9,1},{25,17},{2,10},{18... | collective-permute-start | bytes 221192 | tf_op jit(solution)/shard_map/ppermute | solution.py:362
  5.0 7.6 %collective-permute-start.3 = (bf16[32,1152]{1,0:T(8,128)(2,1)}, bf16[32,1152]{1,0:T(8,128)(2,1)}, u32[]{:S(2)}, u32[]{:S(2)}) collective-permute-start(bf16[32,1152]{1,0:T(8,128)(2,1)} %get-tuple-element.17), channel_id=1, source_target_pairs={{8,16},{24,0},{16,8},{0,24},{9,17},{25,1},{17,9},{1,25},{10,18},{2... | collective-permute-start | bytes 221192 | tf_op jit(solution)/shard_map/ppermute | solution.py:362
  6.5 6.1 %collective-permute-start = (bf16[16,1152]{1,0:T(8,128)(2,1)}, bf16[16,1152]{1,0:T(8,128)(2,1)}, u32[]{:S(2)}, u32[]{:S(2)}) collective-permute-start(bf16[16,1152]{1,0:T(8,128)(2,1)} %get-tuple-element.14), channel_id=1, source_target_pairs={{0,1},{2,3},{4,5},{6,7},{1,0},{3,2},{5,4},{7,6},{8,9},{10,11},{12,... | collective-permute-start | bytes 110600 | tf_op jit(solution)/shard_map/ppermute | solution.py:362
  6.5 6.1 %collective-permute-start.1 = (bf16[16,1152]{1,0:T(8,128)(2,1)}, bf16[16,1152]{1,0:T(8,128)(2,1)}, u32[]{:S(2)}, u32[]{:S(2)}) collective-permute-start(bf16[16,1152]{1,0:T(8,128)(2,1)} %get-tuple-element.15), channel_id=1, source_target_pairs={{1,2},{3,4},{5,6},{7,0},{2,1},{4,3},{6,5},{0,7},{9,10},{11,12},{13... | collective-permute-start | bytes 110600 | tf_op jit(solution)/shard_map/ppermute | solution.py:362
  10.2 15.9 %collective-permute-start.5 = (bf16[16,128,128]{2,1,0:T(8,128)(2,1)}, bf16[16,128,128]{2,1,0:T(8,128)(2,1)}, u32[]{:S(2)}, u32[]{:S(2)}) collective-permute-start(bf16[16,128,128]{2,1,0:T(8,128)(2,1)} %own_ref.1), channel_id=1, source_target_pairs={{0,6},{1,7},{6,0},{7,1},{8,14},{9,15},{14,8},{15,9},{16,22},{17,23... | collective-permute-start | bytes 1572872 | tf_op jit(solution)/shard_map/ppermute | solution.py:410
  17.4 3.9 %copy-start.2 = (bf16[16,128,128]{2,1,0:T(8,128)(2,1)S(1)}, bf16[16,128,128]{2,1,0:T(8,128)(2,1)}, u32[]{:S(2)}) copy-start(bf16[16,128,128]{2,1,0:T(8,128)(2,1)} %own_ref.1) | copy-start | bytes 1572868
  17.5 27.3 %all-to-all-start = ((bf16[16,49,8,128]{3,2,1,0:T(8,128)(2,1)}), bf16[16,49,8,128]{3,2,1,0:T(8,128)(2,1)S(1)}, u32[]{:S(2)}, u32[]{:S(2)}) async-start(bf16[16,49,8,128]{3,2,1,0:T(8,128)(2,1)} %bitcast.8), calls=%async_computation | async-start | bytes 3211264 | tf_op jit(solution)/shard_map/all_to_all | solution.py:457
  21.3 6.1 %collective-permute-start.4 = (bf16[16,128,128]{2,1,0:T(8,128)(2,1)S(1)}, bf16[16,128,128]{2,1,0:T(8,128)(2,1)S(1)}, u32[]{:S(2)}, u32[]{:S(2)}) collective-permute-start(bf16[16,128,128]{2,1,0:T(8,128)(2,1)S(1)} %copy-done.2), channel_id=1, source_target_pairs={{2,4},{3,5},{4,2},{5,3},{10,12},{11,13},{12,10},{13,11},{18,20},{1... | collective-permute-start | bytes 1572872 | tf_op jit(solution)/shard_map/ppermute | solution.py:453
  47.6 25.4 %copy-start = (f32[16,256,128]{2,1,0:T(8,128)S(1)}, f32[16,256,128]{2,1,0:T(8,128)}, u32[]{:S(2)}) copy-start(f32[16,256,128]{2,1,0:T(8,128)} %get-tuple-element.22.dyn_ref) | copy-start | bytes 6291460
  47.6 25.4 %copy-start.1 = (s32[16,128]{1,0:T(8,128)S(1)}, s32[16,128]{1,0:T(8,128)}, u32[]{:S(2)}) copy-start(s32[16,128]{1,0:T(8,128)} %get-tuple-element.18.pos_ref) | copy-start | bytes 24580

commit v11 on v9

--- a/solution.py
+++ b/solution.py
@@ -185,7 +185,7 @@
         )
         return carry
 
-    lax.fori_loop(0, rows, relayout, 0, unroll=4)
+    lax.fori_loop(0, rows, relayout, 0, unroll=16)
     for copy in copies[3:]:
         copy.wait()
     spread(lambda t: south_ref[:, lanes(t)], tracers, cells, tracers)
@@ -206,7 +206,7 @@
         )
         return carry
 
-    lax.fori_loop(0, rows, faces, 0, unroll=4)
+    lax.fori_loop(0, rows, faces, 0, unroll=16)
     wind_y[0:cells, :] = south_ref[:, width:].astype(f32)
     wind_y[cells : (rows + 1) * cells, :] = v_ref[...].reshape(rows * cells, levels).astype(f32)
     wind_y[(rows + 1) * cells :, :] = north_ref[:, width:].astype(f32)

time: 75.9 us -> 75.9 us (level)
  no operation moved by 1% of the time
where the time goes in v11:
time: 75.9 us; the launch traced here: 75.6 us
  blocking collectives  25.3 us (33%)
  waiting for transfers between devices  21.3 us (28%)
  starting transfers between devices  15.1 us (20%)
  Pallas kernels  13.7 us (18%)
    all_to_all x1, blocking collectives, exchange(): x = lax.all_to_all(x, GROUP_AXES, split_axis=0, concat_axis=0, tiled=True)  25.3 us
    all_to_all x1, waiting for transfers between devices, exchange(): x = lax.all_to_all(x, GROUP_AXES, split_axis=0, concat_axis=0, tiled=True)  17.1 us
    ppermute x4, starting transfers between devices, in_pairs(): return lax.ppermute(x, axis, pairs + [(b, a) for a, b in pairs])  8.21 us
    pallas_call x1, Pallas kernels, shards(): pl.pallas_call(functools.partial(flux_kernel, cap, owned, lats, lons, low...  4.78 us
    ppermute x1, waiting for transfers between devices, shards(): outer = lax.ppermute(inverses, LON_AXES, opposite(0, lows // 2))  4.13 us
    all_to_all x1, starting transfers between devices, exchange(): x = lax.all_to_all(x, GROUP_AXES, split_axis=0, concat_axis=0, tiled=True)  3.85 us
    pallas_call x1, Pallas kernels, shards(): pl.pallas_call(functools.partial(relax_kernel, lows), out_shape=jax.Shape...  3 us
    pallas_call x1, Pallas kernels, shards(): pl.pallas_call(finish_kernel, out_shape=jax.ShapeDtypeStruct((rows, cells...  2.39 us
  transfers between devices with their start and end apart: 7, of which 2 were waited for; matrix products, arithmetic and copies ran while one was open for 0% of the time, Pallas kernels for 8%

profile of v11, /device:TPU:0, one launch (start us, length us, event | category | flops | bytes accessed | tf_op | source)
XLA Modules:
  0.0 75.6 jit_solution(1863547303838680421)
XLA Ops:
  0.0 2.0 %edges.1 = (bf16[16,1152]{1,0:T(8,128)(2,1)}, bf16[16,1152]{1,0:T(8,128)(2,1)}, bf16[32,1152]{1,0:T(8,128)(2,1)}, bf16[32,1152]{1,0:T(8,128)(2,1)}) custom-call(s32[1]{0:T(128)} %bitcast.place_ref, bf16[16,32,1024]{2,1,0:T(8,128)(2,1)} %refs_2_.1, bf16[16,32,128]{2,1,0:T(8,128)(2,1)} %refs_3_.1, bf16[16,32,128]{2,1,0:T(8,128)(2,1)} %refs_4_.1), custom_call_target="tpu_custom_call" | custom-call | tf_op jit(solution)/shard_map/edges/pallas_call | solution.py:381
  2.0 3.0 %collective-permute-start.2 = (bf16[32,1152]{1,0:T(8,128)(2,1)}, bf16[32,1152]{1,0:T(8,128)(2,1)}, u32[]{:S(2)}, u32[]{:S(2)}) collective-permute-start(bf16[32,1152]{1,0:T(8,128)(2,1)} %get-tuple-element.16), channel_id=1, source_target_pairs={{0,8},{16,24},{8,0},{24,16},{1,9},{17,25},{9,1},{25,17},{2,10},{18... | collective-permute-start | bytes 221192 | tf_op jit(solution)/shard_map/ppermute | solution.py:361
  5.0 1.5 %collective-permute-start.3 = (bf16[32,1152]{1,0:T(8,128)(2,1)}, bf16[32,1152]{1,0:T(8,128)(2,1)}, u32[]{:S(2)}, u32[]{:S(2)}) collective-permute-start(bf16[32,1152]{1,0:T(8,128)(2,1)} %get-tuple-element.17), channel_id=1, source_target_pairs={{8,16},{24,0},{16,8},{0,24},{9,17},{25,1},{17,9},{1,25},{10,18},{2... | collective-permute-start | bytes 221192 | tf_op jit(solution)/shard_map/ppermute | solution.py:361
  6.5 0.0 collective-permute-start
  6.5 3.7 %collective-permute-start.1 = (bf16[16,1152]{1,0:T(8,128)(2,1)}, bf16[16,1152]{1,0:T(8,128)(2,1)}, u32[]{:S(2)}, u32[]{:S(2)}) collective-permute-start(bf16[16,1152]{1,0:T(8,128)(2,1)} %get-tuple-element.15), channel_id=1, source_target_pairs={{1,2},{3,4},{5,6},{7,0},{2,1},{4,3},{6,5},{0,7},{9,10},{11,12},{13... | collective-permute-start | bytes 110600 | tf_op jit(solution)/shard_map/ppermute | solution.py:361
  10.2 2.3 %collective-permute-start.4 = (bf16[16,128,128]{2,1,0:T(8,128)(2,1)}, bf16[16,128,128]{2,1,0:T(8,128)(2,1)}, u32[]{:S(2)}, u32[]{:S(2)}) collective-permute-start(bf16[16,128,128]{2,1,0:T(8,128)(2,1)} %refs_0_.3), channel_id=1, source_target_pairs={{0,6},{1,7},{6,0},{7,1},{8,14},{9,15},{14,8},{15,9},{16,22},{17,23... | collective-permute-start | bytes 1572872 | tf_op jit(solution)/shard_map/ppermute | solution.py:409
  12.5 0.0 collective-permute-done.refs_5_
  12.6 0.0 collective-permute-done.1.refs_6_
  12.6 0.0 collective-permute-done.2.refs_7_
  12.6 0.0 collective-permute-done.3.refs_8_
  12.6 4.8 %flux.1 = (bf16[784,8,128]{2,1,0:T(8,128)(2,1)}, s32[16,128]{1,0:T(8,128)}, f32[16,256,128]{2,1,0:T(8,128)}) custom-call(s32[1]{0:T(128)} %bitcast.place_ref, s32[16,32]{1,0:T(8,128)} %refs_0_.2, s32[16,32]{1,0:T(8,128)} %refs_1_.1, bf16[16,32,1024]{2,1,0:T(8,128)(2,1)} %refs_2_.1, bf16[16,32,128]{2,1,0:T(8,128)(2,1)} %refs_3_.1, ...), custom_call_target="tpu_custom_call" | custom-call | flops 10000000000 | bytes 1048576 | tf_op jit(solution)/shard_map/flux/pallas_call | solution.py:419
  17.4 0.0 copy-start.2
  17.4 3.9 %all-to-all-start = ((bf16[16,49,8,128]{3,2,1,0:T(8,128)(2,1)}), bf16[16,49,8,128]{3,2,1,0:T(8,128)(2,1)S(1)}, u32[]{:S(2)}, u32[]{:S(2)}) async-start(bf16[16,49,8,128]{3,2,1,0:T(8,128)(2,1)} %bitcast.8), calls=%async_computation | async-start | bytes 3211264 | tf_op jit(solution)/shard_map/all_to_all | solution.py:456
  21.3 0.0 copy-done.2
  21.3 0.7 collective-permute-start.5
  22.0 4.1 %collective-permute-done.4.refs_1_ = bf16[16,128,128]{2,1,0:T(8,128)(2,1)} collective-permute-done((bf16[16,128,128]{2,1,0:T(8,128)(2,1)}, bf16[16,128,128]{2,1,0:T(8,128)(2,1)}, u32[]{:S(2)}, u32[]{:S(2)}) %collective-permute-start.4) | collective-permute-done | bytes 524320 | tf_op jit(solution)/shard_map/ppermute | solution.py:409
  26.1 1.4 %turn.2.outer_ref = bf16[32,128,128]{2,1,0:T(8,128)(2,1)S(1)} custom-call(bf16[16,128,128]{2,1,0:T(8,128)(2,1)S(1)} %copy-done.2, bf16[16,128,128]{2,1,0:T(8,128)(2,1)} %collective-permute-done.4.refs_1_), custom_call_target="tpu_custom_call" | custom-call | flops 30000001024 | bytes 1048576 | tf_op jit(solution)/shard_map/turn/pallas_call | solution.py:461
  27.5 0.0 collective-permute-done.5.refs_0_
  27.5 0.2 turn.3.inner_ref
  27.7 17.1 %all-to-all-done = bf16[16,49,8,128]{3,2,1,0:T(8,128)(2,1)S(1)} async-done(((bf16[16,49,8,128]{3,2,1,0:T(8,128)(2,1)}), bf16[16,49,8,128]{3,2,1,0:T(8,128)(2,1)S(1)}, u32[]{:S(2)}, u32[]{:S(2)}) %all-to-all-start) | async-done | bytes 1605664 | tf_op jit(solution)/shard_map/all_to_all | solution.py:456
  44.8 3.0 %relax.1 = bf16[768,8,128]{2,1,0:T(8,128)(2,1)S(1)} custom-call(s32[1]{0:T(128)} %bitcast.place_ref, bf16[784,8,128]{2,1,0:T(8,128)(2,1)S(1)} %bitcast.5, bf16[32,128,128]{2,1,0:T(8,128)(2,1)S(1)} %turn.2.outer_ref, bf16[16,128,128]{2,1,0:T(8,128)(2,1)S(1)} %turn.3.inner_ref), custom_call_target="tpu_custom_call" | custom-call | tf_op jit(solution)/shard_map/relax/pallas_call | solution.py:471
  47.8 0.0 copy-start
  47.8 0.0 copy-start.1
  47.8 25.3 %all_to_all.10 = bf16[16,48,8,128]{3,2,1,0:T(8,128)(2,1)S(1)} all-to-all(bf16[16,48,8,128]{3,2,1,0:T(8,128)(2,1)S(1)} %bitcast.6), channel_id=1, replica_groups=mesh['lat'=4,'hi'=2,'lo'=4] {'lat','lo'}, dimensions={0} | all-to-all | bytes 3145728 | tf_op jit(solution)/shard_map/all_to_all | solution.py:456
  73.2 0.0 copy-done
  73.2 0.0 copy-done.1
  73.2 2.4 %finish.1 = f32[16,32,1024]{2,1,0:T(8,128)} custom-call(s32[16,128]{1,0:T(8,128)S(1)} %copy-done.1, bf16[768,8,128]{2,1,0:T(8,128)(2,1)S(1)} %bitcast.7, f32[16,256,128]{2,1,0:T(8,128)S(1)} %copy-done), custom_call_target="tpu_custom_call" | custom-call | tf_op jit(solution)/shard_map/finish/pallas_call | solution.py:487
Async XLA Ops:
  2.0 10.6 %collective-permute-start.2 = (bf16[32,1152]{1,0:T(8,128)(2,1)}, bf16[32,1152]{1,0:T(8,128)(2,1)}, u32[]{:S(2)}, u32[]{:S(2)}) collective-permute-start(bf16[32,1152]{1,0:T(8,128)(2,1)} %get-tuple-element.16), channel_id=1, source_target_pairs={{0,8},{16,24},{8,0},{24,16},{1,9},{17,25},{9,1},{25,17},{2,10},{18... | collective-permute-start | bytes 221192 | tf_op jit(solution)/shard_map/ppermute | solution.py:361
  5.0 7.6 %collective-permute-start.3 = (bf16[32,1152]{1,0:T(8,128)(2,1)}, bf16[32,1152]{1,0:T(8,128)(2,1)}, u32[]{:S(2)}, u32[]{:S(2)}) collective-permute-start(bf16[32,1152]{1,0:T(8,128)(2,1)} %get-tuple-element.17), channel_id=1, source_target_pairs={{8,16},{24,0},{16,8},{0,24},{9,17},{25,1},{17,9},{1,25},{10,18},{2... | collective-permute-start | bytes 221192 | tf_op jit(solution)/shard_map/ppermute | solution.py:361
  6.5 6.1 %collective-permute-start = (bf16[16,1152]{1,0:T(8,128)(2,1)}, bf16[16,1152]{1,0:T(8,128)(2,1)}, u32[]{:S(2)}, u32[]{:S(2)}) collective-permute-start(bf16[16,1152]{1,0:T(8,128)(2,1)} %get-tuple-element.14), channel_id=1, source_target_pairs={{0,1},{2,3},{4,5},{6,7},{1,0},{3,2},{5,4},{7,6},{8,9},{10,11},{12,... | collective-permute-start | bytes 110600 | tf_op jit(solution)/shard_map/ppermute | solution.py:361
  6.5 6.1 %collective-permute-start.1 = (bf16[16,1152]{1,0:T(8,128)(2,1)}, bf16[16,1152]{1,0:T(8,128)(2,1)}, u32[]{:S(2)}, u32[]{:S(2)}) collective-permute-start(bf16[16,1152]{1,0:T(8,128)(2,1)} %get-tuple-element.15), channel_id=1, source_target_pairs={{1,2},{3,4},{5,6},{7,0},{2,1},{4,3},{6,5},{0,7},{9,10},{11,12},{13... | collective-permute-start | bytes 110600 | tf_op jit(solution)/shard_map/ppermute | solution.py:361
  10.2 15.9 %collective-permute-start.4 = (bf16[16,128,128]{2,1,0:T(8,128)(2,1)}, bf16[16,128,128]{2,1,0:T(8,128)(2,1)}, u32[]{:S(2)}, u32[]{:S(2)}) collective-permute-start(bf16[16,128,128]{2,1,0:T(8,128)(2,1)} %refs_0_.3), channel_id=1, source_target_pairs={{0,6},{1,7},{6,0},{7,1},{8,14},{9,15},{14,8},{15,9},{16,22},{17,23... | collective-permute-start | bytes 1572872 | tf_op jit(solution)/shard_map/ppermute | solution.py:409
  17.4 3.9 %copy-start.2 = (bf16[16,128,128]{2,1,0:T(8,128)(2,1)S(1)}, bf16[16,128,128]{2,1,0:T(8,128)(2,1)}, u32[]{:S(2)}) copy-start(bf16[16,128,128]{2,1,0:T(8,128)(2,1)} %refs_0_.3) | copy-start | bytes 1572868
  17.4 27.4 %all-to-all-start = ((bf16[16,49,8,128]{3,2,1,0:T(8,128)(2,1)}), bf16[16,49,8,128]{3,2,1,0:T(8,128)(2,1)S(1)}, u32[]{:S(2)}, u32[]{:S(2)}) async-start(bf16[16,49,8,128]{3,2,1,0:T(8,128)(2,1)} %bitcast.8), calls=%async_computation | async-start | bytes 3211264 | tf_op jit(solution)/shard_map/all_to_all | solution.py:456
  21.3 6.2 %collective-permute-start.5 = (bf16[16,128,128]{2,1,0:T(8,128)(2,1)S(1)}, bf16[16,128,128]{2,1,0:T(8,128)(2,1)S(1)}, u32[]{:S(2)}, u32[]{:S(2)}) collective-permute-start(bf16[16,128,128]{2,1,0:T(8,128)(2,1)S(1)} %copy-done.2), channel_id=1, source_target_pairs={{2,4},{3,5},{4,2},{5,3},{10,12},{11,13},{12,10},{13,11},{18,20},{1... | collective-permute-start | bytes 1572872 | tf_op jit(solution)/shard_map/ppermute | solution.py:452
  47.8 25.4 %copy-start = (f32[16,256,128]{2,1,0:T(8,128)S(1)}, f32[16,256,128]{2,1,0:T(8,128)}, u32[]{:S(2)}) copy-start(f32[16,256,128]{2,1,0:T(8,128)} %get-tuple-element.22.dyn_ref) | copy-start | bytes 6291460
  47.8 25.4 %copy-start.1 = (s32[16,128]{1,0:T(8,128)S(1)}, s32[16,128]{1,0:T(8,128)}, u32[]{:S(2)}) copy-start(s32[16,128]{1,0:T(8,128)} %get-tuple-element.18.pos_ref) | copy-start | bytes 24580
